TPU v7x, 32 devices: a whole 2x2x4 slice. The times are simulated.
32 devices in a mesh: groups: 2 (over x), kvp: 16 (over z, y, core).
Axes of the slice: x: 2, y: 2, z: 4, core: 2. Of those that a mesh axis runs over, the one named last changes fastest.
Arguments:
- queries: bfloat16 [512, 4096], P(('groups', 'kvp')), parts along dimension 0, may hold values from -8 to 8
- rotated_span_keys: bfloat16 [512, 512], P(('groups', 'kvp')), parts along dimension 0, may hold values from -8 to 8
- incoming_values: bfloat16 [512, 512], P(('groups', 'kvp')), parts along dimension 0, may hold values from -6 to 6
- stored_keys: bfloat16 [32768, 512], P(('groups', 'kvp')), parts along dimension 0, may hold values from -8 to 8
- stored_values: bfloat16 [32768, 512], P(('groups', 'kvp')), parts along dimension 0, may hold values from -6 to 6
- shard_lens: int32 [32], P('groups'), parts along dimension 0, may hold values from 1 to 1024, 12288 in all
- span_starts: int32 [4], P('groups'), parts along dimension 0, may hold values from 6144 to 12288
Outputs:
- attended: bfloat16 [512, 4096], P(('groups', 'kvp')), parts along dimension 0
There are 2 independent parts, one for each index of `groups`. A program takes and returns all parts, laid end to end along the dimension named above; each array names one. Nothing has to cross between parts.
Inputs may be any that keep to these rules, and one draw needn't show every extreme that they name: `shard_lens`: the lengths of the 16 shards sum to 12288; one shard is full.
All inputs are finite; a program needn't handle non-finite values.
Results may differ from a plain program's by a relative error of at most 0.0023.
Values may be sent and summed in bfloat16 or wider, within the bound.
No kernel may reach another device: no remote copies, remote signals or barrier semaphores. Data moves between devices by JAX's collectives and lax.ppermute only.
A program may use at most 64 MiB of HBM per device.

v0:
```python
import jax
import jax.numpy as jnp
from jax import lax
from jax.sharding import PartitionSpec as P

QUERY_HEADS = 32
KEY_VALUE_HEADS = 4
HEAD_SIZE = 128
SPAN = 128
SPANS = 2


NEG_LARGE = -1e30


def softmax_part(query_rows, per_head_keys, per_head_values, visible, scale):
    scores = (
        jnp.einsum("rhgd,khd->rhgk", query_rows, per_head_keys, preferred_element_type=jnp.float32)
        * scale
    )
    visible_mask = visible[:, None, None, :]
    maxima = jnp.max(jnp.where(visible_mask, scores, NEG_LARGE), axis=-1)
    weights = jnp.where(visible_mask, jnp.exp(scores - maxima[..., None]), 0.0)
    totals = jnp.sum(weights, axis=-1)
    numerators = jnp.einsum(
        "rhgk,khd->rhgd",
        weights.astype(jnp.bfloat16),
        per_head_values,
        preferred_element_type=jnp.float32,
    )
    return (numerators, maxima, totals)


def shards(
    queries, rotated_span_keys, incoming_values, stored_keys, stored_values, shard_lens, span_starts
):
    shard_count = lax.axis_size("kvp")
    device = lax.axis_index("kvp")
    device_local_rows = queries.shape[0]
    cache_slot_count = stored_keys.shape[0]
    query_group_size = QUERY_HEADS // KEY_VALUE_HEADS
    scale = HEAD_SIZE ** (-0.5)
    offsets = jnp.cumsum(shard_lens) - shard_lens
    device_pick = (jnp.arange(shard_count, dtype=jnp.int32) == device).astype(jnp.int32)
    my_start = jnp.sum(offsets * device_pick)
    my_length = jnp.sum(shard_lens * device_pick)
    slot_index = jnp.arange(cache_slot_count, dtype=jnp.int32)
    positions = my_start + slot_index
    live_slots = slot_index < my_length
    per_head_keys = stored_keys.reshape(cache_slot_count, KEY_VALUE_HEADS, HEAD_SIZE)
    per_head_values = stored_values.reshape(cache_slot_count, KEY_VALUE_HEADS, HEAD_SIZE)
    span_index = jnp.arange(SPANS, dtype=jnp.int32)
    every_query = lax.all_gather(queries, "kvp", axis=0, tiled=True)
    overall_rows = every_query.shape[0]
    block_row_range = 64

    def one_block(first):
        rows_here = lax.dynamic_slice_in_dim(every_query, first, block_row_range, 0).reshape(
            block_row_range, KEY_VALUE_HEADS, query_group_size, HEAD_SIZE
        )
        row_ids = first + jnp.arange(block_row_range, dtype=jnp.int32)
        compare = (row_ids // SPAN)[:, None] == span_index[None, :]
        limits = jnp.sum(jnp.where(compare, span_starts[None, :], 0), axis=1)
        visible = live_slots[None, :] & (positions[None, :] < limits[:, None])
        numerators, maxima, totals = softmax_part(
            rows_here, per_head_keys, per_head_values, visible, scale
        )
        return (
            numerators.reshape(block_row_range, QUERY_HEADS * HEAD_SIZE),
            maxima.reshape(block_row_range, QUERY_HEADS),
            totals.reshape(block_row_range, QUERY_HEADS),
        )

    block_starts = jnp.arange(overall_rows // block_row_range, dtype=jnp.int32) * block_row_range
    numerators, maxima, totals = lax.map(one_block, block_starts)
    numerators = numerators.reshape(overall_rows, QUERY_HEADS * HEAD_SIZE)
    maxima = maxima.reshape(overall_rows, QUERY_HEADS)
    totals = totals.reshape(overall_rows, QUERY_HEADS)
    span_key_rows, span_value_rows = (
        lax.all_gather(rotated_span_keys, "kvp", axis=0, tiled=True),
        lax.all_gather(incoming_values, "kvp", axis=0, tiled=True),
    )
    own_ids = device * device_local_rows + jnp.arange(device_local_rows, dtype=jnp.int32)
    key_ids = jnp.arange(overall_rows, dtype=jnp.int32)
    span_visible = (key_ids[None, :] // SPAN == own_ids[:, None] // SPAN) & (
        key_ids[None, :] <= own_ids[:, None]
    )
    local_query = queries.reshape(device_local_rows, KEY_VALUE_HEADS, query_group_size, HEAD_SIZE)
    span_num, span_max, span_total = softmax_part(
        local_query,
        span_key_rows.reshape(overall_rows, KEY_VALUE_HEADS, HEAD_SIZE),
        span_value_rows.reshape(overall_rows, KEY_VALUE_HEADS, HEAD_SIZE),
        span_visible,
        scale,
    )
    span_num = span_num.reshape(device_local_rows, QUERY_HEADS, HEAD_SIZE)
    span_max = span_max.reshape(device_local_rows, QUERY_HEADS)
    span_total = span_total.reshape(device_local_rows, QUERY_HEADS)
    arrived_num, arrived_max, arrived_total = (
        lax.all_to_all(
            numerators.reshape(shard_count, device_local_rows, QUERY_HEADS * HEAD_SIZE),
            "kvp",
            split_axis=0,
            concat_axis=0,
            tiled=True,
        ),
        lax.all_to_all(
            maxima.reshape(shard_count, device_local_rows, QUERY_HEADS),
            "kvp",
            split_axis=0,
            concat_axis=0,
            tiled=True,
        ),
        lax.all_to_all(
            totals.reshape(shard_count, device_local_rows, QUERY_HEADS),
            "kvp",
            split_axis=0,
            concat_axis=0,
            tiled=True,
        ),
    )
    own_max = jnp.max(arrived_max, axis=0)
    factor = jnp.exp(arrived_max - own_max[None])
    summed_num = jnp.sum(
        arrived_num.reshape(shard_count, device_local_rows, QUERY_HEADS, HEAD_SIZE)
        * factor[..., None],
        axis=0,
    )
    summed_total = jnp.sum(arrived_total * factor, axis=0)
    overall = jnp.maximum(own_max, span_max)
    shard_factor = jnp.exp(own_max - overall)
    span_factor = jnp.exp(span_max - overall)
    numerator = summed_num * shard_factor[..., None] + span_num * span_factor[..., None]
    denominator = summed_total * shard_factor + span_total * span_factor
    return (
        (numerator / denominator[..., None])
        .reshape(device_local_rows, QUERY_HEADS * HEAD_SIZE)
        .astype(jnp.bfloat16)
    )


def solution(mesh):
    in_specs = (
        P(("groups", "kvp"), None),
        P(("groups", "kvp"), None),
        P(("groups", "kvp"), None),
        P(("groups", "kvp"), None),
        P(("groups", "kvp"), None),
        P("groups"),
        P("groups"),
    )
    out_specs = P(("groups", "kvp"), None)
    return jax.shard_map(shards, mesh=mesh, in_specs=in_specs, out_specs=out_specs, check_vma=False)
```

profile of v0, /device:TPU:0, one launch (start us, length us, event | category | flops | bytes accessed | tf_op | source)
XLA Modules:
  0.0 307.2 jit_solution(7402948748695958223)
XLA Ops:
  6.5 0.7 all-gather.2.cloned.1.call-update
  7.3 0.7 copy.122
  8.2 1.5 copy.120
  9.7 0.7 copy.123
  10.3 1.5 copy.121
  11.8 1.3 copy.124
  13.2 0.7 fusion.35
  13.9 39.8 %all-gather.2.cloned.1.call-done = bf16[256,4096]{1,0:T(8,128)(2,1)} async-done(((bf16[16,4096]{1,0:T(8,128)(2,1)}), bf16[256,4096]{1,0:T(8,128)(2,1)}) %all-gather.2.cloned.1.call-update) | async-done | bytes 2097168 | tf_op jit(solution)/shard_map/all_gather | solution.py:53
  53.7 81.5 %while.17 = (s32[]{:T(128)}, f32[4,64,4096]{2,1,0:T(8,128)}, f32[4,64,32]{1,2,0:T(8,128)S(1)}, f32[4,64,32]{1,2,0:T(8,128)S(1)}, s32[4]{0:T(128)S(1)}, /*index=5...) while((s32[]{:T(128)}, f32[4,64,4096]{2,1,0:T(8,128)}, ...), condition=%wide.region_7.8_spmd.clone, body=%wide.region_3.7_spmd.clone.sunk | while | flops 1096940800 | bytes 71184104 | solution.py:75
  53.7 0.7 dynamic_slice.19
  56.5 1.2 dynamic-slice_bitcast_fusion.2
  57.8 0.7 and_select_fusion.4
  58.6 0.6 iota_add_fusion.3
  59.2 0.6 iota_compare_fusion.3
  60.0 1.9 fusion.49
  61.9 3.2 %copy-done = f32[4,64,8,1024]{3,2,1,0:T(8,128)} copy-done((f32[4,64,8,1024]{3,2,1,0:T(8,128)}, f32[4,64,8,1024]{3,2,1,0:T(8,128)S(1)}, u32[]{:S(2)}) %copy-start) | copy-done | bytes 8388632 | tf_op jit(solution)/shard_map/while
  65.1 2.5 fusion.51
  67.8 4.8 %fusion.50 = f32[64,4,8,128]{3,2,0,1:T(8,128)S(1)} fusion(f32[4,64,8,1024]{3,2,1,0:T(8,128)} %copy-done, f32[64,4,8]{2,0,1:T(8,128)S(1)} %get-tuple-element.365, pred[64,1024]{1,0:T(8,128)(4,1)S(1)} %compare_and_fusion.2, bf16[1024,4,128]{2,0,1:T(8,128)(2,1)} %get-tuple-element.404), kind=kOutput, calls=%fused_computation.12.clone.1 | convolution fusion | flops 545259520 | bytes 10559488 | tf_op jit(solution)/shard_map/while/body/eval_jaxpr/rhgk,khd->rhgd/dot_general | solution.py:25
  73.0 1.2 constant_dynamic-update-slice_fusion.2
  74.2 0.7 dynamic_slice.19
  76.9 1.2 dynamic-slice_bitcast_fusion.2
  78.2 0.7 and_select_fusion.4
  79.0 0.6 iota_add_fusion.3
  79.7 0.6 iota_compare_fusion.3
  80.4 1.9 fusion.49
  82.3 3.2 %copy-done = f32[4,64,8,1024]{3,2,1,0:T(8,128)} copy-done((f32[4,64,8,1024]{3,2,1,0:T(8,128)}, f32[4,64,8,1024]{3,2,1,0:T(8,128)S(1)}, u32[]{:S(2)}) %copy-start) | copy-done | bytes 8388632 | tf_op jit(solution)/shard_map/while
  85.6 2.5 fusion.51
  88.3 4.8 %fusion.50 = f32[64,4,8,128]{3,2,0,1:T(8,128)S(1)} fusion(f32[4,64,8,1024]{3,2,1,0:T(8,128)} %copy-done, f32[64,4,8]{2,0,1:T(8,128)S(1)} %get-tuple-element.365, pred[64,1024]{1,0:T(8,128)(4,1)S(1)} %compare_and_fusion.2, bf16[1024,4,128]{2,0,1:T(8,128)(2,1)} %get-tuple-element.404), kind=kOutput, calls=%fused_computation.12.clone.1 | convolution fusion | flops 545259520 | bytes 10559488 | tf_op jit(solution)/shard_map/while/body/eval_jaxpr/rhgk,khd->rhgd/dot_general | solution.py:25
  93.4 1.1 constant_dynamic-update-slice_fusion.2
  94.5 0.7 dynamic_slice.19
  97.2 1.2 dynamic-slice_bitcast_fusion.2
  98.6 0.7 and_select_fusion.4
  99.4 0.6 iota_add_fusion.3
  100.0 0.6 iota_compare_fusion.3
  100.8 1.9 fusion.49
  102.7 3.2 %copy-done = f32[4,64,8,1024]{3,2,1,0:T(8,128)} copy-done((f32[4,64,8,1024]{3,2,1,0:T(8,128)}, f32[4,64,8,1024]{3,2,1,0:T(8,128)S(1)}, u32[]{:S(2)}) %copy-start) | copy-done | bytes 8388632 | tf_op jit(solution)/shard_map/while
  105.9 2.5 fusion.51
  108.6 4.8 %fusion.50 = f32[64,4,8,128]{3,2,0,1:T(8,128)S(1)} fusion(f32[4,64,8,1024]{3,2,1,0:T(8,128)} %copy-done, f32[64,4,8]{2,0,1:T(8,128)S(1)} %get-tuple-element.365, pred[64,1024]{1,0:T(8,128)(4,1)S(1)} %compare_and_fusion.2, bf16[1024,4,128]{2,0,1:T(8,128)(2,1)} %get-tuple-element.404), kind=kOutput, calls=%fused_computation.12.clone.1 | convolution fusion | flops 545259520 | bytes 10559488 | tf_op jit(solution)/shard_map/while/body/eval_jaxpr/rhgk,khd->rhgd/dot_general | solution.py:25
  113.8 1.1 constant_dynamic-update-slice_fusion.2
  114.8 0.7 dynamic_slice.19
  117.6 1.2 dynamic-slice_bitcast_fusion.2
  118.9 0.7 and_select_fusion.4
  119.7 0.6 iota_add_fusion.3
  120.3 0.6 iota_compare_fusion.3
  121.1 1.9 fusion.49
  123.0 3.2 %copy-done = f32[4,64,8,1024]{3,2,1,0:T(8,128)} copy-done((f32[4,64,8,1024]{3,2,1,0:T(8,128)}, f32[4,64,8,1024]{3,2,1,0:T(8,128)S(1)}, u32[]{:S(2)}) %copy-start) | copy-done | bytes 8388632 | tf_op jit(solution)/shard_map/while
  126.2 2.5 fusion.51
  128.9 4.8 %fusion.50 = f32[64,4,8,128]{3,2,0,1:T(8,128)S(1)} fusion(f32[4,64,8,1024]{3,2,1,0:T(8,128)} %copy-done, f32[64,4,8]{2,0,1:T(8,128)S(1)} %get-tuple-element.365, pred[64,1024]{1,0:T(8,128)(4,1)S(1)} %compare_and_fusion.2, bf16[1024,4,128]{2,0,1:T(8,128)(2,1)} %get-tuple-element.404), kind=kOutput, calls=%fused_computation.12.clone.1 | convolution fusion | flops 545259520 | bytes 10559488 | tf_op jit(solution)/shard_map/while/body/eval_jaxpr/rhgk,khd->rhgd/dot_general | solution.py:25
  134.1 1.1 constant_dynamic-update-slice_fusion.2
  135.3 0.7 reshape.300
  136.0 3.5 %all-to-all-start.1 = ((f32[16,1,512]{2,1,0:T(1,128)}), f32[16,1,512]{2,1,0:T(1,128)S(1)}, u32[]{:S(2)}, u32[]{:S(2)}) async-start(f32[16,1,512]{2,1,0:T(1,128)} %reshape.300), calls=%async_computation.1 | async-start | bytes 65536 | tf_op jit(solution)/shard_map/all_to_all | solution.py:107
  139.7 6.4 %all-to-all-done.1 = f32[16,1,512]{2,1,0:T(1,128)S(1)} async-done(((f32[16,1,512]{2,1,0:T(1,128)}), f32[16,1,512]{2,1,0:T(1,128)S(1)}, u32[]{:S(2)}, u32[]{:S(2)}) %all-to-all-start.1) | async-done | bytes 32800 | tf_op jit(solution)/shard_map/all_to_all | solution.py:107
  146.1 9.2 %all_to_all.15 = f32[16,1,512]{2,1,0:T(1,128)S(1)} all-to-all(f32[16,1,512]{2,1,0:T(1,128)S(1)} %reshape.302), channel_id=1, replica_groups=mesh['groups'=2,'kvp'=16] {'kvp'}, dimensions={0} | all-to-all | bytes 65536 | tf_op jit(solution)/shard_map/all_to_all | solution.py:114
  155.3 4.5 %all-to-all-start = ((f32[16,16,4096]{2,1,0:T(8,128)}), f32[16,16,4096]{2,1,0:T(8,128)}, u32[]{:S(2)}, u32[]{:S(2)}) async-start(f32[16,16,4096]{2,1,0:T(8,128)} %bitcast.112), calls=%async_computation | async-start | bytes 8388608 | tf_op jit(solution)/shard_map/all_to_all | solution.py:100
  159.9 87.9 %all_gather.10 = bf16[256,512]{1,0:T(8,128)(2,1)S(1)} all-gather(bf16[16,512]{1,0:T(8,128)(2,1)S(1)} %copy-done.2), channel_id=1, replica_groups=mesh['groups'=2,'kvp'=16] {'kvp'}, dimensions={0}, use_global_device_ids=true | all-gather | bytes 278528 | tf_op jit(solution)/shard_map/all_gather | solution.py:80
  248.0 0.3 select_reduce_fusion
  248.7 35.9 %all_gather.11 = bf16[256,512]{1,0:T(8,128)(2,1)S(1)} all-gather(bf16[16,512]{1,0:T(8,128)(2,1)S(1)} %copy-done.3), channel_id=1, replica_groups=mesh['groups'=2,'kvp'=16] {'kvp'}, dimensions={0}, use_global_device_ids=true | all-gather | bytes 278528 | tf_op jit(solution)/shard_map/all_gather | solution.py:81
  285.0 0.5 broadcast.249
  285.5 0.7 reduce.3
  286.4 0.7 reduce.2
  287.2 2.6 mul.83
  289.8 5.0 %mul.84 = f32[16,16,4096]{2,1,0:T(8,128)} reshape(f32[16,16,32,128]{3,2,1,0:T(8,128)} %mul.83) | data formatting | bytes 8388608 | tf_op jit(solution)/shard_map/mul | solution.py:125
  294.8 3.9 %multiply_reduce_fusion = f32[16,4096]{1,0:T(8,128)S(1)} fusion(f32[16,16,4096]{2,1,0:T(8,128)} %all-to-all-done, f32[16,16,4096]{2,1,0:T(8,128)} %mul.84), kind=kLoop, calls=%fused_computation.32 | loop fusion | flops 2031616 | bytes 8650752 | tf_op jit(solution)/shard_map/reduce_sum | solution.py:124
  299.1 1.2 fusion.27
  (76 shorter events, 5.3 us)
Async XLA Ops:
  6.5 6.6 %copy-start.4 = (s32[16]{0:T(128)S(1)}, s32[16]{0:T(128)}, u32[]{:S(2)}) copy-start(s32[16]{0:T(128)} %param.14) | copy-start | bytes 196
  6.5 47.2 %copy-start.5 = (s32[2]{0:T(128)S(1)}, s32[2]{0:T(128)}, u32[]{:S(2)}) copy-start(s32[2]{0:T(128)} %param.15) | copy-start | bytes 28
  6.5 47.2 %all-gather.2.cloned.1.call-start = ((), (), s32[]{:S(2)}) async-start(), calls=%async_computation.3 | async-start | bytes 2228224 | tf_op jit(solution)/shard_map/all_gather | solution.py:53
  61.9 3.2 %copy-start = (f32[4,64,8,1024]{3,2,1,0:T(8,128)}, f32[4,64,8,1024]{3,2,1,0:T(8,128)S(1)}, u32[]{:S(2)}) copy-start(f32[4,64,8,1024]{3,2,1,0:T(8,128)S(1)} %get-tuple-element.364) | copy-start | bytes 25165828 | tf_op jit(solution)/shard_map/while
  82.3 3.2 %copy-start = (f32[4,64,8,1024]{3,2,1,0:T(8,128)}, f32[4,64,8,1024]{3,2,1,0:T(8,128)S(1)}, u32[]{:S(2)}) copy-start(f32[4,64,8,1024]{3,2,1,0:T(8,128)S(1)} %get-tuple-element.364) | copy-start | bytes 25165828 | tf_op jit(solution)/shard_map/while
  102.7 3.2 %copy-start = (f32[4,64,8,1024]{3,2,1,0:T(8,128)}, f32[4,64,8,1024]{3,2,1,0:T(8,128)S(1)}, u32[]{:S(2)}) copy-start(f32[4,64,8,1024]{3,2,1,0:T(8,128)S(1)} %get-tuple-element.364) | copy-start | bytes 25165828 | tf_op jit(solution)/shard_map/while
  123.0 3.2 %copy-start = (f32[4,64,8,1024]{3,2,1,0:T(8,128)}, f32[4,64,8,1024]{3,2,1,0:T(8,128)S(1)}, u32[]{:S(2)}) copy-start(f32[4,64,8,1024]{3,2,1,0:T(8,128)S(1)} %get-tuple-element.364) | copy-start | bytes 25165828 | tf_op jit(solution)/shard_map/while
  135.2 24.7 %copy-start.2 = (bf16[16,512]{1,0:T(8,128)(2,1)S(1)}, bf16[16,512]{1,0:T(8,128)(2,1)}, u32[]{:S(2)}) copy-start(bf16[16,512]{1,0:T(8,128)(2,1)} %param.10) | copy-start | bytes 49156
  135.2 112.7 %copy-start.1 = (bf16[16,4096]{1,0:T(8,128)(2,1)S(1)}, bf16[16,4096]{1,0:T(8,128)(2,1)}, u32[]{:S(2)}) copy-start(bf16[16,4096]{1,0:T(8,128)(2,1)} %param.9) | copy-start | bytes 393220
  135.2 113.6 %copy-start.3 = (bf16[16,512]{1,0:T(8,128)(2,1)S(1)}, bf16[16,512]{1,0:T(8,128)(2,1)}, u32[]{:S(2)}) copy-start(bf16[16,512]{1,0:T(8,128)(2,1)} %param.11) | copy-start | bytes 49156
  136.0 10.1 %all-to-all-start.1 = ((f32[16,1,512]{2,1,0:T(1,128)}), f32[16,1,512]{2,1,0:T(1,128)S(1)}, u32[]{:S(2)}, u32[]{:S(2)}) async-start(f32[16,1,512]{2,1,0:T(1,128)} %reshape.300), calls=%async_computation.1 | async-start | bytes 65536 | tf_op jit(solution)/shard_map/all_to_all | solution.py:107
  155.3 139.5 %all-to-all-start = ((f32[16,16,4096]{2,1,0:T(8,128)}), f32[16,16,4096]{2,1,0:T(8,128)}, u32[]{:S(2)}, u32[]{:S(2)}) async-start(f32[16,16,4096]{2,1,0:T(8,128)} %bitcast.112), calls=%async_computation | async-start | bytes 8388608 | tf_op jit(solution)/shard_map/all_to_all | solution.py:100
Sparse Core Ops, SparseCore 0:
  9.5 44.1 all-gather.1
where the time goes:
time: 308 us; the launch traced here: 307 us
  blocking collectives  133 us (43%)
  waiting for transfers between devices  46.9 us (15%)
  local copies, waits for them, and re-layouts  42.8 us (14%)
  matrix products  27.5 us (9%)
  other arithmetic  26.7 us (9%)
  between operations  13.6 us (4%)
  loops' own time  8.62 us (3%)
  starting transfers between devices  8.03 us (3%)
    all_gather x1, blocking collectives, shards(): lax.all_gather(rotated_span_keys, 'kvp', axis=0, tiled=True)  87.9 us
    all_gather x1, waiting for transfers between devices, shards(): every_query = lax.all_gather(queries, 'kvp', axis=0, tiled=True)  39.8 us
    all_gather x1, blocking collectives, shards(): lax.all_gather(incoming_values, 'kvp', axis=0, tiled=True)  35.9 us
    dot_general x5, matrix products, softmax_part(): jnp.einsum('rhgk,khd->rhgd', weights.astype(jnp.bfloat16), per_head_value...  19.6 us
    while x16, local copies, waits for them, and re-layouts  18.1 us
    reduce_sum x4, other arithmetic, softmax_part(): totals = jnp.sum(weights, axis=-1)  10.1 us
    all_to_all x1, blocking collectives, shards(): lax.all_to_all(totals.reshape(shard_count, device_local_rows, QUERY_HEADS...  9.19 us
    another operation x1, loops' own time, shards(): numerators, maxima, totals = lax.map(one_block, block_starts)  8.62 us
  transfers between devices with their start and end apart: 3, of which 2 were waited for; matrix products, arithmetic and copies ran while one was open for 6% of the time, Pallas kernels for 0%

commit v1 on v0

--- a/solution.py
+++ b/solution.py
@@ -1,6 +1,11 @@
+import functools
+
 import jax
 import jax.numpy as jnp
+import numpy as np
 from jax import lax
+from jax.experimental import pallas as pl
+from jax.experimental.pallas import tpu as pltpu
 from jax.sharding import PartitionSpec as P
 
 QUERY_HEADS = 32
@@ -8,9 +13,314 @@
 HEAD_SIZE = 128
 SPAN = 128
 SPANS = 2
-
-
+GROUP = QUERY_HEADS // KEY_VALUE_HEADS
+WIDTH = GROUP * HEAD_SIZE
 NEG_LARGE = -1e30
+LOG2_SCALE = float(HEAD_SIZE**-0.5 * np.log2(np.e))
+CODE = 32767.0
+F32, BF16, I16 = jnp.float32, jnp.bfloat16, jnp.int16
+
+
+def row_limit(meta, shard, span, shards, slots):
+    start = jnp.int32(0)
+    length = jnp.int32(0)
+    for j in range(shards):
+        n = meta[1 + j]
+        start = start + jnp.where(j < shard, n, 0)
+        length = jnp.where(j == shard, n, length)
+    limit = meta[1 + shards]
+    for j in range(1, SPANS):
+        limit = jnp.where(span == j, meta[1 + shards + j], limit)
+    return jnp.clip(jnp.minimum(length, limit - start), 0, slots)
+
+
+def stack_heads(q):
+    return jnp.concatenate([q[:, g * HEAD_SIZE : (g + 1) * HEAD_SIZE] for g in range(GROUP)], axis=0)
+
+
+def attend(q, k, v, bias):
+    s = lax.dot_general(q, k, (((1,), (1,)), ((), ())), preferred_element_type=F32) + bias
+    m = jnp.max(s, axis=1, keepdims=True)
+    w = jnp.exp2((s - m) * LOG2_SCALE)
+    t = jnp.sum(w, axis=1, keepdims=True)
+    n = jnp.dot(w.astype(BF16), v, preferred_element_type=F32)
+    return n, m, t
+
+
+def merge(a, b):
+    if a is None:
+        return b
+    m = jnp.maximum(a[1], b[1])
+    fa, fb = jnp.exp2((a[1] - m) * LOG2_SCALE), jnp.exp2((b[1] - m) * LOG2_SCALE)
+    return a[0] * fa + b[0] * fb, m, a[2] * fa + b[2] * fb
+
+
+def encode(state, out_ref, rows):
+    n, m, t = state
+    top = jnp.maximum(jnp.max(jnp.abs(n), axis=1, keepdims=True), 1e-30)
+    codes = jnp.round(n * (CODE / top)).astype(jnp.int32).astype(I16)
+    base = m * LOG2_SCALE
+    lane = lax.broadcasted_iota(jnp.int32, (rows, HEAD_SIZE), 1)
+    stats = jnp.zeros((rows, HEAD_SIZE), jnp.int32)
+    for j, value in enumerate((base + jnp.log2(top), base + jnp.log2(t))):
+        value = jnp.maximum(value, -2000.0)
+        high = jnp.round(value * 16.0)
+        low = jnp.round((value - high * (1 / 16.0)) * 524288.0)
+        for i, part in enumerate((high.astype(jnp.int32), low.astype(jnp.int32))):
+            for g in range(GROUP):
+                stats = jnp.where(lane == 4 * g + 2 * j + i, part[g * rows : (g + 1) * rows], stats)
+    for g in range(GROUP):
+        out_ref[:, g * HEAD_SIZE : (g + 1) * HEAD_SIZE] = codes[g * rows : (g + 1) * rows]
+    out_ref[:, WIDTH:] = stats.astype(I16)
+
+
+def split_kernel(rows, meta, q_ref, sk_ref, sv_ref, k_ref, v_ref, *outs):
+    me = meta[0] % 4
+    for j in range(1, 4):
+        at = pl.ds(pl.multiple_of((me ^ j) * HEAD_SIZE, HEAD_SIZE), HEAD_SIZE)
+        outs[3 + j][:, :HEAD_SIZE] = k_ref[:, at]
+        outs[3 + j][:, HEAD_SIZE:] = v_ref[:, at]
+
+    @pl.when(pl.program_id(0) == 0)
+    def _():
+        for j in range(4):
+            at = pl.ds(pl.multiple_of((me ^ j) * HEAD_SIZE, HEAD_SIZE), HEAD_SIZE)
+            wide = pl.ds(pl.multiple_of((me ^ j) * WIDTH, WIDTH), WIDTH)
+            outs[j][:, :WIDTH] = q_ref[:, wide]
+            outs[j][:, WIDTH : WIDTH + HEAD_SIZE] = sk_ref[:, at]
+            outs[j][:, WIDTH + HEAD_SIZE :] = sv_ref[:, at]
+
+
+def whole(shape):
+    return pl.BlockSpec(shape, lambda i, meta: (0,) * len(shape))
+
+
+def split(meta, queries, span_keys, span_values, keys, values):
+    rows, slots = queries.shape[0], keys.shape[0]
+    steps = 4
+    wide = WIDTH + 2 * HEAD_SIZE
+    part = slots // steps
+    return pl.pallas_call(
+        functools.partial(split_kernel, rows),
+        out_shape=[jax.ShapeDtypeStruct((rows, wide), BF16)] * 4
+        + [jax.ShapeDtypeStruct((slots, 2 * HEAD_SIZE), BF16)] * 3,
+        grid_spec=pltpu.PrefetchScalarGridSpec(
+            num_scalar_prefetch=1,
+            grid=(steps,),
+            in_specs=[
+                whole(queries.shape),
+                whole(span_keys.shape),
+                whole(span_values.shape),
+                pl.BlockSpec((part, keys.shape[1]), lambda i, meta: (i, 0)),
+                pl.BlockSpec((part, keys.shape[1]), lambda i, meta: (i, 0)),
+            ],
+            out_specs=[whole((rows, wide))] * 4
+            + [pl.BlockSpec((part, 2 * HEAD_SIZE), lambda i, meta: (i, 0))] * 3,
+        ),
+        name="split",
+    )(meta, queries, span_keys, span_values, keys, values)
+
+
+def attend_kernel(cfg, meta, *refs):
+    shards, blocks, pieces, own, prior, finish, rows = cfg
+    refs = list(refs)
+    q_refs = [refs.pop(0) for _ in blocks]
+    kv = []
+    for j in pieces:
+        if own and j == 0:
+            kv.append((refs.pop(0), refs.pop(0)))
+        else:
+            kv.append((refs.pop(0), None))
+    prior_refs = [(refs.pop(0), refs.pop(0)) for _ in blocks] if prior else None
+    span_ref = refs.pop(0) if finish == "span" else None
+    outs = refs
+    me = meta[0]
+    zs = shards // 4
+    z, b = me // 4, me % 4
+    slots = kv[0][0].shape[0]
+    lane = lax.broadcasted_iota(jnp.int32, (1, slots), 1)
+    for i, d in enumerate(blocks):
+        q = stack_heads(q_refs[i][:, :WIDTH])
+        span = lax.rem(z - d + zs, zs) * rows // SPAN
+        state = None
+        if prior:
+            p_ref, s_ref = prior_refs[i]
+            state = (
+                jnp.concatenate([p_ref[:, g * HEAD_SIZE : (g + 1) * HEAD_SIZE] for g in range(GROUP)], axis=0),
+                s_ref[:, 0:1],
+                s_ref[:, 1:2],
+            )
+        for j, (k_ref, v_ref) in zip(pieces, kv):
+            seen = row_limit(meta, z * 4 + (b ^ j), span, shards, slots)
+            bias = jnp.where(lane < seen, 0.0, NEG_LARGE)
+            if v_ref is None:
+                k, v = k_ref[:, :HEAD_SIZE], k_ref[:, HEAD_SIZE:]
+            else:
+                k, v = k_ref[...], v_ref[...]
+            state = merge(state, attend(q, k, v, bias))
+        if finish == "encode":
+            encode(state, outs[i], rows)
+            continue
+        if finish == "span":
+            mine, before = q_refs[i], span_ref
+            k = jnp.concatenate([mine[:, WIDTH : WIDTH + HEAD_SIZE], before[:, WIDTH : WIDTH + HEAD_SIZE]], axis=0)
+            v = jnp.concatenate([mine[:, WIDTH + HEAD_SIZE :], before[:, WIDTH + HEAD_SIZE :]], axis=0)
+            s = lax.dot_general(q, k, (((1,), (1,)), ((), ())), preferred_element_type=F32)
+            part = rows // 4
+            r = lax.broadcasted_iota(jnp.int32, s.shape, 0) % rows
+            c = lax.broadcasted_iota(jnp.int32, s.shape, 1)
+            r = ((r // part) ^ b) * part + r % part
+            here = (((c // part) ^ b) * part + c % part <= r) & (c < rows)
+            earlier = (c >= rows) & ((z * rows) % SPAN > 0)
+            visible = here | earlier
+            s = jnp.where(visible, s, NEG_LARGE)
+            m = jnp.max(s, axis=1, keepdims=True)
+            w = jnp.where(visible, jnp.exp2((s - m) * LOG2_SCALE), 0.0)
+            t = jnp.sum(w, axis=1, keepdims=True)
+            state = merge(state, (jnp.dot(w.astype(BF16), v, preferred_element_type=F32), m, t))
+        n, m, t = state
+        for g in range(GROUP):
+            outs[2 * i][:, g * HEAD_SIZE : (g + 1) * HEAD_SIZE] = n[g * rows : (g + 1) * rows]
+        outs[2 * i + 1][:, 0:1] = m
+        outs[2 * i + 1][:, 1:2] = t
+
+
+def attention(meta, shards, q, pieces, own=None, prior=None, finish=None, before=None, name="attend"):
+    blocks = tuple(q)
+    rows = q[blocks[0]].shape[0]
+    order = ((0,) if own is not None else ()) + tuple(pieces)
+    args, specs = [], []
+
+    def add(x, spec=None):
+        args.append(x)
+        specs.append(spec or whole(x.shape))
+
+    for d in blocks:
+        add(q[d])
+    if own is not None:
+        for x in own:
+            add(x, pl.BlockSpec((x.shape[0], HEAD_SIZE), lambda i, meta: (0, meta[0] % 4)))
+    for j in pieces:
+        add(pieces[j])
+    if prior is not None:
+        for d in blocks:
+            add(prior[d][0])
+            add(prior[d][1])
+    if finish == "span":
+        add(before)
+    if finish == "encode":
+        shapes = [((rows, WIDTH + HEAD_SIZE), I16)] * len(blocks)
+    else:
+        shapes = [((rows, WIDTH), F32), ((GROUP * rows, HEAD_SIZE), F32)] * len(blocks)
+    slots = args[len(blocks)].shape[0]
+    work = len(blocks) * len(order) * GROUP * rows * slots
+    outs = pl.pallas_call(
+        functools.partial(attend_kernel, (shards, blocks, order, own is not None, prior is not None, finish, rows)),
+        out_shape=[jax.ShapeDtypeStruct(s, t) for s, t in shapes],
+        grid_spec=pltpu.PrefetchScalarGridSpec(
+            num_scalar_prefetch=1,
+            grid=(1,),
+            in_specs=specs,
+            out_specs=[whole(s) for s, _ in shapes],
+        ),
+        cost_estimate=pl.CostEstimate(
+            flops=4 * HEAD_SIZE * work, transcendentals=work, bytes_accessed=sum(x.size * 2 for x in args)
+        ),
+        name=name,
+    )(meta, *args)
+    if finish == "encode":
+        return dict(zip(blocks, outs))
+    return {d: (outs[2 * i], outs[2 * i + 1]) for i, d in enumerate(blocks)}
+
+
+def final_kernel(rows, n_ref, s_ref, *refs):
+    codes, outs = refs[:3], refs[3:]
+    part = rows // 4
+    stats = [c[:, WIDTH:].astype(F32) for c in codes]
+    for g in range(GROUP):
+        cols = slice(g * HEAD_SIZE, (g + 1) * HEAD_SIZE)
+        head = slice(g * rows, (g + 1) * rows)
+        m, t = s_ref[head, 0:1] * LOG2_SCALE, s_ref[head, 1:2]
+        tops = [x[:, 4 * g : 4 * g + 1] * (1 / 16.0) + x[:, 4 * g + 1 : 4 * g + 2] * (1 / 524288.0) for x in stats]
+        sums = [x[:, 4 * g + 2 : 4 * g + 3] * (1 / 16.0) + x[:, 4 * g + 3 : 4 * g + 4] * (1 / 524288.0) for x in stats]
+        over = m
+        for x in sums:
+            over = jnp.maximum(over, x)
+        f = jnp.exp2(m - over)
+        n, t = n_ref[:, cols] * f, t * f
+        for c, top, total in zip(codes, tops, sums):
+            n = n + c[:, cols].astype(F32) * (jnp.exp2(top - over) * (1 / CODE))
+            t = t + jnp.exp2(total - over)
+        n = (n / t).astype(BF16)
+        for k in range(4):
+            outs[k][:, cols] = n[k * part : (k + 1) * part]
+
+
+def final(own, codes):
+    rows = own[0].shape[0]
+    return pl.pallas_call(
+        functools.partial(final_kernel, rows),
+        out_shape=[jax.ShapeDtypeStruct((rows // 4, WIDTH), BF16)] * 4,
+        name="final",
+    )(*own, *codes)
+
+
+def join_kernel(meta, *refs):
+    me = meta[0] % 4
+    out = refs[4]
+    for j in range(4):
+        out[:, pl.ds(pl.multiple_of((me ^ j) * WIDTH, WIDTH), WIDTH)] = refs[j][...]
+
+
+def join(meta, parts):
+    rows = parts[0].shape[0]
+    return pl.pallas_call(
+        join_kernel,
+        out_shape=jax.ShapeDtypeStruct((rows, 4 * WIDTH), BF16),
+        grid_spec=pltpu.PrefetchScalarGridSpec(
+            num_scalar_prefetch=1,
+            grid=(1,),
+            in_specs=[whole(p.shape) for p in parts],
+            out_specs=whole((rows, 4 * WIDTH)),
+        ),
+        name="join",
+    )(meta, *parts)
+
+
+def pipelined(queries, span_keys, span_values, keys, values, shard_lens, span_starts):
+    n = lax.axis_size("kvp")
+    zs = n // 4
+    meta = jnp.concatenate([lax.axis_index("kvp").astype(jnp.int32)[None], shard_lens, span_starts])
+
+    def within(x, j):
+        return lax.ppermute(x, "kvp", [(i, i ^ j) for i in range(n)])
+
+    def along(x, d):
+        return lax.ppermute(x, "kvp", [(i, (i // 4 + d) % zs * 4 + i % 4) for i in range(n)])
+
+    cut = split(meta, queries, span_keys, span_values, keys, values)
+    q_parts, kv_parts = cut[:4], cut[4:]
+    got = [q_parts[0]] + [within(q_parts[j], j) for j in range(1, 4)]
+    own = (keys, values)
+    kv = {1: within(kv_parts[0], 1), 2: within(kv_parts[1], 2)}
+    last, _ = lax.optimization_barrier((kv_parts[2], kv[2]))
+    kv[3] = within(last, 3)
+    q = {0: jnp.concatenate(got, axis=0)}
+    for d in range(1, zs):
+        q[d] = along(q[0], d)
+
+    s0 = attention(meta, n, {0: q[0]}, {1: kv[1]}, own=own, name="attend_a")
+    s13 = attention(meta, n, {1: q[1], 3: q[3]}, {1: kv[1], 2: kv[2]}, own=own, name="attend_b")
+    s2 = attention(meta, n, {2: q[2]}, {1: kv[1], 2: kv[2]}, own=own, name="attend_c")
+    codes = attention(meta, n, {2: q[2]}, {3: kv[3]}, prior=s2, finish="encode", name="attend_d")
+    codes |= attention(meta, n, {1: q[1], 3: q[3]}, {3: kv[3]}, prior=s13, finish="encode", name="attend_e")
+    back = [along(codes[d], -d) for d in (2, 1, 3)]
+    mine = attention(
+        meta, n, {0: q[0]}, {2: kv[2], 3: kv[3]}, prior=s0, finish="span", before=q[1], name="attend_f"
+    )[0]
+    parts = final(mine, back)
+    parts = [parts[0]] + [within(parts[j], j) for j in range(1, 4)]
+    return join(meta, parts)
 
 
 def softmax_part(query_rows, per_head_keys, per_head_values, visible, scale):
@@ -139,6 +449,12 @@
     )
 
 
+def local(*args):
+    queries, keys = args[0], args[3]
+    four_by_four = lax.axis_size("kvp") == 16 and queries.shape[0] * 4 * 2 == SPAN and keys.shape[0] % 512 == 0
+    return pipelined(*args) if four_by_four else shards(*args)
+
+
 def solution(mesh):
     in_specs = (
         P(("groups", "kvp"), None),
@@ -150,4 +466,4 @@
         P("groups"),
     )
     out_specs = P(("groups", "kvp"), None)
-    return jax.shard_map(shards, mesh=mesh, in_specs=in_specs, out_specs=out_specs, check_vma=False)
+    return jax.shard_map(local, mesh=mesh, in_specs=in_specs, out_specs=out_specs, check_vma=False)

time: 308 us -> 98.8 us (0.32)
  blocking collectives: 133 us -> 0 us
  Pallas kernels: 0 us -> 49.5 us
  local copies, waits for them, and re-layouts: 42.8 us -> 6.36 us
  matrix products: 27.5 us -> 0 us
  other arithmetic: 26.7 us -> 0.65 us
  waiting for transfers between devices: 46.9 us -> 22.4 us
  between operations: 13.6 us -> 0.11 us
  starting transfers between devices: 8.03 us -> 19.2 us
  loops' own time: 8.62 us -> 0 us
    all_gather x2 -> x0, blocking collectives: 124 us -> none  [the longest x1 87.9 us: shards(): lax.all_gather(rotated_span_keys, 'kvp', axis=0, tiled=True)]
    pallas_call x0 -> x9, Pallas kernels: none -> 49.5 us  [the longest x6 38.2 us: attention(): pl.pallas_call(functools.partial(attend_kernel, (shards, blocks, order, o...]
    all_gather x1 -> x0, waiting for transfers between devices: 39.8 us -> none  [shards(): every_query = lax.all_gather(queries, 'kvp', axis=0, tiled=True)]
    dot_general x10 -> x0, matrix products: 27.5 us -> none  [the longest x5 19.6 us: softmax_part(): jnp.einsum('rhgk,khd->rhgd', weights.astype(jnp.bfloat16), per_head_value...]
    ppermute x0 -> x15, waiting for transfers between devices: none -> 22.4 us  [the longest x9 15.5 us: within(): return lax.ppermute(x, 'kvp', [(i, i ^ j) for i in range(n)])]
    ppermute x0 -> x15, starting transfers between devices: none -> 19.2 us  [the longest x6 12.3 us: along(): lax.ppermute(x, 'kvp', [(i, (i // 4 + d) % zs * 4 + i % 4) for i in range...]
    while x18 -> x0, local copies, waits for them, and re-layouts: 18.3 us -> none
    reduce_sum x11 -> x0, other arithmetic: 15.1 us -> none  [the longest x4 10.1 us: softmax_part(): totals = jnp.sum(weights, axis=-1)]
  transfers between devices with their start and end apart: 3 -> 15, of which waited for: 2 -> 4; matrix products, arithmetic and copies ran while one was open for 6% -> 1% of each run, Pallas kernels for 0% -> 34%
where the time goes in v1:
time: 98.8 us; the launch traced here: 98.2 us
  Pallas kernels  49.5 us (50%)
  waiting for transfers between devices  22.4 us (23%)
  starting transfers between devices  19.2 us (19%)
  local copies, waits for them, and re-layouts  6.36 us (6%)
    pallas_call x6, Pallas kernels, attention(): pl.pallas_call(functools.partial(attend_kernel, (shards, blocks, order, o...  38.2 us
    ppermute x9, waiting for transfers between devices, within(): return lax.ppermute(x, 'kvp', [(i, i ^ j) for i in range(n)])  15.5 us
    ppermute x6, starting transfers between devices, along(): lax.ppermute(x, 'kvp', [(i, (i // 4 + d) % zs * 4 + i % 4) for i in range...  12.3 us
    ppermute x6, waiting for transfers between devices, along(): lax.ppermute(x, 'kvp', [(i, (i // 4 + d) % zs * 4 + i % 4) for i in range...  6.92 us
    ppermute x9, starting transfers between devices, within(): return lax.ppermute(x, 'kvp', [(i, i ^ j) for i in range(n)])  6.88 us
    unnamed x33, local copies, waits for them, and re-layouts  6.36 us
    pallas_call x1, Pallas kernels, final(): pl.pallas_call(functools.partial(final_kernel, rows), out_shape=[jax.Shap...  4.66 us
    pallas_call x1, Pallas kernels, split(): pl.pallas_call(functools.partial(split_kernel, rows), out_shape=[jax.Shap...  4.56 us
  transfers between devices with their start and end apart: 15, of which 4 were waited for; matrix products, arithmetic and copies ran while one was open for 1% of the time, Pallas kernels for 34%

profile of v1, /device:TPU:0, one launch (start us, length us, event | category | flops | bytes accessed | tf_op | source)
XLA Modules:
  0.0 98.2 jit_solution(16047277392600920340)
XLA Ops:
  0.0 0.0 copy-start.11
  0.0 0.0 copy-start.12
  0.0 0.7 copy-done.11
  0.7 0.0 copy-done.12
  0.7 0.7 pad_add_fusion.meta
  1.3 4.6 %split.1 = (bf16[16,1280]{1,0:T(8,128)(2,1)}, bf16[16,1280]{1,0:T(8,128)(2,1)}, bf16[16,1280]{1,0:T(8,128)(2,1)}, bf16[16,1280]{1,0:T(8,128)(2,1)}, bf16[1024,25...) custom-call(s32[19]{0:T(128)} %pad_add_fusion.meta, bf16[16,4096]{1,0:T(8,128)(2,1)} %q_ref.1, ...), custom_call_target="tpu_custom_call" | custom-call | tf_op jit(solution)/shard_map/split/pallas_call | solution.py:103
  5.9 0.5 collective-permute-start
  6.4 2.6 %collective-permute-start.1 = (bf16[16,1280]{1,0:T(8,128)(2,1)}, bf16[16,1280]{1,0:T(8,128)(2,1)S(1)}, u32[]{:S(2)}, u32[]{:S(2)}) collective-permute-start(bf16[16,1280]{1,0:T(8,128)(2,1)} %get-tuple-element.31), channel_id=1, source_target_pairs={{0,2},{1,3},{2,0},{3,1},{4,6},{5,7},{6,4},{7,5},{8,10},{9,11},{10,... | collective-permute-start | bytes 122888 | tf_op jit(solution)/shard_map/ppermute | solution.py:296
  9.0 0.0 collective-permute-start.2
  9.0 1.7 %collective-permute-start.3 = (bf16[1024,256]{1,0:T(8,128)(2,1)}, bf16[1024,256]{1,0:T(8,128)(2,1)S(1)}, u32[]{:S(2)}, u32[]{:S(2)}) collective-permute-start(bf16[1024,256]{1,0:T(8,128)(2,1)} %get-tuple-element.33), channel_id=1, source_target_pairs={{0,2},{1,3},{2,0},{3,1},{4,6},{5,7},{6,4},{7,5},{8,10},{9,11},{10,... | collective-permute-start | bytes 1572872 | tf_op jit(solution)/shard_map/ppermute | solution.py:296
  10.8 0.1 collective-permute-start.5
  10.8 0.8 constant_dynamic-update-slice_fusion.3
  11.6 0.0 collective-permute-done
  11.6 0.0 collective-permute-done.1
  11.7 12.6 %collective-permute-done.3.refs_1_.refs_4_.refs_5_ = bf16[1024,256]{1,0:T(8,128)(2,1)S(1)} collective-permute-done((bf16[1024,256]{1,0:T(8,128)(2,1)}, bf16[1024,256]{1,0:T(8,128)(2,1)S(1)}, u32[]{:S(2)}, u32[]{:S(2)}) %collective-permute-start.3) | collective-permute-done | bytes 524320 | tf_op jit(solution)/shard_map/ppermute | solution.py:296
  24.3 0.1 collective-permute-start.4
  24.4 0.0 collective-permute-done.2
  24.4 0.0 copy-start.4
  24.4 2.7 %collective-permute-start.7 = (bf16[64,1280]{1,0:T(8,128)(2,1)S(1)}, bf16[64,1280]{1,0:T(8,128)(2,1)S(1)}, u32[]{:S(2)}, u32[]{:S(2)}) collective-permute-start(bf16[64,1280]{1,0:T(8,128)(2,1)S(1)} %constant_dynamic-update-slice_fusion.refs_0_), channel_id=1, source_target_pairs={{0,8},{1,9},{2,10},{3,11},{4,12},{5,13},{6,14},{7,15},{8,0},{9,1},... | collective-permute-start | bytes 491528 | tf_op jit(solution)/shard_map/ppermute | solution.py:299
  27.1 1.3 %collective-permute-start.9 = (bf16[64,1280]{1,0:T(8,128)(2,1)S(1)}, bf16[64,1280]{1,0:T(8,128)(2,1)S(1)}, u32[]{:S(2)}, u32[]{:S(2)}) collective-permute-start(bf16[64,1280]{1,0:T(8,128)(2,1)S(1)} %constant_dynamic-update-slice_fusion.refs_0_), channel_id=1, source_target_pairs={{0,12},{1,13},{2,14},{3,15},{4,0},{5,1},{6,2},{7,3},{8,4},{9,5},{1... | collective-permute-start | bytes 491528 | tf_op jit(solution)/shard_map/ppermute | solution.py:299
  28.4 0.7 collective-permute-start.6
  29.1 6.9 %collective-permute-done.7.refs_0_ = bf16[64,1280]{1,0:T(8,128)(2,1)S(1)} collective-permute-done((bf16[64,1280]{1,0:T(8,128)(2,1)S(1)}, bf16[64,1280]{1,0:T(8,128)(2,1)S(1)}, u32[]{:S(2)}, u32[]{:S(2)}) %collective-permute-start.7) | collective-permute-done | bytes 163872 | tf_op jit(solution)/shard_map/ppermute | solution.py:299
  36.0 0.0 copy-start.1
  36.0 0.0 collective-permute-done.5.refs_3_.refs_4_
  36.0 0.0 copy-done.3
  36.0 0.7 copy-done.1
  36.7 0.0 copy-start
  36.7 0.8 copy-done
  37.5 5.6 %attend_c.1 = (f32[64,1024]{1,0:T(8,128)}, f32[512,128]{1,0:T(8,128)}) custom-call(s32[19]{0:T(128)} %pad_add_fusion.meta, bf16[64,1280]{1,0:T(8,128)(2,1)} %copy-done.1, bf16[1024,512]{1,0:T(8,128)(2,1)} %refs_2_.5, bf16[1024,512]{1,0:T(8,128)(2,1)} %refs_3_.1, bf16[1024,256]{1,0:T(8,128)(2,1)} %copy-done, bf16[1024,256]{1,0:T(8,128)(2,1)} %copy-done.3), custom_call_target="tpu_custom_call" | custom-call | flops 805306368 | bytes 3309568 | tf_op jit(solution)/shard_map/attend_c/pallas_call | solution.py:217
  43.1 0.0 copy-done.4
  43.1 0.0 collective-permute-done.9.refs_1_
  43.1 0.0 copy-start.14
  43.1 0.0 collective-permute-done.6.refs_5_.refs_0_
  43.1 0.6 copy-done.14
  43.8 0.7 copy-done.13
  44.4 7.8 %attend_b.1 = (f32[64,1024]{1,0:T(8,128)}, f32[512,128]{1,0:T(8,128)}, f32[64,1024]{1,0:T(8,128)}, f32[512,128]{1,0:T(8,128)}) custom-call(s32[19]{0:T(128)} %pad_add_fusion.meta, bf16[64,1280]{1,0:T(8,128)(2,1)} %copy-done.13, bf16[64,1280]{1,0:T(8,128)(2,1)} %copy-done.14, bf16[1024,512]{1,0:T(8,128)(2,1)} %refs_2_.5, bf16[1024,512]{1,0:T(8,128)(2,1)} %refs_3_.1, ...), custom_call_target="tpu_custom_call" | custom-call | flops 1610612736 | bytes 3473408 | tf_op jit(solution)/shard_map/attend_b/pallas_call | solution.py:217
  52.2 0.0 collective-permute-done.4.refs_2_.refs_1_
  52.2 0.8 copy-done.2
  53.0 5.2 %attend_d.1 = s16[64,1152]{1,0:T(8,128)(2,1)} custom-call(s32[19]{0:T(128)} %pad_add_fusion.meta, bf16[64,1280]{1,0:T(8,128)(2,1)} %copy-done.1, bf16[1024,256]{1,0:T(8,128)(2,1)} %copy-done.2, f32[64,1024]{1,0:T(8,128)} %get-tuple-element.41.refs_2_, f32[512,128]{1,0:T(8,128)} %get-tuple-element.42.refs_3_), custom_call_target="tpu_custom_call" | custom-call | flops 268435456 | bytes 950272 | tf_op jit(solution)/shard_map/attend_d/pallas_call | solution.py:217
  58.2 1.8 %collective-permute-start.8 = (s16[64,1152]{1,0:T(8,128)(2,1)}, s16[64,1152]{1,0:T(8,128)(2,1)S(1)}, u32[]{:S(2)}, u32[]{:S(2)}) collective-permute-start(s16[64,1152]{1,0:T(8,128)(2,1)} %attend_d.1), channel_id=1, source_target_pairs={{0,8},{1,9},{2,10},{3,11},{4,12},{5,13},{6,14},{7,15},{8,0},{9,1},... | collective-permute-start | bytes 442376 | tf_op jit(solution)/shard_map/ppermute | solution.py:299
  60.1 7.3 %attend_e.1 = (s16[64,1152]{1,0:T(8,128)(2,1)}, s16[64,1152]{1,0:T(8,128)(2,1)}) custom-call(s32[19]{0:T(128)} %pad_add_fusion.meta, bf16[64,1280]{1,0:T(8,128)(2,1)} %copy-done.13, bf16[64,1280]{1,0:T(8,128)(2,1)} %copy-done.14, bf16[1024,256]{1,0:T(8,128)(2,1)} %copy-done.2, f32[64,1024]{1,0:T(8,128)} %get-tuple-element.43.refs_3_, ...), custom_call_target="tpu_custom_call" | custom-call | flops 536870912 | bytes 1376256 | tf_op jit(solution)/shard_map/attend_e/pallas_call | solution.py:217
  67.4 5.2 %collective-permute-start.10 = (s16[64,1152]{1,0:T(8,128)(2,1)}, s16[64,1152]{1,0:T(8,128)(2,1)S(1)}, u32[]{:S(2)}, u32[]{:S(2)}) collective-permute-start(s16[64,1152]{1,0:T(8,128)(2,1)} %get-tuple-element.47), channel_id=1, source_target_pairs={{0,12},{1,13},{2,14},{3,15},{4,0},{5,1},{6,2},{7,3},{8,4},{9,5},{1... | collective-permute-start | bytes 442376 | tf_op jit(solution)/shard_map/ppermute | solution.py:299
  72.6 0.6 collective-permute-start.11
  73.2 4.8 %attend_a.1 = (f32[64,1024]{1,0:T(8,128)}, f32[512,128]{1,0:T(8,128)}) custom-call(s32[19]{0:T(128)} %pad_add_fusion.meta, bf16[64,1280]{1,0:T(8,128)(2,1)} %copy-done.4, bf16[1024,512]{1,0:T(8,128)(2,1)} %refs_2_.5, bf16[1024,512]{1,0:T(8,128)(2,1)} %refs_3_.1, bf16[1024,256]{1,0:T(8,128)(2,1)} %copy-done), custom_call_target="tpu_custom_call" | custom-call | flops 536870912 | bytes 2785280 | tf_op jit(solution)/shard_map/attend_a/pallas_call | solution.py:217
  78.0 7.4 %attend_f.1 = (f32[64,1024]{1,0:T(8,128)}, f32[512,128]{1,0:T(8,128)}) custom-call(s32[19]{0:T(128)} %pad_add_fusion.meta, bf16[64,1280]{1,0:T(8,128)(2,1)} %copy-done.4, bf16[1024,256]{1,0:T(8,128)(2,1)} %copy-done.3, bf16[1024,256]{1,0:T(8,128)(2,1)} %copy-done.2, f32[64,1024]{1,0:T(8,128)} %get-tuple-element.37.refs_3_, ...), custom_call_target="tpu_custom_call" | custom-call | flops 536870912 | bytes 1638400 | tf_op jit(solution)/shard_map/attend_f/pallas_call | solution.py:217
  85.4 0.0 collective-permute-done.8.refs_0_
  85.4 0.0 collective-permute-done.10.refs_1_
  85.4 0.0 copy-start.6
  85.4 0.0 collective-permute-done.11.refs_2_
  85.4 0.0 copy-start.7
  85.4 0.6 copy-done.5
  86.0 0.1 copy-done.6
  86.1 0.0 copy-done.7
  86.1 4.7 %final.1 = (bf16[16,1024]{1,0:T(8,128)(2,1)}, bf16[16,1024]{1,0:T(8,128)(2,1)}, bf16[16,1024]{1,0:T(8,128)(2,1)}, bf16[16,1024]{1,0:T(8,128)(2,1)}) custom-call(f32[64,1024]{1,0:T(8,128)} %get-tuple-element.39.n_ref, f32[512,128]{1,0:T(8,128)} %get-tuple-element.40.s_ref, s16[64,1152]{1,0:T(8,128)(2,1)} %copy-done.5, s16[64,1152]{1,0:T(8,128)(2,1)} %copy-done.6, ...), custom_call_target="tpu_custom_call" | custom-call | tf_op jit(solution)/shard_map/final/pallas_call | solution.py:261
  90.8 0.0 collective-permute-start.12
  90.8 1.1 %collective-permute-start.13 = (bf16[16,1024]{1,0:T(8,128)(2,1)}, bf16[16,1024]{1,0:T(8,128)(2,1)S(1)}, u32[]{:S(2)}, u32[]{:S(2)}) collective-permute-start(bf16[16,1024]{1,0:T(8,128)(2,1)} %get-tuple-element.51), channel_id=1, source_target_pairs={{0,2},{1,3},{2,0},{3,1},{4,6},{5,7},{6,4},{7,5},{8,10},{9,11},{10,... | collective-permute-start | bytes 98312 | tf_op jit(solution)/shard_map/ppermute | solution.py:296
  91.9 0.7 collective-permute-start.14
  92.7 0.0 collective-permute-done.12.refs_1_
  92.7 2.3 %collective-permute-done.13.refs_2_ = bf16[16,1024]{1,0:T(8,128)(2,1)S(1)} collective-permute-done((bf16[16,1024]{1,0:T(8,128)(2,1)}, bf16[16,1024]{1,0:T(8,128)(2,1)S(1)}, u32[]{:S(2)}, u32[]{:S(2)}) %collective-permute-start.13) | collective-permute-done | bytes 32800 | tf_op jit(solution)/shard_map/ppermute | solution.py:296
  95.0 0.5 collective-permute-done.14.refs_3_
  95.5 0.0 copy-done.8
  95.5 0.1 copy-done.9
  95.6 0.5 copy-done.10
  96.1 2.1 %join.1 = bf16[16,4096]{1,0:T(8,128)(2,1)} custom-call(s32[19]{0:T(128)} %pad_add_fusion.meta, bf16[16,1024]{1,0:T(8,128)(2,1)} %get-tuple-element.49.refs_0_, bf16[16,1024]{1,0:T(8,128)(2,1)} %copy-done.8, bf16[16,1024]{1,0:T(8,128)(2,1)} %copy-done.9, bf16[16,1024]{1,0:T(8,128)(2,1)} %copy-done.10), custom_call_target="tpu_custom_call" | custom-call | tf_op jit(solution)/shard_map/join/pallas_call | solution.py:277
  (10 shorter events, 0.0 us)
Async XLA Ops:
  0.0 0.7 copy-start.11
  0.0 0.7 copy-start.12
  5.9 5.7 %collective-permute-start = (bf16[16,1280]{1,0:T(8,128)(2,1)}, bf16[16,1280]{1,0:T(8,128)(2,1)S(1)}, u32[]{:S(2)}, u32[]{:S(2)}) collective-permute-start(bf16[16,1280]{1,0:T(8,128)(2,1)} %get-tuple-element.30), channel_id=1, source_target_pairs={{0,1},{1,0},{2,3},{3,2},{4,5},{5,4},{6,7},{7,6},{8,9},{9,8},{10,11... | collective-permute-start | bytes 122888 | tf_op jit(solution)/shard_map/ppermute | solution.py:296
  6.4 5.2 %collective-permute-start.1 = (bf16[16,1280]{1,0:T(8,128)(2,1)}, bf16[16,1280]{1,0:T(8,128)(2,1)S(1)}, u32[]{:S(2)}, u32[]{:S(2)}) collective-permute-start(bf16[16,1280]{1,0:T(8,128)(2,1)} %get-tuple-element.31), channel_id=1, source_target_pairs={{0,2},{1,3},{2,0},{3,1},{4,6},{5,7},{6,4},{7,5},{8,10},{9,11},{10,... | collective-permute-start | bytes 122888 | tf_op jit(solution)/shard_map/ppermute | solution.py:296
  9.0 15.4 %collective-permute-start.2 = (bf16[16,1280]{1,0:T(8,128)(2,1)}, bf16[16,1280]{1,0:T(8,128)(2,1)S(1)}, u32[]{:S(2)}, u32[]{:S(2)}) collective-permute-start(bf16[16,1280]{1,0:T(8,128)(2,1)} %get-tuple-element.32), channel_id=1, source_target_pairs={{0,3},{1,2},{2,1},{3,0},{4,7},{5,6},{6,5},{7,4},{8,11},{9,10},{10,... | collective-permute-start | bytes 122888 | tf_op jit(solution)/shard_map/ppermute | solution.py:296
  9.0 15.3 %collective-permute-start.3 = (bf16[1024,256]{1,0:T(8,128)(2,1)}, bf16[1024,256]{1,0:T(8,128)(2,1)S(1)}, u32[]{:S(2)}, u32[]{:S(2)}) collective-permute-start(bf16[1024,256]{1,0:T(8,128)(2,1)} %get-tuple-element.33), channel_id=1, source_target_pairs={{0,2},{1,3},{2,0},{3,1},{4,6},{5,7},{6,4},{7,5},{8,10},{9,11},{10,... | collective-permute-start | bytes 1572872 | tf_op jit(solution)/shard_map/ppermute | solution.py:296
  10.8 25.3 %collective-permute-start.5 = (bf16[1024,256]{1,0:T(8,128)(2,1)}, bf16[1024,256]{1,0:T(8,128)(2,1)S(1)}, u32[]{:S(2)}, u32[]{:S(2)}) collective-permute-start(bf16[1024,256]{1,0:T(8,128)(2,1)} %get-tuple-element.36), channel_id=1, source_target_pairs={{0,1},{1,0},{2,3},{3,2},{4,5},{5,4},{6,7},{7,6},{8,9},{9,8},{10,11... | collective-permute-start | bytes 1572872 | tf_op jit(solution)/shard_map/ppermute | solution.py:296
  24.3 11.7 %copy-start.3 = (bf16[1024,256]{1,0:T(8,128)(2,1)}, bf16[1024,256]{1,0:T(8,128)(2,1)S(1)}, u32[]{:S(2)}) copy-start(bf16[1024,256]{1,0:T(8,128)(2,1)S(1)} %collective-permute-done.3.refs_1_.refs_4_.refs_5_) | copy-start | bytes 1572868
  24.3 27.9 %collective-permute-start.4 = (bf16[1024,256]{1,0:T(8,128)(2,1)}, bf16[1024,256]{1,0:T(8,128)(2,1)S(1)}, u32[]{:S(2)}, u32[]{:S(2)}) collective-permute-start(bf16[1024,256]{1,0:T(8,128)(2,1)} %get-tuple-element.35), channel_id=1, source_target_pairs={{0,3},{1,2},{2,1},{3,0},{4,7},{5,6},{6,5},{7,4},{8,11},{9,10},{10,... | collective-permute-start | bytes 1572872 | tf_op jit(solution)/shard_map/ppermute | solution.py:296
  24.4 18.7 %copy-start.4 = (bf16[64,1280]{1,0:T(8,128)(2,1)}, bf16[64,1280]{1,0:T(8,128)(2,1)S(1)}, u32[]{:S(2)}) copy-start(bf16[64,1280]{1,0:T(8,128)(2,1)S(1)} %constant_dynamic-update-slice_fusion.refs_0_) | copy-start | bytes 491524
  24.4 11.6 %collective-permute-start.7 = (bf16[64,1280]{1,0:T(8,128)(2,1)S(1)}, bf16[64,1280]{1,0:T(8,128)(2,1)S(1)}, u32[]{:S(2)}, u32[]{:S(2)}) collective-permute-start(bf16[64,1280]{1,0:T(8,128)(2,1)S(1)} %constant_dynamic-update-slice_fusion.refs_0_), channel_id=1, source_target_pairs={{0,8},{1,9},{2,10},{3,11},{4,12},{5,13},{6,14},{7,15},{8,0},{9,1},... | collective-permute-start | bytes 491528 | tf_op jit(solution)/shard_map/ppermute | solution.py:299
  27.1 16.0 %collective-permute-start.9 = (bf16[64,1280]{1,0:T(8,128)(2,1)S(1)}, bf16[64,1280]{1,0:T(8,128)(2,1)S(1)}, u32[]{:S(2)}, u32[]{:S(2)}) collective-permute-start(bf16[64,1280]{1,0:T(8,128)(2,1)S(1)} %constant_dynamic-update-slice_fusion.refs_0_), channel_id=1, source_target_pairs={{0,12},{1,13},{2,14},{3,15},{4,0},{5,1},{6,2},{7,3},{8,4},{9,5},{1... | collective-permute-start | bytes 491528 | tf_op jit(solution)/shard_map/ppermute | solution.py:299
  28.4 14.7 %collective-permute-start.6 = (bf16[64,1280]{1,0:T(8,128)(2,1)S(1)}, bf16[64,1280]{1,0:T(8,128)(2,1)S(1)}, u32[]{:S(2)}, u32[]{:S(2)}) collective-permute-start(bf16[64,1280]{1,0:T(8,128)(2,1)S(1)} %constant_dynamic-update-slice_fusion.refs_0_), channel_id=1, source_target_pairs={{0,4},{1,5},{2,6},{3,7},{4,8},{5,9},{6,10},{7,11},{8,12},{9,13},{1... | collective-permute-start | bytes 491528 | tf_op jit(solution)/shard_map/ppermute | solution.py:299
  36.0 0.7 copy-start.1
  36.7 0.8 copy-start
  43.1 0.7 copy-start.14
  43.8 0.7 copy-start.13
  52.2 0.8 copy-start.2
  58.2 27.2 %collective-permute-start.8 = (s16[64,1152]{1,0:T(8,128)(2,1)}, s16[64,1152]{1,0:T(8,128)(2,1)S(1)}, u32[]{:S(2)}, u32[]{:S(2)}) collective-permute-start(s16[64,1152]{1,0:T(8,128)(2,1)} %attend_d.1), channel_id=1, source_target_pairs={{0,8},{1,9},{2,10},{3,11},{4,12},{5,13},{6,14},{7,15},{8,0},{9,1},... | collective-permute-start | bytes 442376 | tf_op jit(solution)/shard_map/ppermute | solution.py:299
  67.4 18.0 %collective-permute-start.10 = (s16[64,1152]{1,0:T(8,128)(2,1)}, s16[64,1152]{1,0:T(8,128)(2,1)S(1)}, u32[]{:S(2)}, u32[]{:S(2)}) collective-permute-start(s16[64,1152]{1,0:T(8,128)(2,1)} %get-tuple-element.47), channel_id=1, source_target_pairs={{0,12},{1,13},{2,14},{3,15},{4,0},{5,1},{6,2},{7,3},{8,4},{9,5},{1... | collective-permute-start | bytes 442376 | tf_op jit(solution)/shard_map/ppermute | solution.py:299
  72.6 12.8 %collective-permute-start.11 = (s16[64,1152]{1,0:T(8,128)(2,1)}, s16[64,1152]{1,0:T(8,128)(2,1)S(1)}, u32[]{:S(2)}, u32[]{:S(2)}) collective-permute-start(s16[64,1152]{1,0:T(8,128)(2,1)} %get-tuple-element.48), channel_id=1, source_target_pairs={{0,4},{1,5},{2,6},{3,7},{4,8},{5,9},{6,10},{7,11},{8,12},{9,13},{1... | collective-permute-start | bytes 442376 | tf_op jit(solution)/shard_map/ppermute | solution.py:299
  85.4 0.7 copy-start.5
  85.4 0.7 copy-start.6
  85.4 0.7 copy-start.7
  90.8 1.9 %collective-permute-start.12 = (bf16[16,1024]{1,0:T(8,128)(2,1)}, bf16[16,1024]{1,0:T(8,128)(2,1)S(1)}, u32[]{:S(2)}, u32[]{:S(2)}) collective-permute-start(bf16[16,1024]{1,0:T(8,128)(2,1)} %get-tuple-element.50), channel_id=1, source_target_pairs={{0,1},{1,0},{2,3},{3,2},{4,5},{5,4},{6,7},{7,6},{8,9},{9,8},{10,11... | collective-permute-start | bytes 98312 | tf_op jit(solution)/shard_map/ppermute | solution.py:296
  90.8 4.2 %collective-permute-start.13 = (bf16[16,1024]{1,0:T(8,128)(2,1)}, bf16[16,1024]{1,0:T(8,128)(2,1)S(1)}, u32[]{:S(2)}, u32[]{:S(2)}) collective-permute-start(bf16[16,1024]{1,0:T(8,128)(2,1)} %get-tuple-element.51), channel_id=1, source_target_pairs={{0,2},{1,3},{2,0},{3,1},{4,6},{5,7},{6,4},{7,5},{8,10},{9,11},{10,... | collective-permute-start | bytes 98312 | tf_op jit(solution)/shard_map/ppermute | solution.py:296
  91.9 3.6 %collective-permute-start.14 = (bf16[16,1024]{1,0:T(8,128)(2,1)}, bf16[16,1024]{1,0:T(8,128)(2,1)S(1)}, u32[]{:S(2)}, u32[]{:S(2)}) collective-permute-start(bf16[16,1024]{1,0:T(8,128)(2,1)} %get-tuple-element.52), channel_id=1, source_target_pairs={{0,3},{1,2},{2,1},{3,0},{4,7},{5,6},{6,5},{7,4},{8,11},{9,10},{10,... | collective-permute-start | bytes 98312 | tf_op jit(solution)/shard_map/ppermute | solution.py:296
  92.7 2.8 %copy-start.8 = (bf16[16,1024]{1,0:T(8,128)(2,1)}, bf16[16,1024]{1,0:T(8,128)(2,1)S(1)}, u32[]{:S(2)}) copy-start(bf16[16,1024]{1,0:T(8,128)(2,1)S(1)} %collective-permute-done.12.refs_1_) | copy-start | bytes 98308
  95.0 0.6 copy-start.9
  95.5 0.6 copy-start.10

commit v2 on v0

--- a/solution.py
+++ b/solution.py
@@ -1,6 +1,11 @@
+import functools
+
 import jax
 import jax.numpy as jnp
+import numpy as np
 from jax import lax
+from jax.experimental import pallas as pl
+from jax.experimental.pallas import tpu as pltpu
 from jax.sharding import PartitionSpec as P
 
 QUERY_HEADS = 32
@@ -8,9 +13,277 @@
 HEAD_SIZE = 128
 SPAN = 128
 SPANS = 2
-
-
+GROUP = QUERY_HEADS // KEY_VALUE_HEADS
+WIDTH = GROUP * HEAD_SIZE
 NEG_LARGE = -1e30
+LOG2_SCALE = float(HEAD_SIZE**-0.5 * np.log2(np.e))
+CODE = 32767.0
+VMEM_GRANT = 24 * 2**20
+F32, BF16, I16 = jnp.float32, jnp.bfloat16, jnp.int16
+
+
+def row_limit(lens, starts, shard, span, shards, slots):
+    start = jnp.int32(0)
+    length = jnp.int32(0)
+    for j in range(shards):
+        n = lens[j]
+        start = start + jnp.where(j < shard, n, 0)
+        length = jnp.where(j == shard, n, length)
+    limit = starts[0]
+    for j in range(1, SPANS):
+        limit = jnp.where(span == j, starts[j], limit)
+    return jnp.clip(jnp.minimum(length, limit - start), 0, slots)
+
+
+def stack_heads(q):
+    return jnp.concatenate([q[:, g * HEAD_SIZE : (g + 1) * HEAD_SIZE] for g in range(GROUP)], axis=0)
+
+
+def attend(q, k, v, bias):
+    s = lax.dot_general(q, k, (((1,), (1,)), ((), ())), preferred_element_type=F32) + bias
+    m = jnp.max(s, axis=1, keepdims=True)
+    w = jnp.exp2((s - m) * LOG2_SCALE)
+    t = jnp.sum(w, axis=1, keepdims=True)
+    n = jnp.dot(w.astype(BF16), v, preferred_element_type=F32)
+    return n, m, t
+
+
+def merge(a, b):
+    if a is None:
+        return b
+    m = jnp.maximum(a[1], b[1])
+    fa, fb = jnp.exp2((a[1] - m) * LOG2_SCALE), jnp.exp2((b[1] - m) * LOG2_SCALE)
+    return a[0] * fa + b[0] * fb, m, a[2] * fa + b[2] * fb
+
+
+def encode(state, out_ref, rows):
+    n, m, t = state
+    top = jnp.maximum(jnp.max(jnp.abs(n), axis=1, keepdims=True), 1e-30)
+    codes = jnp.round(n * (CODE / top)).astype(jnp.int32).astype(I16)
+    lane = lax.broadcasted_iota(jnp.int32, (rows, HEAD_SIZE), 1)
+    base = jnp.zeros((rows, HEAD_SIZE), F32)
+    value = jnp.ones((rows, HEAD_SIZE), F32)
+    for g in range(GROUP):
+        head = slice(g * rows, (g + 1) * rows)
+        out_ref[:, g * HEAD_SIZE : (g + 1) * HEAD_SIZE] = codes[head]
+        base = jnp.where(lane % GROUP == g, m[head], base)
+        value = jnp.where(lane % GROUP == g, jnp.where(lane < 2 * GROUP, top[head], t[head]), value)
+    value = jnp.maximum(base * LOG2_SCALE + jnp.log2(value), -2000.0)
+    high = jnp.round(value * 16.0)
+    low = jnp.round((value - high * (1 / 16.0)) * 524288.0)
+    stats = jnp.where(lane % (2 * GROUP) < GROUP, high, low)
+    out_ref[:, WIDTH:] = stats.astype(jnp.int32).astype(I16)
+
+
+def columns(j, width):
+    return pl.ds(pl.multiple_of(((lax.axis_index("kvp") % 4) ^ j) * width, width), width)
+
+
+def local_call(kernel, shapes, args, tables=(), work=0, scratch=(), space=pltpu.VMEM):
+    moved = sum(x.size * x.dtype.itemsize for x in args)
+    return pl.pallas_call(
+        kernel,
+        out_shape=[jax.ShapeDtypeStruct(s, t) for s, t in shapes],
+        in_specs=[pl.BlockSpec(memory_space=pltpu.SMEM)] * len(tables)
+        + [pl.BlockSpec(memory_space=space)] * len(args),
+        out_specs=[pl.BlockSpec(memory_space=pltpu.VMEM)] * len(shapes),
+        scratch_shapes=scratch,
+        compiler_params=pltpu.CompilerParams(vmem_limit_bytes=VMEM_GRANT),
+        cost_estimate=pl.CostEstimate(flops=4 * HEAD_SIZE * work, transcendentals=work, bytes_accessed=moved),
+    )(*tables, *args)
+
+
+def split_kernel(shards, lens, starts, q_ref, sk_ref, sv_ref, k_ref, v_ref, *refs):
+    outs, bias_ref, sems = refs[:8], refs[8], refs[9]
+    copies = []
+
+    def copy(src, dst):
+        copies.append(pltpu.make_async_copy(src, dst, sems.at[len(copies)]))
+        copies[-1].start()
+
+    for j in (2, 3, 1, 0):
+        at = columns(j, HEAD_SIZE)
+        copy(q_ref.at[:, columns(j, WIDTH)], outs[j].at[:, pl.ds(0, WIDTH)])
+        copy(sk_ref.at[:, at], outs[j].at[:, pl.ds(WIDTH, HEAD_SIZE)])
+        copy(sv_ref.at[:, at], outs[j].at[:, pl.ds(WIDTH + HEAD_SIZE, HEAD_SIZE)])
+    for j in (2, 3, 1, 0):
+        at = columns(j, HEAD_SIZE)
+        copy(k_ref.at[:, at], outs[4 + j].at[:, pl.ds(0, HEAD_SIZE)])
+        copy(v_ref.at[:, at], outs[4 + j].at[:, pl.ds(HEAD_SIZE, HEAD_SIZE)])
+    me = lax.axis_index("kvp")
+    slots = k_ref.shape[0]
+    lane = lax.broadcasted_iota(jnp.int32, (1, slots), 1)
+    for span in range(SPANS):
+        for j in range(4):
+            seen = row_limit(lens, starts, me // 4 * 4 + ((me % 4) ^ j), span, shards, slots)
+            bias_ref[span * 4 + j : span * 4 + j + 1, :] = jnp.where(lane < seen, 0.0, NEG_LARGE)
+    for c in copies:
+        c.wait()
+
+
+def stack_kernel(*refs):
+    rows = refs[0].shape[0]
+    for j, ref in enumerate(refs[:-1]):
+        refs[-1][j * rows : (j + 1) * rows, :] = ref[...]
+
+
+def attend_kernel(cfg, bias_ref, *refs):
+    shards, blocks, pieces, prior, finish, rows = cfg
+    refs = list(refs)
+    q_refs = [refs.pop(0) for _ in blocks]
+    kv = [refs.pop(0) for _ in pieces]
+    prior_refs = [(refs.pop(0), refs.pop(0)) for _ in blocks] if prior else None
+    span_ref = refs.pop(0) if finish == "span" else None
+    outs = refs
+    me = lax.axis_index("kvp")
+    zs = shards // 4
+    z, b = me // 4, me % 4
+    for i, d in enumerate(blocks):
+        q = stack_heads(q_refs[i][:, :WIDTH])
+        span = lax.rem(z - d + zs, zs) * rows // SPAN
+        state = None
+        if prior:
+            p_ref, s_ref = prior_refs[i]
+            state = (
+                jnp.concatenate([p_ref[:, g * HEAD_SIZE : (g + 1) * HEAD_SIZE] for g in range(GROUP)], axis=0),
+                s_ref[:, :HEAD_SIZE],
+                s_ref[:, HEAD_SIZE:],
+            )
+        for j, kv_ref in zip(pieces, kv):
+            bias = bias_ref[pl.ds(span * 4 + j, 1), :]
+            state = merge(state, attend(q, kv_ref[:, :HEAD_SIZE], kv_ref[:, HEAD_SIZE:], bias))
+        if finish == "encode":
+            encode(state, outs[i], rows)
+            continue
+        if finish == "span":
+            mine, before = q_refs[i], span_ref
+            k = jnp.concatenate([mine[:, WIDTH : WIDTH + HEAD_SIZE], before[:, WIDTH : WIDTH + HEAD_SIZE]], axis=0)
+            v = jnp.concatenate([mine[:, WIDTH + HEAD_SIZE :], before[:, WIDTH + HEAD_SIZE :]], axis=0)
+            s = lax.dot_general(q, k, (((1,), (1,)), ((), ())), preferred_element_type=F32)
+            part = rows // 4
+            r = lax.broadcasted_iota(jnp.int32, s.shape, 0) % rows
+            c = lax.broadcasted_iota(jnp.int32, s.shape, 1)
+            r = ((r // part) ^ b) * part + r % part
+            here = (((c // part) ^ b) * part + c % part <= r) & (c < rows)
+            earlier = (c >= rows) & ((z * rows) % SPAN > 0)
+            visible = here | earlier
+            s = jnp.where(visible, s, NEG_LARGE)
+            m = jnp.max(s, axis=1, keepdims=True)
+            w = jnp.where(visible, jnp.exp2((s - m) * LOG2_SCALE), 0.0)
+            t = jnp.sum(w, axis=1, keepdims=True)
+            state = merge(state, (jnp.dot(w.astype(BF16), v, preferred_element_type=F32), m, t))
+        n, m, t = state
+        for g in range(GROUP):
+            outs[2 * i][:, g * HEAD_SIZE : (g + 1) * HEAD_SIZE] = n[g * rows : (g + 1) * rows]
+        outs[2 * i + 1][:, :HEAD_SIZE] = jnp.broadcast_to(m, n.shape)
+        outs[2 * i + 1][:, HEAD_SIZE:] = jnp.broadcast_to(t, n.shape)
+
+
+def attention(bias, shards, q, pieces, prior=None, finish=None, before=None):
+    blocks = tuple(q)
+    rows = q[blocks[0]].shape[0]
+    args = [bias] + [q[d] for d in blocks] + [pieces[j] for j in pieces]
+    if prior is not None:
+        args += [x for d in blocks for x in prior[d]]
+    if finish == "span":
+        args.append(before)
+    if finish == "encode":
+        shapes = [((rows, WIDTH + HEAD_SIZE), I16)] * len(blocks)
+    else:
+        shapes = [((rows, WIDTH), F32), ((GROUP * rows, 2 * HEAD_SIZE), F32)] * len(blocks)
+    work = len(blocks) * GROUP * rows * sum(x.shape[0] for x in pieces.values())
+    cfg = (shards, blocks, tuple(pieces), prior is not None, finish, rows)
+    outs = local_call(functools.partial(attend_kernel, cfg), shapes, args, work=work)
+    if finish == "encode":
+        return dict(zip(blocks, outs))
+    return {d: (outs[2 * i], outs[2 * i + 1]) for i, d in enumerate(blocks)}
+
+
+def final_kernel(rows, n_ref, s_ref, *refs):
+    codes, outs = refs[:3], refs[3:]
+    part = rows // 4
+    lane = lax.broadcasted_iota(jnp.int32, (rows, HEAD_SIZE), 1)
+    m = jnp.zeros((rows, HEAD_SIZE), F32)
+    t = jnp.zeros((rows, HEAD_SIZE), F32)
+    for g in range(GROUP):
+        head = slice(g * rows, (g + 1) * rows)
+        m = jnp.where(lane == g, s_ref[head, :HEAD_SIZE], m)
+        t = jnp.where(lane == g, s_ref[head, HEAD_SIZE:], t)
+    m = m * LOG2_SCALE
+    tops, sums = [], []
+    for c in codes:
+        x = c[:, WIDTH:].astype(F32)
+        x = x * (1 / 16.0) + pltpu.roll(x, HEAD_SIZE - GROUP, 1) * (1 / 524288.0)
+        tops.append(x)
+        sums.append(pltpu.roll(x, HEAD_SIZE - 2 * GROUP, 1))
+    over = m
+    for x in sums:
+        over = jnp.maximum(over, x)
+    mine = jnp.exp2(m - over)
+    total = t * mine
+    for x in sums:
+        total = total + jnp.exp2(x - over)
+    inverse = 1.0 / jnp.where(lane < GROUP, total, 1.0)
+    factors = [mine * inverse] + [jnp.exp2(jnp.where(lane < GROUP, x - over, 0.0)) * (inverse * (1 / CODE)) for x in tops]
+    for g in range(GROUP):
+        cols = slice(g * HEAD_SIZE, (g + 1) * HEAD_SIZE)
+        n = n_ref[:, cols] * factors[0][:, g : g + 1]
+        for c, f in zip(codes, factors[1:]):
+            n = n + c[:, cols].astype(F32) * f[:, g : g + 1]
+        n = n.astype(BF16)
+        for k in range(4):
+            outs[k][:, cols] = n[k * part : (k + 1) * part]
+
+
+def join_kernel(*refs):
+    for j in range(4):
+        refs[4][:, columns(j, WIDTH)] = refs[j][...]
+
+
+def pipelined(queries, span_keys, span_values, keys, values, shard_lens, span_starts):
+    n = lax.axis_size("kvp")
+    zs = n // 4
+    tables = (shard_lens, span_starts)
+
+    def within(x, j):
+        return lax.ppermute(x, "kvp", [(i, i ^ j) for i in range(n)])
+
+    def along(x, d):
+        return lax.ppermute(x, "kvp", [(i, (i // 4 + d) % zs * 4 + i % 4) for i in range(n)])
+
+    def attend(*args, **kwargs):
+        return attention(bias, n, *args, **kwargs)
+
+    part, slots = queries.shape[0], keys.shape[0]
+    wide = WIDTH + 2 * HEAD_SIZE
+    *cut, bias = local_call(
+        functools.partial(split_kernel, n),
+        [((part, wide), BF16)] * 4 + [((slots, 2 * HEAD_SIZE), BF16)] * 4 + [((SPANS * 4, slots), F32)],
+        (queries, span_keys, span_values, keys, values),
+        tables=tables,
+        scratch=[pltpu.SemaphoreType.DMA((20,))],
+        space=pltpu.HBM,
+    )
+    q_parts, kv_parts = cut[:4], cut[4:]
+    q_parts = [q_parts[0]] + [within(q_parts[j], j) for j in range(1, 4)]
+    kv = {0: kv_parts[0]} | {j: within(kv_parts[j], j) for j in (2, 3, 1)}
+    q = {0: local_call(stack_kernel, [((4 * part, wide), BF16)], q_parts)[0]}
+    for d in range(1, zs):
+        q[d] = along(q[0], d)
+
+    near = {j: kv[j] for j in (0, 1)}
+    s0 = attend({0: q[0]}, near)
+    s13 = attend({1: q[1], 3: q[3]}, near)
+    s2 = attend({2: q[2]}, near)
+    kv[2], kv[3], s0, s13, s2 = lax.optimization_barrier((kv[2], kv[3], s0, s13, s2))
+    far = {j: kv[j] for j in (2, 3)}
+    codes = attend({2: q[2]}, far, prior=s2, finish="encode")
+    codes |= attend({1: q[1], 3: q[3]}, far, prior=s13, finish="encode")
+    back = [along(codes[d], -d) for d in (2, 1, 3)]
+    mine = attend({0: q[0]}, far, prior=s0, finish="span", before=q[1])[0]
+    parts = local_call(functools.partial(final_kernel, q[0].shape[0]), [((part, WIDTH), BF16)] * 4, (*mine, *back))
+    parts = [parts[0]] + [within(parts[j], j) for j in range(1, 4)]
+    return local_call(join_kernel, [((part, 4 * WIDTH), BF16)], parts)[0]
 
 
 def softmax_part(query_rows, per_head_keys, per_head_values, visible, scale):
@@ -139,6 +412,14 @@
     )
 
 
+def local(*args):
+    queries, keys = args[0], args[3]
+    four_by_four = lax.axis_size("kvp") == 16 and queries.shape[0] * 4 * 2 == SPAN and keys.shape[0] % 512 == 0
+    if not four_by_four:
+        return shards(*args)
+    return pipelined(*args)
+
+
 def solution(mesh):
     in_specs = (
         P(("groups", "kvp"), None),
@@ -150,4 +431,4 @@
         P("groups"),
     )
     out_specs = P(("groups", "kvp"), None)
-    return jax.shard_map(shards, mesh=mesh, in_specs=in_specs, out_specs=out_specs, check_vma=False)
+    return jax.shard_map(local, mesh=mesh, in_specs=in_specs, out_specs=out_specs, check_vma=False)

time: 308 us -> 84.6 us (0.27)
  blocking collectives: 133 us -> 0 us
  local copies, waits for them, and re-layouts: 42.8 us -> 6.1 us
  matrix products: 27.5 us -> 0 us
  other arithmetic: 26.7 us -> 0 us
  Pallas kernels: 0 us -> 18.7 us
  between operations: 13.6 us -> 0.11 us
  starting transfers between devices: 8.03 us -> 19.9 us
  loops' own time: 8.62 us -> 0 us
  waiting for transfers between devices: 46.9 us -> 39.4 us
    all_gather x2 -> x0, blocking collectives: 124 us -> none  [the longest x1 87.9 us: shards(): lax.all_gather(rotated_span_keys, 'kvp', axis=0, tiled=True)]
    all_gather x1 -> x0, waiting for transfers between devices: 39.8 us -> none  [shards(): every_query = lax.all_gather(queries, 'kvp', axis=0, tiled=True)]
    ppermute x0 -> x15, waiting for transfers between devices: none -> 39.4 us  [the longest x9 25.4 us: within(): return lax.ppermute(x, 'kvp', [(i, i ^ j) for i in range(n)])]
    dot_general x10 -> x0, matrix products: 27.5 us -> none  [the longest x5 19.6 us: softmax_part(): jnp.einsum('rhgk,khd->rhgd', weights.astype(jnp.bfloat16), per_head_value...]
    ppermute x0 -> x15, starting transfers between devices: none -> 19.9 us  [the longest x6 11.9 us: along(): lax.ppermute(x, 'kvp', [(i, (i // 4 + d) % zs * 4 + i % 4) for i in range...]
    pallas_call x0 -> x10, Pallas kernels: none -> 18.7 us  [local_call(): pl.pallas_call(kernel, out_shape=[jax.ShapeDtypeStruct(s, t) for s, t in...]
    while x18 -> x0, local copies, waits for them, and re-layouts: 18.3 us -> none
    reduce_sum x11 -> x0, other arithmetic: 15.1 us -> none  [the longest x4 10.1 us: softmax_part(): totals = jnp.sum(weights, axis=-1)]
  transfers between devices with their start and end apart: 3 -> 15, of which waited for: 2 -> 8; matrix products, arithmetic and copies ran while one was open for 6% -> 0% of each run, Pallas kernels for 0% -> 15%
where the time goes in v2:
time: 84.6 us; the launch traced here: 84.3 us
  waiting for transfers between devices  39.4 us (47%)
  starting transfers between devices  19.9 us (24%)
  Pallas kernels  18.7 us (22%)
  local copies, waits for them, and re-layouts  6.1 us (7%)
    ppermute x9, waiting for transfers between devices, within(): return lax.ppermute(x, 'kvp', [(i, i ^ j) for i in range(n)])  25.4 us
    pallas_call x10, Pallas kernels, local_call(): pl.pallas_call(kernel, out_shape=[jax.ShapeDtypeStruct(s, t) for s, t in...  18.7 us
    ppermute x6, waiting for transfers between devices, along(): lax.ppermute(x, 'kvp', [(i, (i // 4 + d) % zs * 4 + i % 4) for i in range...  14.1 us
    ppermute x6, starting transfers between devices, along(): lax.ppermute(x, 'kvp', [(i, (i // 4 + d) % zs * 4 + i % 4) for i in range...  11.9 us
    ppermute x9, starting transfers between devices, within(): return lax.ppermute(x, 'kvp', [(i, i ^ j) for i in range(n)])  8.02 us
    unnamed x14, local copies, waits for them, and re-layouts  6.1 us
  transfers between devices with their start and end apart: 15, of which 8 were waited for; matrix products, arithmetic and copies ran while one was open for 0% of the time, Pallas kernels for 15%

profile of v2, /device:TPU:0, one launch (start us, length us, event | category | flops | bytes accessed | tf_op | source)
XLA Modules:
  0.0 84.3 jit_solution(13421527647725590184)
XLA Ops:
  0.0 0.0 copy-start
  0.0 1.2 %copy-done = bf16[1024,512]{1,0:T(8,128)(2,1)S(1)} copy-done((bf16[1024,512]{1,0:T(8,128)(2,1)S(1)}, bf16[1024,512]{1,0:T(8,128)(2,1)}, u32[]{:S(2)}) %copy-start) | copy-done | bytes 1048600
  1.2 0.0 copy-start.1
  1.2 1.2 %copy-done.1 = bf16[1024,512]{1,0:T(8,128)(2,1)S(1)} copy-done((bf16[1024,512]{1,0:T(8,128)(2,1)S(1)}, bf16[1024,512]{1,0:T(8,128)(2,1)}, u32[]{:S(2)}) %copy-start.1) | copy-done | bytes 1048600
  2.5 0.0 copy-start.2
  2.5 0.9 %copy-done.2 = bf16[16,4096]{1,0:T(8,128)(2,1)S(1)} copy-done((bf16[16,4096]{1,0:T(8,128)(2,1)S(1)}, bf16[16,4096]{1,0:T(8,128)(2,1)}, u32[]{:S(2)}) %copy-start.2) | copy-done | bytes 131096
  3.4 0.0 copy-start.3
  3.4 0.7 copy-done.3
  4.1 0.0 copy-start.4
  4.1 0.7 copy-done.4
  4.8 0.0 copy-start.5
  4.8 0.7 copy-done.5
  5.4 0.0 copy-start.6
  5.4 0.7 copy-done.6
  6.1 1.5 %shard_map.73 = (bf16[16,1280]{1,0:T(8,128)(2,1)S(1)}, bf16[16,1280]{1,0:T(8,128)(2,1)S(1)}, bf16[16,1280]{1,0:T(8,128)(2,1)S(1)}, bf16[16,1280]{1,0:T(8,128)(2,...) custom-call(s32[16]{0:T(128)S(1)} %copy-done.5, ...), custom_call_target="tpu_custom_call" | custom-call | bytes 2260992 | tf_op jit(solution)/shard_map/pallas_call | solution.py:84
  7.6 0.6 collective-permute-start.5
  8.2 2.6 %collective-permute-start.3 = (bf16[1024,256]{1,0:T(8,128)(2,1)S(1)}, bf16[1024,256]{1,0:T(8,128)(2,1)S(1)}, u32[]{:S(2)}, u32[]{:S(2)}) collective-permute-start(bf16[1024,256]{1,0:T(8,128)(2,1)S(1)} %get-tuple-element.45), channel_id=1, source_target_pairs={{0,2},{1,3},{2,0},{3,1},{4,6},{5,7},{6,4},{7,5},{8,10},{9,11},{10,... | collective-permute-start | bytes 1572872 | tf_op jit(solution)/shard_map/ppermute | solution.py:249
  10.8 0.0 collective-permute-start.4
  10.8 0.2 collective-permute-start
  11.0 1.9 %collective-permute-start.1 = (bf16[16,1280]{1,0:T(8,128)(2,1)S(1)}, bf16[16,1280]{1,0:T(8,128)(2,1)S(1)}, u32[]{:S(2)}, u32[]{:S(2)}) collective-permute-start(bf16[16,1280]{1,0:T(8,128)(2,1)S(1)} %get-tuple-element.43), channel_id=1, source_target_pairs={{0,2},{1,3},{2,0},{3,1},{4,6},{5,7},{6,4},{7,5},{8,10},{9,11},{10,... | collective-permute-start | bytes 122888 | tf_op jit(solution)/shard_map/ppermute | solution.py:249
  12.9 0.0 collective-permute-done.refs_1_
  12.9 0.8 collective-permute-start.2
  13.7 21.9 %collective-permute-done.1.refs_2_ = bf16[16,1280]{1,0:T(8,128)(2,1)S(1)} collective-permute-done((bf16[16,1280]{1,0:T(8,128)(2,1)S(1)}, bf16[16,1280]{1,0:T(8,128)(2,1)S(1)}, u32[]{:S(2)}, u32[]{:S(2)}) %collective-permute-start.1) | collective-permute-done | bytes 40992 | tf_op jit(solution)/shard_map/ppermute | solution.py:249
  35.6 0.4 collective-permute-done.2.refs_3_
  36.0 2.7 %collective-permute-start.8 = (bf16[64,1280]{1,0:T(8,128)(2,1)S(1)}, bf16[64,1280]{1,0:T(8,128)(2,1)S(1)}, u32[]{:S(2)}, u32[]{:S(2)}) collective-permute-start(bf16[64,1280]{1,0:T(8,128)(2,1)S(1)} %shard_map.74.refs_0_), channel_id=1, source_target_pairs={{0,8},{1,9},{2,10},{3,11},{4,12},{5,13},{6,14},{7,15},{8,0},{9,1},... | collective-permute-start | bytes 491528 | tf_op jit(solution)/shard_map/ppermute | solution.py:252
  38.7 1.3 %collective-permute-start.7 = (bf16[64,1280]{1,0:T(8,128)(2,1)S(1)}, bf16[64,1280]{1,0:T(8,128)(2,1)S(1)}, u32[]{:S(2)}, u32[]{:S(2)}) collective-permute-start(bf16[64,1280]{1,0:T(8,128)(2,1)S(1)} %shard_map.74.refs_0_), channel_id=1, source_target_pairs={{0,12},{1,13},{2,14},{3,15},{4,0},{5,1},{6,2},{7,3},{8,4},{9,5},{1... | collective-permute-start | bytes 491528 | tf_op jit(solution)/shard_map/ppermute | solution.py:252
  40.1 0.0 collective-permute-done.5.refs_2_.refs_3_
  40.1 0.7 collective-permute-start.6
  40.8 2.1 %shard_map.75 = (f32[64,1024]{1,0:T(8,128)S(1)}, f32[512,256]{1,0:T(8,128)S(1)}) custom-call(f32[8,1024]{1,0:T(8,128)S(1)} %get-tuple-element.40.bias_ref, bf16[64,1280]{1,0:T(8,128)(2,1)S(1)} %shard_map.74.refs_0_, bf16[1024,256]{1,0:T(8,128)(2,1)S(1)} %get-tuple-element.47.refs_1_.refs_2_, bf16[1024,256]{1,0:T(8,128)(2,1)S(1)} %collective-permute-done.5.refs_2_.refs_3_), custom_call_target="tpu_custom_call" | custom-call | flops 536870912 | bytes 1245184 | tf_op jit(solution)/shard_map/pallas_call | solution.py:84
  42.9 5.1 %collective-permute-done.8.refs_0_ = bf16[64,1280]{1,0:T(8,128)(2,1)S(1)} collective-permute-done((bf16[64,1280]{1,0:T(8,128)(2,1)S(1)}, bf16[64,1280]{1,0:T(8,128)(2,1)S(1)}, u32[]{:S(2)}, u32[]{:S(2)}) %collective-permute-start.8) | collective-permute-done | bytes 163872 | tf_op jit(solution)/shard_map/ppermute | solution.py:252
  48.0 2.1 %shard_map.77 = (f32[64,1024]{1,0:T(8,128)S(1)}, f32[512,256]{1,0:T(8,128)S(1)}) custom-call(f32[8,1024]{1,0:T(8,128)S(1)} %get-tuple-element.40.bias_ref, bf16[64,1280]{1,0:T(8,128)(2,1)S(1)} %collective-permute-done.8.refs_0_, bf16[1024,256]{1,0:T(8,128)(2,1)S(1)} %get-tuple-element.47.refs_1_.refs_2_, ...), custom_call_target="tpu_custom_call" | custom-call | flops 536870912 | bytes 1245184 | tf_op jit(solution)/shard_map/pallas_call | solution.py:84
  50.1 0.0 collective-permute-done.7.refs_1_
  50.1 1.5 %collective-permute-done.6.refs_0_.refs_5_ = bf16[64,1280]{1,0:T(8,128)(2,1)S(1)} collective-permute-done((bf16[64,1280]{1,0:T(8,128)(2,1)S(1)}, bf16[64,1280]{1,0:T(8,128)(2,1)S(1)}, u32[]{:S(2)}, u32[]{:S(2)}) %collective-permute-start.6) | collective-permute-done | bytes 163872 | tf_op jit(solution)/shard_map/ppermute | solution.py:252
  51.6 3.5 %shard_map.76 = (f32[64,1024]{1,0:T(8,128)S(1)}, f32[512,256]{1,0:T(8,128)S(1)}, f32[64,1024]{1,0:T(8,128)S(1)}, f32[512,256]{1,0:T(8,128)S(1)}) custom-call(f32[8,1024]{1,0:T(8,128)S(1)} %get-tuple-element.40.bias_ref, bf16[64,1280]{1,0:T(8,128)(2,1)S(1)} %collective-permute-done.6.refs_0_.refs_5_, bf16[64,1280]{1,0:T(8,128)(2,1)S(1)} %collective-permute-done.7.refs_1_, ...), custom_call_target="tpu_custom_call" | custom-call | flops 1073741824 | bytes 1409024 | tf_op jit(solution)/shard_map/pallas_call | solution.py:84
  55.0 0.0 collective-permute-done.3.refs_1_.refs_2_
  55.1 0.0 collective-permute-done.4.refs_2_.refs_3_
  55.1 3.7 %shard_map.80 = (s16[64,1152]{1,0:T(8,128)(2,1)S(1)}, s16[64,1152]{1,0:T(8,128)(2,1)S(1)}) custom-call(f32[8,1024]{1,0:T(8,128)S(1)} %get-tuple-element.40.bias_ref, bf16[64,1280]{1,0:T(8,128)(2,1)S(1)} %collective-permute-done.6.refs_0_.refs_5_, bf16[64,1280]{1,0:T(8,128)(2,1)S(1)} %collective-permute-done.7.refs_1_, ...), custom_call_target="tpu_custom_call" | custom-call | flops 1073741824 | bytes 2981888 | tf_op jit(solution)/shard_map/pallas_call | solution.py:84
  58.8 4.7 %collective-permute-start.10 = (s16[64,1152]{1,0:T(8,128)(2,1)S(1)}, s16[64,1152]{1,0:T(8,128)(2,1)S(1)}, u32[]{:S(2)}, u32[]{:S(2)}) collective-permute-start(s16[64,1152]{1,0:T(8,128)(2,1)S(1)} %get-tuple-element.69), channel_id=1, source_target_pairs={{0,12},{1,13},{2,14},{3,15},{4,0},{5,1},{6,2},{7,3},{8,4},{9,5},{1... | collective-permute-start | bytes 442376 | tf_op jit(solution)/shard_map/ppermute | solution.py:252
  63.4 0.0 collective-permute-start.11
  63.4 2.2 %shard_map.79 = s16[64,1152]{1,0:T(8,128)(2,1)S(1)} custom-call(f32[8,1024]{1,0:T(8,128)S(1)} %get-tuple-element.40.bias_ref, bf16[64,1280]{1,0:T(8,128)(2,1)S(1)} %collective-permute-done.8.refs_0_, bf16[1024,256]{1,0:T(8,128)(2,1)S(1)} %collective-permute-done.3.refs_1_.refs_2_, bf16[1024,256]{1,0:T(8,128)(2,1)S(1)} %collective-permute-done.4.refs_2_.refs_3_, ...), custom_call_target="tpu_custom_call" | custom-call | flops 536870912 | bytes 2031616 | tf_op jit(solution)/shard_map/pallas_call | solution.py:84
  65.7 2.5 %collective-permute-start.9 = (s16[64,1152]{1,0:T(8,128)(2,1)S(1)}, s16[64,1152]{1,0:T(8,128)(2,1)S(1)}, u32[]{:S(2)}, u32[]{:S(2)}) collective-permute-start(s16[64,1152]{1,0:T(8,128)(2,1)S(1)} %shard_map.79), channel_id=1, source_target_pairs={{0,8},{1,9},{2,10},{3,11},{4,12},{5,13},{6,14},{7,15},{8,0},{9,1},... | collective-permute-start | bytes 442376 | tf_op jit(solution)/shard_map/ppermute | solution.py:252
  68.2 2.3 %shard_map.78 = (f32[64,1024]{1,0:T(8,128)S(1)}, f32[512,256]{1,0:T(8,128)S(1)}) custom-call(f32[8,1024]{1,0:T(8,128)S(1)} %get-tuple-element.40.bias_ref, bf16[64,1280]{1,0:T(8,128)(2,1)S(1)} %shard_map.74.refs_0_, bf16[1024,256]{1,0:T(8,128)(2,1)S(1)} %collective-permute-done.3.refs_1_.refs_2_, ...), custom_call_target="tpu_custom_call" | custom-call | flops 536870912 | bytes 2195456 | tf_op jit(solution)/shard_map/pallas_call | solution.py:84
  70.5 0.0 collective-permute-done.10.refs_1_
  70.5 2.8 %collective-permute-done.11.refs_2_ = s16[64,1152]{1,0:T(8,128)(2,1)S(1)} collective-permute-done((s16[64,1152]{1,0:T(8,128)(2,1)S(1)}, s16[64,1152]{1,0:T(8,128)(2,1)S(1)}, u32[]{:S(2)}, u32[]{:S(2)}) %collective-permute-start.11) | collective-permute-done | bytes 147488 | tf_op jit(solution)/shard_map/ppermute | solution.py:252
  73.2 4.8 %collective-permute-done.9.refs_0_ = s16[64,1152]{1,0:T(8,128)(2,1)S(1)} collective-permute-done((s16[64,1152]{1,0:T(8,128)(2,1)S(1)}, s16[64,1152]{1,0:T(8,128)(2,1)S(1)}, u32[]{:S(2)}, u32[]{:S(2)}) %collective-permute-start.9) | collective-permute-done | bytes 147488 | tf_op jit(solution)/shard_map/ppermute | solution.py:252
  78.0 0.5 shard_map.81
  78.6 0.1 collective-permute-start.12
  78.6 1.6 %collective-permute-start.13 = (bf16[16,1024]{1,0:T(8,128)(2,1)S(1)}, bf16[16,1024]{1,0:T(8,128)(2,1)S(1)}, u32[]{:S(2)}, u32[]{:S(2)}) collective-permute-start(bf16[16,1024]{1,0:T(8,128)(2,1)S(1)} %get-tuple-element.73), channel_id=1, source_target_pairs={{0,2},{1,3},{2,0},{3,1},{4,6},{5,7},{6,4},{7,5},{8,10},{9,11},{10,... | collective-permute-start | bytes 98312 | tf_op jit(solution)/shard_map/ppermute | solution.py:249
  80.2 0.3 collective-permute-start.14
  80.5 0.0 collective-permute-done.12.refs_1_
  80.5 2.1 %collective-permute-done.13.refs_2_ = bf16[16,1024]{1,0:T(8,128)(2,1)S(1)} collective-permute-done((bf16[16,1024]{1,0:T(8,128)(2,1)S(1)}, bf16[16,1024]{1,0:T(8,128)(2,1)S(1)}, u32[]{:S(2)}, u32[]{:S(2)}) %collective-permute-start.13) | collective-permute-done | bytes 32800 | tf_op jit(solution)/shard_map/ppermute | solution.py:249
  82.6 1.0 %collective-permute-done.14.refs_3_ = bf16[16,1024]{1,0:T(8,128)(2,1)S(1)} collective-permute-done((bf16[16,1024]{1,0:T(8,128)(2,1)S(1)}, bf16[16,1024]{1,0:T(8,128)(2,1)S(1)}, u32[]{:S(2)}, u32[]{:S(2)}) %collective-permute-start.14) | collective-permute-done | bytes 32800 | tf_op jit(solution)/shard_map/ppermute | solution.py:249
  83.6 0.7 shard_map.82
  (1 shorter events, 0.0 us)
Async XLA Ops:
  0.0 1.2 %copy-start = (bf16[1024,512]{1,0:T(8,128)(2,1)S(1)}, bf16[1024,512]{1,0:T(8,128)(2,1)}, u32[]{:S(2)}) copy-start(bf16[1024,512]{1,0:T(8,128)(2,1)} %k_ref.1) | copy-start | bytes 3145732
  1.2 1.2 %copy-start.1 = (bf16[1024,512]{1,0:T(8,128)(2,1)S(1)}, bf16[1024,512]{1,0:T(8,128)(2,1)}, u32[]{:S(2)}) copy-start(bf16[1024,512]{1,0:T(8,128)(2,1)} %v_ref.1) | copy-start | bytes 3145732
  2.5 0.9 %copy-start.2 = (bf16[16,4096]{1,0:T(8,128)(2,1)S(1)}, bf16[16,4096]{1,0:T(8,128)(2,1)}, u32[]{:S(2)}) copy-start(bf16[16,4096]{1,0:T(8,128)(2,1)} %q_ref.1) | copy-start | bytes 393220
  3.4 0.7 copy-start.3
  4.1 0.7 copy-start.4
  4.8 0.7 copy-start.5
  5.4 0.7 copy-start.6
  7.6 32.5 %collective-permute-start.5 = (bf16[1024,256]{1,0:T(8,128)(2,1)S(1)}, bf16[1024,256]{1,0:T(8,128)(2,1)S(1)}, u32[]{:S(2)}, u32[]{:S(2)}) collective-permute-start(bf16[1024,256]{1,0:T(8,128)(2,1)S(1)} %get-tuple-element.48), channel_id=1, source_target_pairs={{0,1},{1,0},{2,3},{3,2},{4,5},{5,4},{6,7},{7,6},{8,9},{9,8},{10,11... | collective-permute-start | bytes 1572872 | tf_op jit(solution)/shard_map/ppermute | solution.py:249
  8.2 46.9 %collective-permute-start.3 = (bf16[1024,256]{1,0:T(8,128)(2,1)S(1)}, bf16[1024,256]{1,0:T(8,128)(2,1)S(1)}, u32[]{:S(2)}, u32[]{:S(2)}) collective-permute-start(bf16[1024,256]{1,0:T(8,128)(2,1)S(1)} %get-tuple-element.45), channel_id=1, source_target_pairs={{0,2},{1,3},{2,0},{3,1},{4,6},{5,7},{6,4},{7,5},{8,10},{9,11},{10,... | collective-permute-start | bytes 1572872 | tf_op jit(solution)/shard_map/ppermute | solution.py:249
  10.8 44.3 %collective-permute-start.4 = (bf16[1024,256]{1,0:T(8,128)(2,1)S(1)}, bf16[1024,256]{1,0:T(8,128)(2,1)S(1)}, u32[]{:S(2)}, u32[]{:S(2)}) collective-permute-start(bf16[1024,256]{1,0:T(8,128)(2,1)S(1)} %get-tuple-element.46), channel_id=1, source_target_pairs={{0,3},{1,2},{2,1},{3,0},{4,7},{5,6},{6,5},{7,4},{8,11},{9,10},{10,... | collective-permute-start | bytes 1572872 | tf_op jit(solution)/shard_map/ppermute | solution.py:249
  10.8 2.1 %collective-permute-start = (bf16[16,1280]{1,0:T(8,128)(2,1)S(1)}, bf16[16,1280]{1,0:T(8,128)(2,1)S(1)}, u32[]{:S(2)}, u32[]{:S(2)}) collective-permute-start(bf16[16,1280]{1,0:T(8,128)(2,1)S(1)} %get-tuple-element.42), channel_id=1, source_target_pairs={{0,1},{1,0},{2,3},{3,2},{4,5},{5,4},{6,7},{7,6},{8,9},{9,8},{10,11... | collective-permute-start | bytes 122888 | tf_op jit(solution)/shard_map/ppermute | solution.py:249
  11.0 24.7 %collective-permute-start.1 = (bf16[16,1280]{1,0:T(8,128)(2,1)S(1)}, bf16[16,1280]{1,0:T(8,128)(2,1)S(1)}, u32[]{:S(2)}, u32[]{:S(2)}) collective-permute-start(bf16[16,1280]{1,0:T(8,128)(2,1)S(1)} %get-tuple-element.43), channel_id=1, source_target_pairs={{0,2},{1,3},{2,0},{3,1},{4,6},{5,7},{6,4},{7,5},{8,10},{9,11},{10,... | collective-permute-start | bytes 122888 | tf_op jit(solution)/shard_map/ppermute | solution.py:249
  12.9 23.1 %collective-permute-start.2 = (bf16[16,1280]{1,0:T(8,128)(2,1)S(1)}, bf16[16,1280]{1,0:T(8,128)(2,1)S(1)}, u32[]{:S(2)}, u32[]{:S(2)}) collective-permute-start(bf16[16,1280]{1,0:T(8,128)(2,1)S(1)} %get-tuple-element.44), channel_id=1, source_target_pairs={{0,3},{1,2},{2,1},{3,0},{4,7},{5,6},{6,5},{7,4},{8,11},{9,10},{10,... | collective-permute-start | bytes 122888 | tf_op jit(solution)/shard_map/ppermute | solution.py:249
  36.0 11.9 %collective-permute-start.8 = (bf16[64,1280]{1,0:T(8,128)(2,1)S(1)}, bf16[64,1280]{1,0:T(8,128)(2,1)S(1)}, u32[]{:S(2)}, u32[]{:S(2)}) collective-permute-start(bf16[64,1280]{1,0:T(8,128)(2,1)S(1)} %shard_map.74.refs_0_), channel_id=1, source_target_pairs={{0,8},{1,9},{2,10},{3,11},{4,12},{5,13},{6,14},{7,15},{8,0},{9,1},... | collective-permute-start | bytes 491528 | tf_op jit(solution)/shard_map/ppermute | solution.py:252
  38.7 11.4 %collective-permute-start.7 = (bf16[64,1280]{1,0:T(8,128)(2,1)S(1)}, bf16[64,1280]{1,0:T(8,128)(2,1)S(1)}, u32[]{:S(2)}, u32[]{:S(2)}) collective-permute-start(bf16[64,1280]{1,0:T(8,128)(2,1)S(1)} %shard_map.74.refs_0_), channel_id=1, source_target_pairs={{0,12},{1,13},{2,14},{3,15},{4,0},{5,1},{6,2},{7,3},{8,4},{9,5},{1... | collective-permute-start | bytes 491528 | tf_op jit(solution)/shard_map/ppermute | solution.py:252
  40.1 11.5 %collective-permute-start.6 = (bf16[64,1280]{1,0:T(8,128)(2,1)S(1)}, bf16[64,1280]{1,0:T(8,128)(2,1)S(1)}, u32[]{:S(2)}, u32[]{:S(2)}) collective-permute-start(bf16[64,1280]{1,0:T(8,128)(2,1)S(1)} %shard_map.74.refs_0_), channel_id=1, source_target_pairs={{0,4},{1,5},{2,6},{3,7},{4,8},{5,9},{6,10},{7,11},{8,12},{9,13},{1... | collective-permute-start | bytes 491528 | tf_op jit(solution)/shard_map/ppermute | solution.py:252
  58.8 11.7 %collective-permute-start.10 = (s16[64,1152]{1,0:T(8,128)(2,1)S(1)}, s16[64,1152]{1,0:T(8,128)(2,1)S(1)}, u32[]{:S(2)}, u32[]{:S(2)}) collective-permute-start(s16[64,1152]{1,0:T(8,128)(2,1)S(1)} %get-tuple-element.69), channel_id=1, source_target_pairs={{0,12},{1,13},{2,14},{3,15},{4,0},{5,1},{6,2},{7,3},{8,4},{9,5},{1... | collective-permute-start | bytes 442376 | tf_op jit(solution)/shard_map/ppermute | solution.py:252
  63.4 9.8 %collective-permute-start.11 = (s16[64,1152]{1,0:T(8,128)(2,1)S(1)}, s16[64,1152]{1,0:T(8,128)(2,1)S(1)}, u32[]{:S(2)}, u32[]{:S(2)}) collective-permute-start(s16[64,1152]{1,0:T(8,128)(2,1)S(1)} %get-tuple-element.70), channel_id=1, source_target_pairs={{0,4},{1,5},{2,6},{3,7},{4,8},{5,9},{6,10},{7,11},{8,12},{9,13},{1... | collective-permute-start | bytes 442376 | tf_op jit(solution)/shard_map/ppermute | solution.py:252
  65.7 12.3 %collective-permute-start.9 = (s16[64,1152]{1,0:T(8,128)(2,1)S(1)}, s16[64,1152]{1,0:T(8,128)(2,1)S(1)}, u32[]{:S(2)}, u32[]{:S(2)}) collective-permute-start(s16[64,1152]{1,0:T(8,128)(2,1)S(1)} %shard_map.79), channel_id=1, source_target_pairs={{0,8},{1,9},{2,10},{3,11},{4,12},{5,13},{6,14},{7,15},{8,0},{9,1},... | collective-permute-start | bytes 442376 | tf_op jit(solution)/shard_map/ppermute | solution.py:252
  78.6 1.9 %collective-permute-start.12 = (bf16[16,1024]{1,0:T(8,128)(2,1)S(1)}, bf16[16,1024]{1,0:T(8,128)(2,1)S(1)}, u32[]{:S(2)}, u32[]{:S(2)}) collective-permute-start(bf16[16,1024]{1,0:T(8,128)(2,1)S(1)} %get-tuple-element.72), channel_id=1, source_target_pairs={{0,1},{1,0},{2,3},{3,2},{4,5},{5,4},{6,7},{7,6},{8,9},{9,8},{10,11... | collective-permute-start | bytes 98312 | tf_op jit(solution)/shard_map/ppermute | solution.py:249
  78.6 4.0 %collective-permute-start.13 = (bf16[16,1024]{1,0:T(8,128)(2,1)S(1)}, bf16[16,1024]{1,0:T(8,128)(2,1)S(1)}, u32[]{:S(2)}, u32[]{:S(2)}) collective-permute-start(bf16[16,1024]{1,0:T(8,128)(2,1)S(1)} %get-tuple-element.73), channel_id=1, source_target_pairs={{0,2},{1,3},{2,0},{3,1},{4,6},{5,7},{6,4},{7,5},{8,10},{9,11},{10,... | collective-permute-start | bytes 98312 | tf_op jit(solution)/shard_map/ppermute | solution.py:249
  80.2 3.4 %collective-permute-start.14 = (bf16[16,1024]{1,0:T(8,128)(2,1)S(1)}, bf16[16,1024]{1,0:T(8,128)(2,1)S(1)}, u32[]{:S(2)}, u32[]{:S(2)}) collective-permute-start(bf16[16,1024]{1,0:T(8,128)(2,1)S(1)} %get-tuple-element.74), channel_id=1, source_target_pairs={{0,3},{1,2},{2,1},{3,0},{4,7},{5,6},{6,5},{7,4},{8,11},{9,10},{10,... | collective-permute-start | bytes 98312 | tf_op jit(solution)/shard_map/ppermute | solution.py:249

commit v3 on v2

--- a/solution.py
+++ b/solution.py
@@ -79,28 +79,29 @@
     return pl.ds(pl.multiple_of(((lax.axis_index("kvp") % 4) ^ j) * width, width), width)
 
 
-def local_call(kernel, shapes, args, tables=(), work=0, scratch=(), space=pltpu.VMEM):
+def local_call(kernel, shapes, args, work=0, scratch=(), space=pltpu.VMEM):
     moved = sum(x.size * x.dtype.itemsize for x in args)
     return pl.pallas_call(
         kernel,
         out_shape=[jax.ShapeDtypeStruct(s, t) for s, t in shapes],
-        in_specs=[pl.BlockSpec(memory_space=pltpu.SMEM)] * len(tables)
-        + [pl.BlockSpec(memory_space=space)] * len(args),
+        in_specs=[pl.BlockSpec(memory_space=space)] * len(args),
         out_specs=[pl.BlockSpec(memory_space=pltpu.VMEM)] * len(shapes),
         scratch_shapes=scratch,
         compiler_params=pltpu.CompilerParams(vmem_limit_bytes=VMEM_GRANT),
         cost_estimate=pl.CostEstimate(flops=4 * HEAD_SIZE * work, transcendentals=work, bytes_accessed=moved),
-    )(*tables, *args)
-
-
-def split_kernel(shards, lens, starts, q_ref, sk_ref, sv_ref, k_ref, v_ref, *refs):
-    outs, bias_ref, sems = refs[:8], refs[8], refs[9]
+    )(*args)
+
+
+def split_kernel(shards, lens_ref, starts_ref, q_ref, sk_ref, sv_ref, k_ref, v_ref, *refs):
+    outs, (bias_ref, lens, starts, sems) = refs[:8], refs[8:]
     copies = []
 
     def copy(src, dst):
         copies.append(pltpu.make_async_copy(src, dst, sems.at[len(copies)]))
         copies[-1].start()
 
+    copy(lens_ref, lens)
+    copy(starts_ref, starts)
     for j in (2, 3, 1, 0):
         at = columns(j, HEAD_SIZE)
         copy(q_ref.at[:, columns(j, WIDTH)], outs[j].at[:, pl.ds(0, WIDTH)])
@@ -112,12 +113,14 @@
         copy(v_ref.at[:, at], outs[4 + j].at[:, pl.ds(HEAD_SIZE, HEAD_SIZE)])
     me = lax.axis_index("kvp")
     slots = k_ref.shape[0]
+    for c in copies[:2]:
+        c.wait()
     lane = lax.broadcasted_iota(jnp.int32, (1, slots), 1)
     for span in range(SPANS):
         for j in range(4):
             seen = row_limit(lens, starts, me // 4 * 4 + ((me % 4) ^ j), span, shards, slots)
             bias_ref[span * 4 + j : span * 4 + j + 1, :] = jnp.where(lane < seen, 0.0, NEG_LARGE)
-    for c in copies:
+    for c in copies[2:]:
         c.wait()
 
 
@@ -128,7 +131,7 @@
 
 
 def attend_kernel(cfg, bias_ref, *refs):
-    shards, blocks, pieces, prior, finish, rows = cfg
+    _, blocks, pieces, prior, finish, rows = cfg
     refs = list(refs)
     q_refs = [refs.pop(0) for _ in blocks]
     kv = [refs.pop(0) for _ in pieces]
@@ -136,11 +139,10 @@
     span_ref = refs.pop(0) if finish == "span" else None
     outs = refs
     me = lax.axis_index("kvp")
-    zs = shards // 4
     z, b = me // 4, me % 4
     for i, d in enumerate(blocks):
         q = stack_heads(q_refs[i][:, :WIDTH])
-        span = lax.rem(z - d + zs, zs) * rows // SPAN
+        span = (z ^ d) * rows // SPAN
         state = None
         if prior:
             p_ref, s_ref = prior_refs[i]
@@ -249,7 +251,7 @@
         return lax.ppermute(x, "kvp", [(i, i ^ j) for i in range(n)])
 
     def along(x, d):
-        return lax.ppermute(x, "kvp", [(i, (i // 4 + d) % zs * 4 + i % 4) for i in range(n)])
+        return lax.ppermute(x, "kvp", [(i, i ^ (4 * d)) for i in range(n)])
 
     def attend(*args, **kwargs):
         return attention(bias, n, *args, **kwargs)
@@ -259,9 +261,8 @@
     *cut, bias = local_call(
         functools.partial(split_kernel, n),
         [((part, wide), BF16)] * 4 + [((slots, 2 * HEAD_SIZE), BF16)] * 4 + [((SPANS * 4, slots), F32)],
-        (queries, span_keys, span_values, keys, values),
-        tables=tables,
-        scratch=[pltpu.SemaphoreType.DMA((20,))],
+        [pltpu.with_memory_space_constraint(x, pltpu.HBM) for x in tables + (queries, span_keys, span_values, keys, values)],
+        scratch=[pltpu.SMEM(x.shape, x.dtype) for x in tables] + [pltpu.SemaphoreType.DMA((22,))],
         space=pltpu.HBM,
     )
     q_parts, kv_parts = cut[:4], cut[4:]
@@ -273,14 +274,15 @@
 
     near = {j: kv[j] for j in (0, 1)}
     s0 = attend({0: q[0]}, near)
-    s13 = attend({1: q[1], 3: q[3]}, near)
-    s2 = attend({2: q[2]}, near)
-    kv[2], kv[3], s0, s13, s2 = lax.optimization_barrier((kv[2], kv[3], s0, s13, s2))
-    far = {j: kv[j] for j in (2, 3)}
-    codes = attend({2: q[2]}, far, prior=s2, finish="encode")
-    codes |= attend({1: q[1], 3: q[3]}, far, prior=s13, finish="encode")
-    back = [along(codes[d], -d) for d in (2, 1, 3)]
-    mine = attend({0: q[0]}, far, prior=s0, finish="span", before=q[1])[0]
+    near[2] = kv[2]
+    s1 = attend({1: q[1]}, near)
+    s23 = attend({2: q[2], 3: q[3]}, near)
+    kv[3], s0, s1, s23 = lax.optimization_barrier((kv[3], s0, s1, s23))
+    last = {3: kv[3]}
+    codes = attend({2: q[2], 3: q[3]}, last, prior=s23, finish="encode")
+    codes |= attend({1: q[1]}, last, prior=s1, finish="encode")
+    back = [along(codes[d], d) for d in (2, 3, 1)]
+    mine = attend({0: q[0]}, {2: kv[2], 3: kv[3]}, prior=s0, finish="span", before=q[1])[0]
     parts = local_call(functools.partial(final_kernel, q[0].shape[0]), [((part, WIDTH), BF16)] * 4, (*mine, *back))
     parts = [parts[0]] + [within(parts[j], j) for j in range(1, 4)]
     return local_call(join_kernel, [((part, 4 * WIDTH), BF16)], parts)[0]

time: 84.6 us -> 78.7 us (0.930)
  local copies, waits for them, and re-layouts: 6.1 us -> 0 us
  starting transfers between devices: 19.9 us -> 17 us
  waiting for transfers between devices: 39.4 us -> 42.2 us
    unnamed x14 -> x0, local copies, waits for them, and re-layouts: 6.1 us -> none
    ppermute x6, starting transfers between devices: 11.9 us -> 8.98 us  [along(): return lax.ppermute(x, 'kvp', [(i, i ^ 4 * d) for i in range(n)])]
    ppermute x6, waiting for transfers between devices: 14.1 us -> 16.9 us  [along(): return lax.ppermute(x, 'kvp', [(i, i ^ 4 * d) for i in range(n)])]
  transfers between devices with their start and end apart: 15 -> 15, of which waited for: 8 -> 7; matrix products, arithmetic and copies ran while one was open for 0% -> 0% of each run, Pallas kernels for 15% -> 18%
where the time goes in v3:
time: 78.7 us; the launch traced here: 78.6 us
  waiting for transfers between devices  42.2 us (54%)
  Pallas kernels  19.2 us (24%)
  starting transfers between devices  17 us (22%)
    ppermute x9, waiting for transfers between devices, within(): return lax.ppermute(x, 'kvp', [(i, i ^ j) for i in range(n)])  25.4 us
    pallas_call x10, Pallas kernels, local_call(): pl.pallas_call(kernel, out_shape=[jax.ShapeDtypeStruct(s, t) for s, t in...  19.2 us
    ppermute x6, waiting for transfers between devices, along(): return lax.ppermute(x, 'kvp', [(i, i ^ 4 * d) for i in range(n)])  16.9 us
    ppermute x6, starting transfers between devices, along(): return lax.ppermute(x, 'kvp', [(i, i ^ 4 * d) for i in range(n)])  8.98 us
    ppermute x9, starting transfers between devices, within(): return lax.ppermute(x, 'kvp', [(i, i ^ j) for i in range(n)])  8.02 us
  transfers between devices with their start and end apart: 15, of which 7 were waited for; matrix products, arithmetic and copies ran while one was open for 0% of the time, Pallas kernels for 18%

profile of v3, /device:TPU:0, one launch (start us, length us, event | category | flops | bytes accessed | tf_op | source)
XLA Modules:
  0.0 78.6 jit_solution(10652045805012586408)
XLA Ops:
  0.0 1.9 %shard_map.73 = (bf16[16,1280]{1,0:T(8,128)(2,1)S(1)}, bf16[16,1280]{1,0:T(8,128)(2,1)S(1)}, bf16[16,1280]{1,0:T(8,128)(2,1)S(1)}, bf16[16,1280]{1,0:T(8,128)(2,...) custom-call(s32[16]{0:T(128)} %lens_ref.1, ...), custom_call_target="tpu_custom_call" | custom-call | bytes 2261064 | tf_op jit(solution)/shard_map/pallas_call | solution.py:84
  1.9 0.6 collective-permute-start.5
  2.5 2.6 %collective-permute-start.3 = (bf16[1024,256]{1,0:T(8,128)(2,1)S(1)}, bf16[1024,256]{1,0:T(8,128)(2,1)S(1)}, u32[]{:S(2)}, u32[]{:S(2)}) collective-permute-start(bf16[1024,256]{1,0:T(8,128)(2,1)S(1)} %get-tuple-element.44), channel_id=1, source_target_pairs={{0,2},{1,3},{2,0},{3,1},{4,6},{5,7},{6,4},{7,5},{8,10},{9,11},{10,... | collective-permute-start | bytes 1572872 | tf_op jit(solution)/shard_map/ppermute | solution.py:251
  5.1 0.0 collective-permute-start.4
  5.1 0.2 collective-permute-start
  5.3 1.9 %collective-permute-start.1 = (bf16[16,1280]{1,0:T(8,128)(2,1)S(1)}, bf16[16,1280]{1,0:T(8,128)(2,1)S(1)}, u32[]{:S(2)}, u32[]{:S(2)}) collective-permute-start(bf16[16,1280]{1,0:T(8,128)(2,1)S(1)} %get-tuple-element.42), channel_id=1, source_target_pairs={{0,2},{1,3},{2,0},{3,1},{4,6},{5,7},{6,4},{7,5},{8,10},{9,11},{10,... | collective-permute-start | bytes 122888 | tf_op jit(solution)/shard_map/ppermute | solution.py:251
  7.2 0.0 collective-permute-done.refs_1_
  7.2 0.8 %collective-permute-start.2 = (bf16[16,1280]{1,0:T(8,128)(2,1)S(1)}, bf16[16,1280]{1,0:T(8,128)(2,1)S(1)}, u32[]{:S(2)}, u32[]{:S(2)}) collective-permute-start(bf16[16,1280]{1,0:T(8,128)(2,1)S(1)} %get-tuple-element.43), channel_id=1, source_target_pairs={{0,3},{1,2},{2,1},{3,0},{4,7},{5,6},{6,5},{7,4},{8,11},{9,10},{10,... | collective-permute-start | bytes 122888 | tf_op jit(solution)/shard_map/ppermute | solution.py:251
  8.0 21.9 %collective-permute-done.1.refs_2_ = bf16[16,1280]{1,0:T(8,128)(2,1)S(1)} collective-permute-done((bf16[16,1280]{1,0:T(8,128)(2,1)S(1)}, bf16[16,1280]{1,0:T(8,128)(2,1)S(1)}, u32[]{:S(2)}, u32[]{:S(2)}) %collective-permute-start.1) | collective-permute-done | bytes 40992 | tf_op jit(solution)/shard_map/ppermute | solution.py:251
  30.0 0.4 collective-permute-done.2.refs_3_
  30.3 1.7 %collective-permute-start.6 = (bf16[64,1280]{1,0:T(8,128)(2,1)S(1)}, bf16[64,1280]{1,0:T(8,128)(2,1)S(1)}, u32[]{:S(2)}, u32[]{:S(2)}) collective-permute-start(bf16[64,1280]{1,0:T(8,128)(2,1)S(1)} %shard_map.74.refs_0_), channel_id=1, source_target_pairs={{0,4},{1,5},{2,6},{3,7},{4,0},{5,1},{6,2},{7,3},{8,12},{9,13},{10,... | collective-permute-start | bytes 491528 | tf_op jit(solution)/shard_map/ppermute | solution.py:254
  32.0 2.5 %collective-permute-start.8 = (bf16[64,1280]{1,0:T(8,128)(2,1)S(1)}, bf16[64,1280]{1,0:T(8,128)(2,1)S(1)}, u32[]{:S(2)}, u32[]{:S(2)}) collective-permute-start(bf16[64,1280]{1,0:T(8,128)(2,1)S(1)} %shard_map.74.refs_0_), channel_id=1, source_target_pairs={{0,12},{1,13},{2,14},{3,15},{4,8},{5,9},{6,10},{7,11},{8,4},{9,5},... | collective-permute-start | bytes 491528 | tf_op jit(solution)/shard_map/ppermute | solution.py:254
  34.5 0.0 collective-permute-done.5.refs_2_.refs_3_
  34.5 0.1 collective-permute-start.7
  34.6 2.1 %shard_map.75 = (f32[64,1024]{1,0:T(8,128)S(1)}, f32[512,256]{1,0:T(8,128)S(1)}) custom-call(f32[8,1024]{1,0:T(8,128)S(1)} %get-tuple-element.39.bias_ref, bf16[64,1280]{1,0:T(8,128)(2,1)S(1)} %shard_map.74.refs_0_, bf16[1024,256]{1,0:T(8,128)(2,1)S(1)} %get-tuple-element.46.refs_1_.refs_2_, bf16[1024,256]{1,0:T(8,128)(2,1)S(1)} %collective-permute-done.5.refs_2_.refs_3_), custom_call_target="tpu_custom_call" | custom-call | flops 536870912 | bytes 1245184 | tf_op jit(solution)/shard_map/pallas_call | solution.py:84
  36.8 0.0 collective-permute-done.6.refs_0_.refs_5_
  36.8 0.0 collective-permute-done.3.refs_3_.refs_4_.refs_1_
  36.8 2.8 %shard_map.76 = (f32[64,1024]{1,0:T(8,128)S(1)}, f32[512,256]{1,0:T(8,128)S(1)}) custom-call(f32[8,1024]{1,0:T(8,128)S(1)} %get-tuple-element.39.bias_ref, bf16[64,1280]{1,0:T(8,128)(2,1)S(1)} %collective-permute-done.6.refs_0_.refs_5_, bf16[1024,256]{1,0:T(8,128)(2,1)S(1)} %get-tuple-element.46.refs_1_.refs_2_, ...), custom_call_target="tpu_custom_call" | custom-call | flops 805306368 | bytes 1769472 | tf_op jit(solution)/shard_map/pallas_call | solution.py:84
  39.6 3.6 %collective-permute-done.8.refs_1_ = bf16[64,1280]{1,0:T(8,128)(2,1)S(1)} collective-permute-done((bf16[64,1280]{1,0:T(8,128)(2,1)S(1)}, bf16[64,1280]{1,0:T(8,128)(2,1)S(1)}, u32[]{:S(2)}, u32[]{:S(2)}) %collective-permute-start.8) | collective-permute-done | bytes 163872 | tf_op jit(solution)/shard_map/ppermute | solution.py:254
  43.2 6.3 %collective-permute-done.7.refs_0_ = bf16[64,1280]{1,0:T(8,128)(2,1)S(1)} collective-permute-done((bf16[64,1280]{1,0:T(8,128)(2,1)S(1)}, bf16[64,1280]{1,0:T(8,128)(2,1)S(1)}, u32[]{:S(2)}, u32[]{:S(2)}) %collective-permute-start.7) | collective-permute-done | bytes 163872 | tf_op jit(solution)/shard_map/ppermute | solution.py:254
  49.5 4.9 %shard_map.77 = (f32[64,1024]{1,0:T(8,128)S(1)}, f32[512,256]{1,0:T(8,128)S(1)}, f32[64,1024]{1,0:T(8,128)S(1)}, f32[512,256]{1,0:T(8,128)S(1)}) custom-call(f32[8,1024]{1,0:T(8,128)S(1)} %get-tuple-element.39.bias_ref, bf16[64,1280]{1,0:T(8,128)(2,1)S(1)} %collective-permute-done.7.refs_0_, bf16[64,1280]{1,0:T(8,128)(2,1)S(1)} %collective-permute-done.8.refs_1_, ...), custom_call_target="tpu_custom_call" | custom-call | flops 1610612736 | bytes 1933312 | tf_op jit(solution)/shard_map/pallas_call | solution.py:84
  54.4 0.0 collective-permute-done.4.refs_2_.refs_1_
  54.4 1.6 %shard_map.80 = s16[64,1152]{1,0:T(8,128)(2,1)S(1)} custom-call(f32[8,1024]{1,0:T(8,128)S(1)} %get-tuple-element.39.bias_ref, bf16[64,1280]{1,0:T(8,128)(2,1)S(1)} %collective-permute-done.6.refs_0_.refs_5_, bf16[1024,256]{1,0:T(8,128)(2,1)S(1)} %collective-permute-done.4.refs_2_.refs_1_, f32[64,1024]{1,0:T(8,128)S(1)} %get-tuple-element.67.refs_2_, ...), custom_call_target="tpu_custom_call" | custom-call | flops 268435456 | bytes 1507328 | tf_op jit(solution)/shard_map/pallas_call | solution.py:84
  56.0 0.3 collective-permute-start.11
  56.2 2.4 %shard_map.79 = (s16[64,1152]{1,0:T(8,128)(2,1)S(1)}, s16[64,1152]{1,0:T(8,128)(2,1)S(1)}) custom-call(f32[8,1024]{1,0:T(8,128)S(1)} %get-tuple-element.39.bias_ref, bf16[64,1280]{1,0:T(8,128)(2,1)S(1)} %collective-permute-done.7.refs_0_, bf16[64,1280]{1,0:T(8,128)(2,1)S(1)} %collective-permute-done.8.refs_1_, ...), custom_call_target="tpu_custom_call" | custom-call | flops 536870912 | bytes 2457600 | tf_op jit(solution)/shard_map/pallas_call | solution.py:84
  58.6 3.3 %collective-permute-start.9 = (s16[64,1152]{1,0:T(8,128)(2,1)S(1)}, s16[64,1152]{1,0:T(8,128)(2,1)S(1)}, u32[]{:S(2)}, u32[]{:S(2)}) collective-permute-start(s16[64,1152]{1,0:T(8,128)(2,1)S(1)} %get-tuple-element.65), channel_id=1, source_target_pairs={{0,8},{1,9},{2,10},{3,11},{4,12},{5,13},{6,14},{7,15},{8,0},{9,1},... | collective-permute-start | bytes 442376 | tf_op jit(solution)/shard_map/ppermute | solution.py:254
  61.9 1.2 %collective-permute-start.10 = (s16[64,1152]{1,0:T(8,128)(2,1)S(1)}, s16[64,1152]{1,0:T(8,128)(2,1)S(1)}, u32[]{:S(2)}, u32[]{:S(2)}) collective-permute-start(s16[64,1152]{1,0:T(8,128)(2,1)S(1)} %get-tuple-element.66), channel_id=1, source_target_pairs={{0,12},{1,13},{2,14},{3,15},{4,8},{5,9},{6,10},{7,11},{8,4},{9,5},... | collective-permute-start | bytes 442376 | tf_op jit(solution)/shard_map/ppermute | solution.py:254
  63.1 2.3 %shard_map.78 = (f32[64,1024]{1,0:T(8,128)S(1)}, f32[512,256]{1,0:T(8,128)S(1)}) custom-call(f32[8,1024]{1,0:T(8,128)S(1)} %get-tuple-element.39.bias_ref, bf16[64,1280]{1,0:T(8,128)(2,1)S(1)} %shard_map.74.refs_0_, bf16[1024,256]{1,0:T(8,128)(2,1)S(1)} %collective-permute-done.3.refs_3_.refs_4_.refs_1_, ...), custom_call_target="tpu_custom_call" | custom-call | flops 536870912 | bytes 2195456 | tf_op jit(solution)/shard_map/pallas_call | solution.py:84
  65.4 0.0 collective-permute-done.11.refs_2_
  65.4 6.9 %collective-permute-done.9.refs_0_ = s16[64,1152]{1,0:T(8,128)(2,1)S(1)} collective-permute-done((s16[64,1152]{1,0:T(8,128)(2,1)S(1)}, s16[64,1152]{1,0:T(8,128)(2,1)S(1)}, u32[]{:S(2)}, u32[]{:S(2)}) %collective-permute-start.9) | collective-permute-done | bytes 147488 | tf_op jit(solution)/shard_map/ppermute | solution.py:254
  72.3 0.0 collective-permute-done.10.refs_1_
  72.3 0.5 shard_map.81
  72.9 0.1 collective-permute-start.12
  72.9 1.6 %collective-permute-start.13 = (bf16[16,1024]{1,0:T(8,128)(2,1)S(1)}, bf16[16,1024]{1,0:T(8,128)(2,1)S(1)}, u32[]{:S(2)}, u32[]{:S(2)}) collective-permute-start(bf16[16,1024]{1,0:T(8,128)(2,1)S(1)} %get-tuple-element.71), channel_id=1, source_target_pairs={{0,2},{1,3},{2,0},{3,1},{4,6},{5,7},{6,4},{7,5},{8,10},{9,11},{10,... | collective-permute-start | bytes 98312 | tf_op jit(solution)/shard_map/ppermute | solution.py:251
  74.5 0.3 collective-permute-start.14
  74.8 0.0 collective-permute-done.12.refs_1_
  74.8 2.1 %collective-permute-done.13.refs_2_ = bf16[16,1024]{1,0:T(8,128)(2,1)S(1)} collective-permute-done((bf16[16,1024]{1,0:T(8,128)(2,1)S(1)}, bf16[16,1024]{1,0:T(8,128)(2,1)S(1)}, u32[]{:S(2)}, u32[]{:S(2)}) %collective-permute-start.13) | collective-permute-done | bytes 32800 | tf_op jit(solution)/shard_map/ppermute | solution.py:251
  76.9 1.0 %collective-permute-done.14.refs_3_ = bf16[16,1024]{1,0:T(8,128)(2,1)S(1)} collective-permute-done((bf16[16,1024]{1,0:T(8,128)(2,1)S(1)}, bf16[16,1024]{1,0:T(8,128)(2,1)S(1)}, u32[]{:S(2)}, u32[]{:S(2)}) %collective-permute-start.14) | collective-permute-done | bytes 32800 | tf_op jit(solution)/shard_map/ppermute | solution.py:251
  77.9 0.7 shard_map.82
  (1 shorter events, 0.0 us)
Async XLA Ops:
  1.9 32.6 %collective-permute-start.5 = (bf16[1024,256]{1,0:T(8,128)(2,1)S(1)}, bf16[1024,256]{1,0:T(8,128)(2,1)S(1)}, u32[]{:S(2)}, u32[]{:S(2)}) collective-permute-start(bf16[1024,256]{1,0:T(8,128)(2,1)S(1)} %get-tuple-element.47), channel_id=1, source_target_pairs={{0,1},{1,0},{2,3},{3,2},{4,5},{5,4},{6,7},{7,6},{8,9},{9,8},{10,11... | collective-permute-start | bytes 1572872 | tf_op jit(solution)/shard_map/ppermute | solution.py:251
  2.5 34.3 %collective-permute-start.3 = (bf16[1024,256]{1,0:T(8,128)(2,1)S(1)}, bf16[1024,256]{1,0:T(8,128)(2,1)S(1)}, u32[]{:S(2)}, u32[]{:S(2)}) collective-permute-start(bf16[1024,256]{1,0:T(8,128)(2,1)S(1)} %get-tuple-element.44), channel_id=1, source_target_pairs={{0,2},{1,3},{2,0},{3,1},{4,6},{5,7},{6,4},{7,5},{8,10},{9,11},{10,... | collective-permute-start | bytes 1572872 | tf_op jit(solution)/shard_map/ppermute | solution.py:251
  5.1 49.3 %collective-permute-start.4 = (bf16[1024,256]{1,0:T(8,128)(2,1)S(1)}, bf16[1024,256]{1,0:T(8,128)(2,1)S(1)}, u32[]{:S(2)}, u32[]{:S(2)}) collective-permute-start(bf16[1024,256]{1,0:T(8,128)(2,1)S(1)} %get-tuple-element.45), channel_id=1, source_target_pairs={{0,3},{1,2},{2,1},{3,0},{4,7},{5,6},{6,5},{7,4},{8,11},{9,10},{10,... | collective-permute-start | bytes 1572872 | tf_op jit(solution)/shard_map/ppermute | solution.py:251
  5.1 2.1 %collective-permute-start = (bf16[16,1280]{1,0:T(8,128)(2,1)S(1)}, bf16[16,1280]{1,0:T(8,128)(2,1)S(1)}, u32[]{:S(2)}, u32[]{:S(2)}) collective-permute-start(bf16[16,1280]{1,0:T(8,128)(2,1)S(1)} %get-tuple-element.41), channel_id=1, source_target_pairs={{0,1},{1,0},{2,3},{3,2},{4,5},{5,4},{6,7},{7,6},{8,9},{9,8},{10,11... | collective-permute-start | bytes 122888 | tf_op jit(solution)/shard_map/ppermute | solution.py:251
  5.3 24.7 %collective-permute-start.1 = (bf16[16,1280]{1,0:T(8,128)(2,1)S(1)}, bf16[16,1280]{1,0:T(8,128)(2,1)S(1)}, u32[]{:S(2)}, u32[]{:S(2)}) collective-permute-start(bf16[16,1280]{1,0:T(8,128)(2,1)S(1)} %get-tuple-element.42), channel_id=1, source_target_pairs={{0,2},{1,3},{2,0},{3,1},{4,6},{5,7},{6,4},{7,5},{8,10},{9,11},{10,... | collective-permute-start | bytes 122888 | tf_op jit(solution)/shard_map/ppermute | solution.py:251
  7.2 23.1 %collective-permute-start.2 = (bf16[16,1280]{1,0:T(8,128)(2,1)S(1)}, bf16[16,1280]{1,0:T(8,128)(2,1)S(1)}, u32[]{:S(2)}, u32[]{:S(2)}) collective-permute-start(bf16[16,1280]{1,0:T(8,128)(2,1)S(1)} %get-tuple-element.43), channel_id=1, source_target_pairs={{0,3},{1,2},{2,1},{3,0},{4,7},{5,6},{6,5},{7,4},{8,11},{9,10},{10,... | collective-permute-start | bytes 122888 | tf_op jit(solution)/shard_map/ppermute | solution.py:251
  30.3 6.4 %collective-permute-start.6 = (bf16[64,1280]{1,0:T(8,128)(2,1)S(1)}, bf16[64,1280]{1,0:T(8,128)(2,1)S(1)}, u32[]{:S(2)}, u32[]{:S(2)}) collective-permute-start(bf16[64,1280]{1,0:T(8,128)(2,1)S(1)} %shard_map.74.refs_0_), channel_id=1, source_target_pairs={{0,4},{1,5},{2,6},{3,7},{4,0},{5,1},{6,2},{7,3},{8,12},{9,13},{10,... | collective-permute-start | bytes 491528 | tf_op jit(solution)/shard_map/ppermute | solution.py:254
  32.0 11.1 %collective-permute-start.8 = (bf16[64,1280]{1,0:T(8,128)(2,1)S(1)}, bf16[64,1280]{1,0:T(8,128)(2,1)S(1)}, u32[]{:S(2)}, u32[]{:S(2)}) collective-permute-start(bf16[64,1280]{1,0:T(8,128)(2,1)S(1)} %shard_map.74.refs_0_), channel_id=1, source_target_pairs={{0,12},{1,13},{2,14},{3,15},{4,8},{5,9},{6,10},{7,11},{8,4},{9,5},... | collective-permute-start | bytes 491528 | tf_op jit(solution)/shard_map/ppermute | solution.py:254
  34.5 15.0 %collective-permute-start.7 = (bf16[64,1280]{1,0:T(8,128)(2,1)S(1)}, bf16[64,1280]{1,0:T(8,128)(2,1)S(1)}, u32[]{:S(2)}, u32[]{:S(2)}) collective-permute-start(bf16[64,1280]{1,0:T(8,128)(2,1)S(1)} %shard_map.74.refs_0_), channel_id=1, source_target_pairs={{0,8},{1,9},{2,10},{3,11},{4,12},{5,13},{6,14},{7,15},{8,0},{9,1},... | collective-permute-start | bytes 491528 | tf_op jit(solution)/shard_map/ppermute | solution.py:254
  56.0 9.4 %collective-permute-start.11 = (s16[64,1152]{1,0:T(8,128)(2,1)S(1)}, s16[64,1152]{1,0:T(8,128)(2,1)S(1)}, u32[]{:S(2)}, u32[]{:S(2)}) collective-permute-start(s16[64,1152]{1,0:T(8,128)(2,1)S(1)} %shard_map.80), channel_id=1, source_target_pairs={{0,4},{1,5},{2,6},{3,7},{4,0},{5,1},{6,2},{7,3},{8,12},{9,13},{10,... | collective-permute-start | bytes 442376 | tf_op jit(solution)/shard_map/ppermute | solution.py:254
  58.6 13.7 %collective-permute-start.9 = (s16[64,1152]{1,0:T(8,128)(2,1)S(1)}, s16[64,1152]{1,0:T(8,128)(2,1)S(1)}, u32[]{:S(2)}, u32[]{:S(2)}) collective-permute-start(s16[64,1152]{1,0:T(8,128)(2,1)S(1)} %get-tuple-element.65), channel_id=1, source_target_pairs={{0,8},{1,9},{2,10},{3,11},{4,12},{5,13},{6,14},{7,15},{8,0},{9,1},... | collective-permute-start | bytes 442376 | tf_op jit(solution)/shard_map/ppermute | solution.py:254
  61.9 10.4 %collective-permute-start.10 = (s16[64,1152]{1,0:T(8,128)(2,1)S(1)}, s16[64,1152]{1,0:T(8,128)(2,1)S(1)}, u32[]{:S(2)}, u32[]{:S(2)}) collective-permute-start(s16[64,1152]{1,0:T(8,128)(2,1)S(1)} %get-tuple-element.66), channel_id=1, source_target_pairs={{0,12},{1,13},{2,14},{3,15},{4,8},{5,9},{6,10},{7,11},{8,4},{9,5},... | collective-permute-start | bytes 442376 | tf_op jit(solution)/shard_map/ppermute | solution.py:254
  72.9 1.9 %collective-permute-start.12 = (bf16[16,1024]{1,0:T(8,128)(2,1)S(1)}, bf16[16,1024]{1,0:T(8,128)(2,1)S(1)}, u32[]{:S(2)}, u32[]{:S(2)}) collective-permute-start(bf16[16,1024]{1,0:T(8,128)(2,1)S(1)} %get-tuple-element.70), channel_id=1, source_target_pairs={{0,1},{1,0},{2,3},{3,2},{4,5},{5,4},{6,7},{7,6},{8,9},{9,8},{10,11... | collective-permute-start | bytes 98312 | tf_op jit(solution)/shard_map/ppermute | solution.py:251
  72.9 4.0 %collective-permute-start.13 = (bf16[16,1024]{1,0:T(8,128)(2,1)S(1)}, bf16[16,1024]{1,0:T(8,128)(2,1)S(1)}, u32[]{:S(2)}, u32[]{:S(2)}) collective-permute-start(bf16[16,1024]{1,0:T(8,128)(2,1)S(1)} %get-tuple-element.71), channel_id=1, source_target_pairs={{0,2},{1,3},{2,0},{3,1},{4,6},{5,7},{6,4},{7,5},{8,10},{9,11},{10,... | collective-permute-start | bytes 98312 | tf_op jit(solution)/shard_map/ppermute | solution.py:251
  74.5 3.4 %collective-permute-start.14 = (bf16[16,1024]{1,0:T(8,128)(2,1)S(1)}, bf16[16,1024]{1,0:T(8,128)(2,1)S(1)}, u32[]{:S(2)}, u32[]{:S(2)}) collective-permute-start(bf16[16,1024]{1,0:T(8,128)(2,1)S(1)} %get-tuple-element.72), channel_id=1, source_target_pairs={{0,3},{1,2},{2,1},{3,0},{4,7},{5,6},{6,5},{7,4},{8,11},{9,10},{10,... | collective-permute-start | bytes 98312 | tf_op jit(solution)/shard_map/ppermute | solution.py:251

commit v4 on v3

--- a/solution.py
+++ b/solution.py
@@ -18,6 +18,7 @@
 NEG_LARGE = -1e30
 LOG2_SCALE = float(HEAD_SIZE**-0.5 * np.log2(np.e))
 CODE = 32767.0
+STATS = 4 * GROUP
 VMEM_GRANT = 24 * 2**20
 F32, BF16, I16 = jnp.float32, jnp.bfloat16, jnp.int16
 
@@ -56,7 +57,7 @@
     return a[0] * fa + b[0] * fb, m, a[2] * fa + b[2] * fb
 
 
-def encode(state, out_ref, rows):
+def encode(state, out_ref, stats_ref, rows):
     n, m, t = state
     top = jnp.maximum(jnp.max(jnp.abs(n), axis=1, keepdims=True), 1e-30)
     codes = jnp.round(n * (CODE / top)).astype(jnp.int32).astype(I16)
@@ -67,12 +68,16 @@
         head = slice(g * rows, (g + 1) * rows)
         out_ref[:, g * HEAD_SIZE : (g + 1) * HEAD_SIZE] = codes[head]
         base = jnp.where(lane % GROUP == g, m[head], base)
-        value = jnp.where(lane % GROUP == g, jnp.where(lane < 2 * GROUP, top[head], t[head]), value)
+        value = jnp.where(lane % GROUP == g, jnp.where(lane % STATS < 2 * GROUP, top[head], t[head]), value)
     value = jnp.maximum(base * LOG2_SCALE + jnp.log2(value), -2000.0)
     high = jnp.round(value * 16.0)
     low = jnp.round((value - high * (1 / 16.0)) * 524288.0)
     stats = jnp.where(lane % (2 * GROUP) < GROUP, high, low)
-    out_ref[:, WIDTH:] = stats.astype(jnp.int32).astype(I16)
+    part = rows // 4
+    packed = stats[:part]
+    for k in range(1, 4):
+        packed = jnp.where(lane[:part] // STATS == k, stats[k * part : (k + 1) * part], packed)
+    stats_ref[...] = packed.astype(jnp.int32).astype(I16)
 
 
 def columns(j, width):
@@ -92,25 +97,36 @@
     )(*args)
 
 
-def split_kernel(shards, lens_ref, starts_ref, q_ref, sk_ref, sv_ref, k_ref, v_ref, *refs):
-    outs, (bias_ref, lens, starts, sems) = refs[:8], refs[8:]
-    copies = []
-
-    def copy(src, dst):
-        copies.append(pltpu.make_async_copy(src, dst, sems.at[len(copies)]))
-        copies[-1].start()
-
-    copy(lens_ref, lens)
-    copy(starts_ref, starts)
+def start_all(pairs, sems):
+    copies = [pltpu.make_async_copy(src, dst, sems.at[i]) for i, (src, dst) in enumerate(pairs)]
+    for c in copies:
+        c.start()
+    return copies
+
+
+def split_far_kernel(q_ref, sk_ref, sv_ref, k_ref, v_ref, *refs):
+    outs, sems = refs[:6], refs[6]
+    pairs = []
     for j in (2, 3, 1, 0):
         at = columns(j, HEAD_SIZE)
-        copy(q_ref.at[:, columns(j, WIDTH)], outs[j].at[:, pl.ds(0, WIDTH)])
-        copy(sk_ref.at[:, at], outs[j].at[:, pl.ds(WIDTH, HEAD_SIZE)])
-        copy(sv_ref.at[:, at], outs[j].at[:, pl.ds(WIDTH + HEAD_SIZE, HEAD_SIZE)])
-    for j in (2, 3, 1, 0):
+        pairs.append((q_ref.at[:, columns(j, WIDTH)], outs[j].at[:, pl.ds(0, WIDTH)]))
+        pairs.append((sk_ref.at[:, at], outs[j].at[:, pl.ds(WIDTH, HEAD_SIZE)]))
+        pairs.append((sv_ref.at[:, at], outs[j].at[:, pl.ds(WIDTH + HEAD_SIZE, HEAD_SIZE)]))
+    for out, j in zip(outs[4:], (2, 3)):
+        pairs.append((k_ref.at[:, columns(j, HEAD_SIZE)], out.at[:, pl.ds(0, HEAD_SIZE)]))
+        pairs.append((v_ref.at[:, columns(j, HEAD_SIZE)], out.at[:, pl.ds(HEAD_SIZE, HEAD_SIZE)]))
+    for c in start_all(pairs, sems):
+        c.wait()
+
+
+def split_near_kernel(shards, lens_ref, starts_ref, k_ref, v_ref, *refs):
+    outs, (bias_ref, lens, starts, sems) = refs[:2], refs[2:]
+    pairs = [(lens_ref, lens), (starts_ref, starts)]
+    for j in (1, 0):
         at = columns(j, HEAD_SIZE)
-        copy(k_ref.at[:, at], outs[4 + j].at[:, pl.ds(0, HEAD_SIZE)])
-        copy(v_ref.at[:, at], outs[4 + j].at[:, pl.ds(HEAD_SIZE, HEAD_SIZE)])
+        pairs.append((k_ref.at[:, at], outs[j].at[:, pl.ds(0, HEAD_SIZE)]))
+        pairs.append((v_ref.at[:, at], outs[j].at[:, pl.ds(HEAD_SIZE, HEAD_SIZE)]))
+    copies = start_all(pairs, sems)
     me = lax.axis_index("kvp")
     slots = k_ref.shape[0]
     for c in copies[:2]:
@@ -126,8 +142,10 @@
 
 def stack_kernel(*refs):
     rows = refs[0].shape[0]
-    for j, ref in enumerate(refs[:-1]):
-        refs[-1][j * rows : (j + 1) * rows, :] = ref[...]
+    both, only = refs[-2:]
+    for j, ref in enumerate(refs[:-2]):
+        both[j * rows : (j + 1) * rows, :] = ref[...]
+        only[j * rows : (j + 1) * rows, :] = ref[:, :WIDTH]
 
 
 def attend_kernel(cfg, bias_ref, *refs):
@@ -155,7 +173,7 @@
             bias = bias_ref[pl.ds(span * 4 + j, 1), :]
             state = merge(state, attend(q, kv_ref[:, :HEAD_SIZE], kv_ref[:, HEAD_SIZE:], bias))
         if finish == "encode":
-            encode(state, outs[i], rows)
+            encode(state, outs[2 * i], outs[2 * i + 1], rows)
             continue
         if finish == "span":
             mine, before = q_refs[i], span_ref
@@ -190,19 +208,19 @@
     if finish == "span":
         args.append(before)
     if finish == "encode":
-        shapes = [((rows, WIDTH + HEAD_SIZE), I16)] * len(blocks)
+        shapes = [((rows, WIDTH), I16), ((rows // 4, 4 * STATS), I16)] * len(blocks)
     else:
         shapes = [((rows, WIDTH), F32), ((GROUP * rows, 2 * HEAD_SIZE), F32)] * len(blocks)
     work = len(blocks) * GROUP * rows * sum(x.shape[0] for x in pieces.values())
     cfg = (shards, blocks, tuple(pieces), prior is not None, finish, rows)
     outs = local_call(functools.partial(attend_kernel, cfg), shapes, args, work=work)
     if finish == "encode":
-        return dict(zip(blocks, outs))
+        return outs
     return {d: (outs[2 * i], outs[2 * i + 1]) for i, d in enumerate(blocks)}
 
 
 def final_kernel(rows, n_ref, s_ref, *refs):
-    codes, outs = refs[:3], refs[3:]
+    codes, packed, outs = refs[:6:2], refs[1:6:2], refs[6:]
     part = rows // 4
     lane = lax.broadcasted_iota(jnp.int32, (rows, HEAD_SIZE), 1)
     m = jnp.zeros((rows, HEAD_SIZE), F32)
@@ -213,8 +231,9 @@
         t = jnp.where(lane == g, s_ref[head, HEAD_SIZE:], t)
     m = m * LOG2_SCALE
     tops, sums = [], []
-    for c in codes:
-        x = c[:, WIDTH:].astype(F32)
+    for p in packed:
+        x = p[...].astype(F32)
+        x = jnp.concatenate([x] + [pltpu.roll(x, 4 * STATS - k * STATS, 1) for k in range(1, 4)], axis=0)
         x = x * (1 / 16.0) + pltpu.roll(x, HEAD_SIZE - GROUP, 1) * (1 / 524288.0)
         tops.append(x)
         sums.append(pltpu.roll(x, HEAD_SIZE - 2 * GROUP, 1))
@@ -258,31 +277,41 @@
 
     part, slots = queries.shape[0], keys.shape[0]
     wide = WIDTH + 2 * HEAD_SIZE
-    *cut, bias = local_call(
-        functools.partial(split_kernel, n),
-        [((part, wide), BF16)] * 4 + [((slots, 2 * HEAD_SIZE), BF16)] * 4 + [((SPANS * 4, slots), F32)],
-        [pltpu.with_memory_space_constraint(x, pltpu.HBM) for x in tables + (queries, span_keys, span_values, keys, values)],
-        scratch=[pltpu.SMEM(x.shape, x.dtype) for x in tables] + [pltpu.SemaphoreType.DMA((22,))],
+    ins = [queries, span_keys, span_values, keys, values]
+    ins, tables = ([pltpu.with_memory_space_constraint(x, pltpu.HBM) for x in xs] for xs in (ins, tables))
+    *q_parts, kv2, kv3 = local_call(
+        split_far_kernel,
+        [((part, wide), BF16)] * 4 + [((slots, 2 * HEAD_SIZE), BF16)] * 2,
+        ins,
+        scratch=[pltpu.SemaphoreType.DMA((16,))],
         space=pltpu.HBM,
     )
-    q_parts, kv_parts = cut[:4], cut[4:]
+    kv0, kv1, bias = local_call(
+        functools.partial(split_near_kernel, n),
+        [((slots, 2 * HEAD_SIZE), BF16)] * 2 + [((SPANS * 4, slots), F32)],
+        tables + ins[3:],
+        scratch=[pltpu.SMEM(x.shape, x.dtype) for x in tables] + [pltpu.SemaphoreType.DMA((6,))],
+        space=pltpu.HBM,
+    )
     q_parts = [q_parts[0]] + [within(q_parts[j], j) for j in range(1, 4)]
-    kv = {0: kv_parts[0]} | {j: within(kv_parts[j], j) for j in (2, 3, 1)}
-    q = {0: local_call(stack_kernel, [((4 * part, wide), BF16)], q_parts)[0]}
-    for d in range(1, zs):
-        q[d] = along(q[0], d)
+    kv = {0: kv0, 1: within(kv1, 1), 2: within(kv2, 2), 3: within(kv3, 3)}
+    both, only = local_call(stack_kernel, [((4 * part, wide), BF16), ((4 * part, WIDTH), BF16)], q_parts)
+    q = {0: both, 1: along(both, 1)} | {d: along(only, d) for d in range(2, zs)}
 
     near = {j: kv[j] for j in (0, 1)}
-    s0 = attend({0: q[0]}, near)
+    state = attend({0: q[0]}, near)
+    state |= attend({1: q[1]}, near)
+    state = attend({0: q[0], 1: q[1]}, {2: kv[2]}, prior=state)
     near[2] = kv[2]
-    s1 = attend({1: q[1]}, near)
-    s23 = attend({2: q[2], 3: q[3]}, near)
-    kv[3], s0, s1, s23 = lax.optimization_barrier((kv[3], s0, s1, s23))
+    state |= attend({2: q[2], 3: q[3]}, near)
+    kv[3], state = lax.optimization_barrier((kv[3], state))
     last = {3: kv[3]}
-    codes = attend({2: q[2], 3: q[3]}, last, prior=s23, finish="encode")
-    codes |= attend({1: q[1]}, last, prior=s1, finish="encode")
-    back = [along(codes[d], d) for d in (2, 3, 1)]
-    mine = attend({0: q[0]}, {2: kv[2], 3: kv[3]}, prior=s0, finish="span", before=q[1])[0]
+    back = {}
+    for d in (2, 3, 1):
+        coded, stats = attend({d: q[d]}, last, prior=state, finish="encode")
+        back[d] = along(coded, d), along(stats, d)
+    back = [x for d in (2, 3, 1) for x in back[d]]
+    mine = attend({0: q[0]}, last, prior=state, finish="span", before=q[1])[0]
     parts = local_call(functools.partial(final_kernel, q[0].shape[0]), [((part, WIDTH), BF16)] * 4, (*mine, *back))
     parts = [parts[0]] + [within(parts[j], j) for j in range(1, 4)]
     return local_call(join_kernel, [((part, 4 * WIDTH), BF16)], parts)[0]

time: 78.7 us -> 77.4 us (0.983)
  waiting for transfers between devices: 42.2 us -> 32.9 us
  starting transfers between devices: 17 us -> 22.1 us
  Pallas kernels: 19.2 us -> 22.1 us
    ppermute x6 -> x9, waiting for transfers between devices: 16.9 us -> 7.43 us  [along(): return lax.ppermute(x, 'kvp', [(i, i ^ 4 * d) for i in range(n)])]
    ppermute x6 -> x9, starting transfers between devices: 8.98 us -> 14 us  [along(): return lax.ppermute(x, 'kvp', [(i, i ^ 4 * d) for i in range(n)])]
    pallas_call x10 -> x13, Pallas kernels: 19.2 us -> 22.1 us  [local_call(): pl.pallas_call(kernel, out_shape=[jax.ShapeDtypeStruct(s, t) for s, t in...]
  transfers between devices with their start and end apart: 15 -> 18, of which waited for: 7 -> 8; matrix products, arithmetic and copies ran while one was open for 0% -> 0% of each run, Pallas kernels for 18% -> 23%
where the time goes in v4:
time: 77.4 us; the launch traced here: 77.2 us
  waiting for transfers between devices  32.9 us (43%)
  Pallas kernels  22.1 us (29%)
  starting transfers between devices  22.1 us (29%)
    ppermute x9, waiting for transfers between devices, within(): return lax.ppermute(x, 'kvp', [(i, i ^ j) for i in range(n)])  25.5 us
    pallas_call x13, Pallas kernels, local_call(): pl.pallas_call(kernel, out_shape=[jax.ShapeDtypeStruct(s, t) for s, t in...  22.1 us
    ppermute x9, starting transfers between devices, along(): return lax.ppermute(x, 'kvp', [(i, i ^ 4 * d) for i in range(n)])  14 us
    ppermute x9, starting transfers between devices, within(): return lax.ppermute(x, 'kvp', [(i, i ^ j) for i in range(n)])  8.04 us
    ppermute x9, waiting for transfers between devices, along(): return lax.ppermute(x, 'kvp', [(i, i ^ 4 * d) for i in range(n)])  7.43 us
  transfers between devices with their start and end apart: 18, of which 8 were waited for; matrix products, arithmetic and copies ran while one was open for 0% of the time, Pallas kernels for 23%

profile of v4, /device:TPU:0, one launch (start us, length us, event | category | flops | bytes accessed | tf_op | source)
XLA Modules:
  0.0 77.2 jit_solution(16352863039188032261)
XLA Ops:
  0.0 1.3 %shard_map.73 = (bf16[1024,256]{1,0:T(8,128)(2,1)S(1)}, bf16[1024,256]{1,0:T(8,128)(2,1)S(1)}, f32[8,1024]{1,0:T(8,128)S(1)}) custom-call(s32[16]{0:T(128)} %lens_ref.1, s32[2]{0:T(128)} %starts_ref.1, bf16[1024,512]{1,0:T(8,128)(2,1)} %k_ref.3, bf16[1024,512]{1,0:T(8,128)(2,1)} %v_ref.3), custom_call_target="tpu_custom_call" | custom-call | bytes 2097224 | tf_op jit(solution)/shard_map/pallas_call | solution.py:89
  1.3 0.6 collective-permute-start.6
  1.8 1.5 %shard_map.74 = (bf16[16,1280]{1,0:T(8,128)(2,1)S(1)}, bf16[16,1280]{1,0:T(8,128)(2,1)S(1)}, bf16[16,1280]{1,0:T(8,128)(2,1)S(1)}, bf16[16,1280]{1,0:T(8,128)(2,...) custom-call(bf16[16,4096]{1,0:T(8,128)(2,1)} %q_ref.1, bf16[16,512]{1,0:T(8,128)(2,1)} %sk_ref.1, ...), custom_call_target="tpu_custom_call" | custom-call | bytes 2260992 | tf_op jit(solution)/shard_map/pallas_call | solution.py:89
  3.4 2.6 %collective-permute-start.5 = (bf16[1024,256]{1,0:T(8,128)(2,1)S(1)}, bf16[1024,256]{1,0:T(8,128)(2,1)S(1)}, u32[]{:S(2)}, u32[]{:S(2)}) collective-permute-start(bf16[1024,256]{1,0:T(8,128)(2,1)S(1)} %get-tuple-element.56), channel_id=1, source_target_pairs={{0,2},{1,3},{2,0},{3,1},{4,6},{5,7},{6,4},{7,5},{8,10},{9,11},{10,... | collective-permute-start | bytes 1572872 | tf_op jit(solution)/shard_map/ppermute | solution.py:270
  6.0 0.2 collective-permute-start.3
  6.1 0.0 collective-permute-start
  6.2 1.9 %collective-permute-start.1 = (bf16[16,1280]{1,0:T(8,128)(2,1)S(1)}, bf16[16,1280]{1,0:T(8,128)(2,1)S(1)}, u32[]{:S(2)}, u32[]{:S(2)}) collective-permute-start(bf16[16,1280]{1,0:T(8,128)(2,1)S(1)} %get-tuple-element.52), channel_id=1, source_target_pairs={{0,2},{1,3},{2,0},{3,1},{4,6},{5,7},{6,4},{7,5},{8,10},{9,11},{10,... | collective-permute-start | bytes 122888 | tf_op jit(solution)/shard_map/ppermute | solution.py:270
  8.1 0.0 collective-permute-done.refs_1_
  8.1 0.8 %collective-permute-start.2 = (bf16[16,1280]{1,0:T(8,128)(2,1)S(1)}, bf16[16,1280]{1,0:T(8,128)(2,1)S(1)}, u32[]{:S(2)}, u32[]{:S(2)}) collective-permute-start(bf16[16,1280]{1,0:T(8,128)(2,1)S(1)} %get-tuple-element.53), channel_id=1, source_target_pairs={{0,3},{1,2},{2,1},{3,0},{4,7},{5,6},{6,5},{7,4},{8,11},{9,10},{10,... | collective-permute-start | bytes 122888 | tf_op jit(solution)/shard_map/ppermute | solution.py:270
  8.9 21.9 %collective-permute-done.1.refs_2_ = bf16[16,1280]{1,0:T(8,128)(2,1)S(1)} collective-permute-done((bf16[16,1280]{1,0:T(8,128)(2,1)S(1)}, bf16[16,1280]{1,0:T(8,128)(2,1)S(1)}, u32[]{:S(2)}, u32[]{:S(2)}) %collective-permute-start.1) | collective-permute-done | bytes 40992 | tf_op jit(solution)/shard_map/ppermute | solution.py:270
  30.9 0.4 collective-permute-done.2.refs_3_
  31.3 1.6 %collective-permute-start.4 = (bf16[64,1280]{1,0:T(8,128)(2,1)S(1)}, bf16[64,1280]{1,0:T(8,128)(2,1)S(1)}, u32[]{:S(2)}, u32[]{:S(2)}) collective-permute-start(bf16[64,1280]{1,0:T(8,128)(2,1)S(1)} %get-tuple-element.54.refs_0_), channel_id=1, source_target_pairs={{0,4},{1,5},{2,6},{3,7},{4,0},{5,1},{6,2},{7,3},{8,12},{9,13},{10,... | collective-permute-start | bytes 491528 | tf_op jit(solution)/shard_map/ppermute | solution.py:273
  33.0 2.5 %collective-permute-start.8 = (bf16[64,1024]{1,0:T(8,128)(2,1)S(1)}, bf16[64,1024]{1,0:T(8,128)(2,1)S(1)}, u32[]{:S(2)}, u32[]{:S(2)}) collective-permute-start(bf16[64,1024]{1,0:T(8,128)(2,1)S(1)} %get-tuple-element.67), channel_id=1, source_target_pairs={{0,12},{1,13},{2,14},{3,15},{4,8},{5,9},{6,10},{7,11},{8,4},{9,5},... | collective-permute-start | bytes 393224 | tf_op jit(solution)/shard_map/ppermute | solution.py:273
  35.4 0.0 collective-permute-done.6.refs_2_.refs_3_
  35.4 0.1 collective-permute-start.7
  35.6 2.1 %shard_map.76 = (f32[64,1024]{1,0:T(8,128)S(1)}, f32[512,256]{1,0:T(8,128)S(1)}) custom-call(f32[8,1024]{1,0:T(8,128)S(1)} %get-tuple-element.49.bias_ref, bf16[64,1280]{1,0:T(8,128)(2,1)S(1)} %get-tuple-element.54.refs_0_, bf16[1024,256]{1,0:T(8,128)(2,1)S(1)} %get-tuple-element.57.refs_1_.refs_2_, bf16[1024,256]{1,0:T(8,128)(2,1)S(1)} %collective-permute-done.6.refs_2_.refs_3_), custom_call_target="tpu_custom_call" | custom-call | flops 536870912 | bytes 1245184 | tf_op jit(solution)/shard_map/pallas_call | solution.py:89
  37.7 0.0 collective-permute-done.4.refs_0_.refs_1_.refs_4_
  37.7 2.1 %shard_map.77 = (f32[64,1024]{1,0:T(8,128)S(1)}, f32[512,256]{1,0:T(8,128)S(1)}) custom-call(f32[8,1024]{1,0:T(8,128)S(1)} %get-tuple-element.49.bias_ref, bf16[64,1280]{1,0:T(8,128)(2,1)S(1)} %collective-permute-done.4.refs_0_.refs_1_.refs_4_, bf16[1024,256]{1,0:T(8,128)(2,1)S(1)} %get-tuple-element.57.refs_1_.refs_2_, ...), custom_call_target="tpu_custom_call" | custom-call | flops 536870912 | bytes 1245184 | tf_op jit(solution)/shard_map/pallas_call | solution.py:89
  39.9 0.0 collective-permute-done.5.refs_2_.refs_4_
  39.9 2.3 %shard_map.78 = (f32[64,1024]{1,0:T(8,128)S(1)}, f32[512,256]{1,0:T(8,128)S(1)}, f32[64,1024]{1,0:T(8,128)S(1)}, f32[512,256]{1,0:T(8,128)S(1)}) custom-call(f32[8,1024]{1,0:T(8,128)S(1)} %get-tuple-element.49.bias_ref, bf16[64,1280]{1,0:T(8,128)(2,1)S(1)} %get-tuple-element.54.refs_0_, bf16[64,1280]{1,0:T(8,128)(2,1)S(1)} %collective-permute-done.4.refs_0_.refs_1_.refs_4_, ...), custom_call_target="tpu_custom_call" | custom-call | flops 536870912 | bytes 2457600 | tf_op jit(solution)/shard_map/pallas_call | solution.py:89
  42.2 1.2 %collective-permute-done.8.refs_1_.refs_0_ = bf16[64,1024]{1,0:T(8,128)(2,1)S(1)} collective-permute-done((bf16[64,1024]{1,0:T(8,128)(2,1)S(1)}, bf16[64,1024]{1,0:T(8,128)(2,1)S(1)}, u32[]{:S(2)}, u32[]{:S(2)}) %collective-permute-start.8) | collective-permute-done | bytes 131104 | tf_op jit(solution)/shard_map/ppermute | solution.py:273
  43.4 4.2 %collective-permute-done.7.refs_0_ = bf16[64,1024]{1,0:T(8,128)(2,1)S(1)} collective-permute-done((bf16[64,1024]{1,0:T(8,128)(2,1)S(1)}, bf16[64,1024]{1,0:T(8,128)(2,1)S(1)}, u32[]{:S(2)}, u32[]{:S(2)}) %collective-permute-start.7) | collective-permute-done | bytes 131104 | tf_op jit(solution)/shard_map/ppermute | solution.py:273
  47.6 4.8 %shard_map.79 = (f32[64,1024]{1,0:T(8,128)S(1)}, f32[512,256]{1,0:T(8,128)S(1)}, f32[64,1024]{1,0:T(8,128)S(1)}, f32[512,256]{1,0:T(8,128)S(1)}) custom-call(f32[8,1024]{1,0:T(8,128)S(1)} %get-tuple-element.49.bias_ref, bf16[64,1024]{1,0:T(8,128)(2,1)S(1)} %collective-permute-done.7.refs_0_, bf16[64,1024]{1,0:T(8,128)(2,1)S(1)} %collective-permute-done.8.refs_1_.refs_0_, ...), custom_call_target="tpu_custom_call" | custom-call | flops 1610612736 | bytes 1867776 | tf_op jit(solution)/shard_map/pallas_call | solution.py:89
  52.5 0.0 collective-permute-done.3.refs_1_
  52.5 1.8 %shard_map.83 = (s16[64,1024]{1,0:T(8,128)(2,1)S(1)}, s16[16,128]{1,0:T(8,128)(2,1)S(1)}) custom-call(f32[8,1024]{1,0:T(8,128)S(1)} %get-tuple-element.49.bias_ref, bf16[64,1280]{1,0:T(8,128)(2,1)S(1)} %collective-permute-done.4.refs_0_.refs_1_.refs_4_, bf16[1024,256]{1,0:T(8,128)(2,1)S(1)} %collective-permute-done.3.refs_1_, ...), custom_call_target="tpu_custom_call" | custom-call | flops 268435456 | bytes 1507328 | tf_op jit(solution)/shard_map/pallas_call | solution.py:89
  54.3 0.1 collective-permute-start.13
  54.4 1.6 %shard_map.82 = (s16[64,1024]{1,0:T(8,128)(2,1)S(1)}, s16[16,128]{1,0:T(8,128)(2,1)S(1)}) custom-call(f32[8,1024]{1,0:T(8,128)S(1)} %get-tuple-element.49.bias_ref, bf16[64,1024]{1,0:T(8,128)(2,1)S(1)} %collective-permute-done.8.refs_1_.refs_0_, bf16[1024,256]{1,0:T(8,128)(2,1)S(1)} %collective-permute-done.3.refs_1_, ...), custom_call_target="tpu_custom_call" | custom-call | flops 268435456 | bytes 1474560 | tf_op jit(solution)/shard_map/pallas_call | solution.py:89
  56.0 2.7 %collective-permute-start.11 = (s16[64,1024]{1,0:T(8,128)(2,1)S(1)}, s16[64,1024]{1,0:T(8,128)(2,1)S(1)}, u32[]{:S(2)}, u32[]{:S(2)}) collective-permute-start(s16[64,1024]{1,0:T(8,128)(2,1)S(1)} %get-tuple-element.83), channel_id=1, source_target_pairs={{0,12},{1,13},{2,14},{3,15},{4,8},{5,9},{6,10},{7,11},{8,4},{9,5},... | collective-permute-start | bytes 393224 | tf_op jit(solution)/shard_map/ppermute | solution.py:273
  58.7 1.6 %shard_map.81 = (s16[64,1024]{1,0:T(8,128)(2,1)S(1)}, s16[16,128]{1,0:T(8,128)(2,1)S(1)}) custom-call(f32[8,1024]{1,0:T(8,128)S(1)} %get-tuple-element.49.bias_ref, bf16[64,1024]{1,0:T(8,128)(2,1)S(1)} %collective-permute-done.7.refs_0_, bf16[1024,256]{1,0:T(8,128)(2,1)S(1)} %collective-permute-done.3.refs_1_, f32[64,1024]{1,0:T(8,128)S(1)} %get-tuple-element.77.refs_2_, ...), custom_call_target="tpu_custom_call" | custom-call | flops 268435456 | bytes 1474560 | tf_op jit(solution)/shard_map/pallas_call | solution.py:89
  60.3 0.9 %collective-permute-start.9 = (s16[64,1024]{1,0:T(8,128)(2,1)S(1)}, s16[64,1024]{1,0:T(8,128)(2,1)S(1)}, u32[]{:S(2)}, u32[]{:S(2)}) collective-permute-start(s16[64,1024]{1,0:T(8,128)(2,1)S(1)} %get-tuple-element.79), channel_id=1, source_target_pairs={{0,8},{1,9},{2,10},{3,11},{4,12},{5,13},{6,14},{7,15},{8,0},{9,1},... | collective-permute-start | bytes 393224 | tf_op jit(solution)/shard_map/ppermute | solution.py:273
  61.2 0.9 %collective-permute-start.14 = (s16[16,128]{1,0:T(8,128)(2,1)S(1)}, s16[16,128]{1,0:T(8,128)(2,1)S(1)}, u32[]{:S(2)}, u32[]{:S(2)}) collective-permute-start(s16[16,128]{1,0:T(8,128)(2,1)S(1)} %get-tuple-element.88), channel_id=1, source_target_pairs={{0,4},{1,5},{2,6},{3,7},{4,0},{5,1},{6,2},{7,3},{8,12},{9,13},{10,... | collective-permute-start | bytes 12296 | tf_op jit(solution)/shard_map/ppermute | solution.py:273
  62.1 2.6 %collective-permute-start.12 = (s16[16,128]{1,0:T(8,128)(2,1)S(1)}, s16[16,128]{1,0:T(8,128)(2,1)S(1)}, u32[]{:S(2)}, u32[]{:S(2)}) collective-permute-start(s16[16,128]{1,0:T(8,128)(2,1)S(1)} %get-tuple-element.84), channel_id=1, source_target_pairs={{0,12},{1,13},{2,14},{3,15},{4,8},{5,9},{6,10},{7,11},{8,4},{9,5},... | collective-permute-start | bytes 12296 | tf_op jit(solution)/shard_map/ppermute | solution.py:273
  64.8 0.1 collective-permute-done.14.refs_5_
  64.8 2.6 %collective-permute-start.10 = (s16[16,128]{1,0:T(8,128)(2,1)S(1)}, s16[16,128]{1,0:T(8,128)(2,1)S(1)}, u32[]{:S(2)}, u32[]{:S(2)}) collective-permute-start(s16[16,128]{1,0:T(8,128)(2,1)S(1)} %get-tuple-element.80), channel_id=1, source_target_pairs={{0,8},{1,9},{2,10},{3,11},{4,12},{5,13},{6,14},{7,15},{8,0},{9,1},... | collective-permute-start | bytes 12296 | tf_op jit(solution)/shard_map/ppermute | solution.py:273
  67.4 1.6 %shard_map.80 = (f32[64,1024]{1,0:T(8,128)S(1)}, f32[512,256]{1,0:T(8,128)S(1)}) custom-call(f32[8,1024]{1,0:T(8,128)S(1)} %get-tuple-element.49.bias_ref, bf16[64,1280]{1,0:T(8,128)(2,1)S(1)} %get-tuple-element.54.refs_0_, bf16[1024,256]{1,0:T(8,128)(2,1)S(1)} %collective-permute-done.3.refs_1_, f32[64,1024]{1,0:T(8,128)S(1)} %get-tuple-element.73.refs_2_, ...), custom_call_target="tpu_custom_call" | custom-call | flops 268435456 | bytes 1671168 | tf_op jit(solution)/shard_map/pallas_call | solution.py:89
  69.0 0.0 collective-permute-done.12.refs_3_
  69.0 1.9 %collective-permute-done.10.refs_1_ = s16[16,128]{1,0:T(8,128)(2,1)S(1)} collective-permute-done((s16[16,128]{1,0:T(8,128)(2,1)S(1)}, s16[16,128]{1,0:T(8,128)(2,1)S(1)}, u32[]{:S(2)}, u32[]{:S(2)}) %collective-permute-start.10) | collective-permute-done | bytes 4128 | tf_op jit(solution)/shard_map/ppermute | solution.py:273
  70.9 0.0 collective-permute-done.13.refs_4_
  71.0 0.0 collective-permute-done.11.refs_2_
  71.0 0.0 collective-permute-done.9.refs_0_
  71.0 0.6 shard_map.84
  71.5 0.1 collective-permute-start.15
  71.6 1.6 %collective-permute-start.16 = (bf16[16,1024]{1,0:T(8,128)(2,1)S(1)}, bf16[16,1024]{1,0:T(8,128)(2,1)S(1)}, u32[]{:S(2)}, u32[]{:S(2)}) collective-permute-start(bf16[16,1024]{1,0:T(8,128)(2,1)S(1)} %get-tuple-element.91), channel_id=1, source_target_pairs={{0,2},{1,3},{2,0},{3,1},{4,6},{5,7},{6,4},{7,5},{8,10},{9,11},{10,... | collective-permute-start | bytes 98312 | tf_op jit(solution)/shard_map/ppermute | solution.py:270
  73.2 0.3 collective-permute-start.17
  73.5 0.0 collective-permute-done.15.refs_1_
  73.5 2.1 %collective-permute-done.16.refs_2_ = bf16[16,1024]{1,0:T(8,128)(2,1)S(1)} collective-permute-done((bf16[16,1024]{1,0:T(8,128)(2,1)S(1)}, bf16[16,1024]{1,0:T(8,128)(2,1)S(1)}, u32[]{:S(2)}, u32[]{:S(2)}) %collective-permute-start.16) | collective-permute-done | bytes 32800 | tf_op jit(solution)/shard_map/ppermute | solution.py:270
  75.6 1.0 %collective-permute-done.17.refs_3_ = bf16[16,1024]{1,0:T(8,128)(2,1)S(1)} collective-permute-done((bf16[16,1024]{1,0:T(8,128)(2,1)S(1)}, bf16[16,1024]{1,0:T(8,128)(2,1)S(1)}, u32[]{:S(2)}, u32[]{:S(2)}) %collective-permute-start.17) | collective-permute-done | bytes 32800 | tf_op jit(solution)/shard_map/ppermute | solution.py:270
  76.6 0.7 shard_map.85
  (1 shorter events, 0.0 us)
Async XLA Ops:
  1.3 34.2 %collective-permute-start.6 = (bf16[1024,256]{1,0:T(8,128)(2,1)S(1)}, bf16[1024,256]{1,0:T(8,128)(2,1)S(1)}, u32[]{:S(2)}, u32[]{:S(2)}) collective-permute-start(bf16[1024,256]{1,0:T(8,128)(2,1)S(1)} %get-tuple-element.58), channel_id=1, source_target_pairs={{0,1},{1,0},{2,3},{3,2},{4,5},{5,4},{6,7},{7,6},{8,9},{9,8},{10,11... | collective-permute-start | bytes 1572872 | tf_op jit(solution)/shard_map/ppermute | solution.py:270
  3.4 36.5 %collective-permute-start.5 = (bf16[1024,256]{1,0:T(8,128)(2,1)S(1)}, bf16[1024,256]{1,0:T(8,128)(2,1)S(1)}, u32[]{:S(2)}, u32[]{:S(2)}) collective-permute-start(bf16[1024,256]{1,0:T(8,128)(2,1)S(1)} %get-tuple-element.56), channel_id=1, source_target_pairs={{0,2},{1,3},{2,0},{3,1},{4,6},{5,7},{6,4},{7,5},{8,10},{9,11},{10,... | collective-permute-start | bytes 1572872 | tf_op jit(solution)/shard_map/ppermute | solution.py:270
  6.0 46.5 %collective-permute-start.3 = (bf16[1024,256]{1,0:T(8,128)(2,1)S(1)}, bf16[1024,256]{1,0:T(8,128)(2,1)S(1)}, u32[]{:S(2)}, u32[]{:S(2)}) collective-permute-start(bf16[1024,256]{1,0:T(8,128)(2,1)S(1)} %get-tuple-element.55), channel_id=1, source_target_pairs={{0,3},{1,2},{2,1},{3,0},{4,7},{5,6},{6,5},{7,4},{8,11},{9,10},{10,... | collective-permute-start | bytes 1572872 | tf_op jit(solution)/shard_map/ppermute | solution.py:270
  6.1 2.0 %collective-permute-start = (bf16[16,1280]{1,0:T(8,128)(2,1)S(1)}, bf16[16,1280]{1,0:T(8,128)(2,1)S(1)}, u32[]{:S(2)}, u32[]{:S(2)}) collective-permute-start(bf16[16,1280]{1,0:T(8,128)(2,1)S(1)} %get-tuple-element.51), channel_id=1, source_target_pairs={{0,1},{1,0},{2,3},{3,2},{4,5},{5,4},{6,7},{7,6},{8,9},{9,8},{10,11... | collective-permute-start | bytes 122888 | tf_op jit(solution)/shard_map/ppermute | solution.py:270
  6.2 24.7 %collective-permute-start.1 = (bf16[16,1280]{1,0:T(8,128)(2,1)S(1)}, bf16[16,1280]{1,0:T(8,128)(2,1)S(1)}, u32[]{:S(2)}, u32[]{:S(2)}) collective-permute-start(bf16[16,1280]{1,0:T(8,128)(2,1)S(1)} %get-tuple-element.52), channel_id=1, source_target_pairs={{0,2},{1,3},{2,0},{3,1},{4,6},{5,7},{6,4},{7,5},{8,10},{9,11},{10,... | collective-permute-start | bytes 122888 | tf_op jit(solution)/shard_map/ppermute | solution.py:270
  8.1 23.2 %collective-permute-start.2 = (bf16[16,1280]{1,0:T(8,128)(2,1)S(1)}, bf16[16,1280]{1,0:T(8,128)(2,1)S(1)}, u32[]{:S(2)}, u32[]{:S(2)}) collective-permute-start(bf16[16,1280]{1,0:T(8,128)(2,1)S(1)} %get-tuple-element.53), channel_id=1, source_target_pairs={{0,3},{1,2},{2,1},{3,0},{4,7},{5,6},{6,5},{7,4},{8,11},{9,10},{10,... | collective-permute-start | bytes 122888 | tf_op jit(solution)/shard_map/ppermute | solution.py:270
  31.3 6.4 %collective-permute-start.4 = (bf16[64,1280]{1,0:T(8,128)(2,1)S(1)}, bf16[64,1280]{1,0:T(8,128)(2,1)S(1)}, u32[]{:S(2)}, u32[]{:S(2)}) collective-permute-start(bf16[64,1280]{1,0:T(8,128)(2,1)S(1)} %get-tuple-element.54.refs_0_), channel_id=1, source_target_pairs={{0,4},{1,5},{2,6},{3,7},{4,0},{5,1},{6,2},{7,3},{8,12},{9,13},{10,... | collective-permute-start | bytes 491528 | tf_op jit(solution)/shard_map/ppermute | solution.py:273
  33.0 10.4 %collective-permute-start.8 = (bf16[64,1024]{1,0:T(8,128)(2,1)S(1)}, bf16[64,1024]{1,0:T(8,128)(2,1)S(1)}, u32[]{:S(2)}, u32[]{:S(2)}) collective-permute-start(bf16[64,1024]{1,0:T(8,128)(2,1)S(1)} %get-tuple-element.67), channel_id=1, source_target_pairs={{0,12},{1,13},{2,14},{3,15},{4,8},{5,9},{6,10},{7,11},{8,4},{9,5},... | collective-permute-start | bytes 393224 | tf_op jit(solution)/shard_map/ppermute | solution.py:273
  35.4 12.2 %collective-permute-start.7 = (bf16[64,1024]{1,0:T(8,128)(2,1)S(1)}, bf16[64,1024]{1,0:T(8,128)(2,1)S(1)}, u32[]{:S(2)}, u32[]{:S(2)}) collective-permute-start(bf16[64,1024]{1,0:T(8,128)(2,1)S(1)} %get-tuple-element.67), channel_id=1, source_target_pairs={{0,8},{1,9},{2,10},{3,11},{4,12},{5,13},{6,14},{7,15},{8,0},{9,1},... | collective-permute-start | bytes 393224 | tf_op jit(solution)/shard_map/ppermute | solution.py:273
  54.3 16.7 %collective-permute-start.13 = (s16[64,1024]{1,0:T(8,128)(2,1)S(1)}, s16[64,1024]{1,0:T(8,128)(2,1)S(1)}, u32[]{:S(2)}, u32[]{:S(2)}) collective-permute-start(s16[64,1024]{1,0:T(8,128)(2,1)S(1)} %get-tuple-element.87), channel_id=1, source_target_pairs={{0,4},{1,5},{2,6},{3,7},{4,0},{5,1},{6,2},{7,3},{8,12},{9,13},{10,... | collective-permute-start | bytes 393224 | tf_op jit(solution)/shard_map/ppermute | solution.py:273
  56.0 15.0 %collective-permute-start.11 = (s16[64,1024]{1,0:T(8,128)(2,1)S(1)}, s16[64,1024]{1,0:T(8,128)(2,1)S(1)}, u32[]{:S(2)}, u32[]{:S(2)}) collective-permute-start(s16[64,1024]{1,0:T(8,128)(2,1)S(1)} %get-tuple-element.83), channel_id=1, source_target_pairs={{0,12},{1,13},{2,14},{3,15},{4,8},{5,9},{6,10},{7,11},{8,4},{9,5},... | collective-permute-start | bytes 393224 | tf_op jit(solution)/shard_map/ppermute | solution.py:273
  60.3 10.7 %collective-permute-start.9 = (s16[64,1024]{1,0:T(8,128)(2,1)S(1)}, s16[64,1024]{1,0:T(8,128)(2,1)S(1)}, u32[]{:S(2)}, u32[]{:S(2)}) collective-permute-start(s16[64,1024]{1,0:T(8,128)(2,1)S(1)} %get-tuple-element.79), channel_id=1, source_target_pairs={{0,8},{1,9},{2,10},{3,11},{4,12},{5,13},{6,14},{7,15},{8,0},{9,1},... | collective-permute-start | bytes 393224 | tf_op jit(solution)/shard_map/ppermute | solution.py:273
  61.2 3.6 %collective-permute-start.14 = (s16[16,128]{1,0:T(8,128)(2,1)S(1)}, s16[16,128]{1,0:T(8,128)(2,1)S(1)}, u32[]{:S(2)}, u32[]{:S(2)}) collective-permute-start(s16[16,128]{1,0:T(8,128)(2,1)S(1)} %get-tuple-element.88), channel_id=1, source_target_pairs={{0,4},{1,5},{2,6},{3,7},{4,0},{5,1},{6,2},{7,3},{8,12},{9,13},{10,... | collective-permute-start | bytes 12296 | tf_op jit(solution)/shard_map/ppermute | solution.py:273
  62.1 6.9 %collective-permute-start.12 = (s16[16,128]{1,0:T(8,128)(2,1)S(1)}, s16[16,128]{1,0:T(8,128)(2,1)S(1)}, u32[]{:S(2)}, u32[]{:S(2)}) collective-permute-start(s16[16,128]{1,0:T(8,128)(2,1)S(1)} %get-tuple-element.84), channel_id=1, source_target_pairs={{0,12},{1,13},{2,14},{3,15},{4,8},{5,9},{6,10},{7,11},{8,4},{9,5},... | collective-permute-start | bytes 12296 | tf_op jit(solution)/shard_map/ppermute | solution.py:273
  64.8 6.1 %collective-permute-start.10 = (s16[16,128]{1,0:T(8,128)(2,1)S(1)}, s16[16,128]{1,0:T(8,128)(2,1)S(1)}, u32[]{:S(2)}, u32[]{:S(2)}) collective-permute-start(s16[16,128]{1,0:T(8,128)(2,1)S(1)} %get-tuple-element.80), channel_id=1, source_target_pairs={{0,8},{1,9},{2,10},{3,11},{4,12},{5,13},{6,14},{7,15},{8,0},{9,1},... | collective-permute-start | bytes 12296 | tf_op jit(solution)/shard_map/ppermute | solution.py:273
  71.5 1.9 %collective-permute-start.15 = (bf16[16,1024]{1,0:T(8,128)(2,1)S(1)}, bf16[16,1024]{1,0:T(8,128)(2,1)S(1)}, u32[]{:S(2)}, u32[]{:S(2)}) collective-permute-start(bf16[16,1024]{1,0:T(8,128)(2,1)S(1)} %get-tuple-element.90), channel_id=1, source_target_pairs={{0,1},{1,0},{2,3},{3,2},{4,5},{5,4},{6,7},{7,6},{8,9},{9,8},{10,11... | collective-permute-start | bytes 98312 | tf_op jit(solution)/shard_map/ppermute | solution.py:270
  71.6 4.0 %collective-permute-start.16 = (bf16[16,1024]{1,0:T(8,128)(2,1)S(1)}, bf16[16,1024]{1,0:T(8,128)(2,1)S(1)}, u32[]{:S(2)}, u32[]{:S(2)}) collective-permute-start(bf16[16,1024]{1,0:T(8,128)(2,1)S(1)} %get-tuple-element.91), channel_id=1, source_target_pairs={{0,2},{1,3},{2,0},{3,1},{4,6},{5,7},{6,4},{7,5},{8,10},{9,11},{10,... | collective-permute-start | bytes 98312 | tf_op jit(solution)/shard_map/ppermute | solution.py:270
  73.2 3.4 %collective-permute-start.17 = (bf16[16,1024]{1,0:T(8,128)(2,1)S(1)}, bf16[16,1024]{1,0:T(8,128)(2,1)S(1)}, u32[]{:S(2)}, u32[]{:S(2)}) collective-permute-start(bf16[16,1024]{1,0:T(8,128)(2,1)S(1)} %get-tuple-element.92), channel_id=1, source_target_pairs={{0,3},{1,2},{2,1},{3,0},{4,7},{5,6},{6,5},{7,4},{8,11},{9,10},{10,... | collective-permute-start | bytes 98312 | tf_op jit(solution)/shard_map/ppermute | solution.py:270

commit v5 on v4

--- a/solution.py
+++ b/solution.py
@@ -57,16 +57,15 @@
     return a[0] * fa + b[0] * fb, m, a[2] * fa + b[2] * fb
 
 
-def encode(state, out_ref, stats_ref, rows):
+def encode(state, out_ref, rows):
     n, m, t = state
     top = jnp.maximum(jnp.max(jnp.abs(n), axis=1, keepdims=True), 1e-30)
-    codes = jnp.round(n * (CODE / top)).astype(jnp.int32).astype(I16)
+    out_ref[: GROUP * rows, :] = jnp.round(n * (CODE / top)).astype(jnp.int32).astype(I16)
     lane = lax.broadcasted_iota(jnp.int32, (rows, HEAD_SIZE), 1)
     base = jnp.zeros((rows, HEAD_SIZE), F32)
     value = jnp.ones((rows, HEAD_SIZE), F32)
     for g in range(GROUP):
         head = slice(g * rows, (g + 1) * rows)
-        out_ref[:, g * HEAD_SIZE : (g + 1) * HEAD_SIZE] = codes[head]
         base = jnp.where(lane % GROUP == g, m[head], base)
         value = jnp.where(lane % GROUP == g, jnp.where(lane % STATS < 2 * GROUP, top[head], t[head]), value)
     value = jnp.maximum(base * LOG2_SCALE + jnp.log2(value), -2000.0)
@@ -77,7 +76,7 @@
     packed = stats[:part]
     for k in range(1, 4):
         packed = jnp.where(lane[:part] // STATS == k, stats[k * part : (k + 1) * part], packed)
-    stats_ref[...] = packed.astype(jnp.int32).astype(I16)
+    out_ref[GROUP * rows :, :] = packed.astype(jnp.int32).astype(I16)
 
 
 def columns(j, width):
@@ -173,7 +172,7 @@
             bias = bias_ref[pl.ds(span * 4 + j, 1), :]
             state = merge(state, attend(q, kv_ref[:, :HEAD_SIZE], kv_ref[:, HEAD_SIZE:], bias))
         if finish == "encode":
-            encode(state, outs[2 * i], outs[2 * i + 1], rows)
+            encode(state, outs[i], rows)
             continue
         if finish == "span":
             mine, before = q_refs[i], span_ref
@@ -208,7 +207,7 @@
     if finish == "span":
         args.append(before)
     if finish == "encode":
-        shapes = [((rows, WIDTH), I16), ((rows // 4, 4 * STATS), I16)] * len(blocks)
+        shapes = [((GROUP * rows + rows // 4, HEAD_SIZE), I16)] * len(blocks)
     else:
         shapes = [((rows, WIDTH), F32), ((GROUP * rows, 2 * HEAD_SIZE), F32)] * len(blocks)
     work = len(blocks) * GROUP * rows * sum(x.shape[0] for x in pieces.values())
@@ -220,7 +219,7 @@
 
 
 def final_kernel(rows, n_ref, s_ref, *refs):
-    codes, packed, outs = refs[:6:2], refs[1:6:2], refs[6:]
+    codes, outs = refs[:3], refs[3:]
     part = rows // 4
     lane = lax.broadcasted_iota(jnp.int32, (rows, HEAD_SIZE), 1)
     m = jnp.zeros((rows, HEAD_SIZE), F32)
@@ -231,8 +230,8 @@
         t = jnp.where(lane == g, s_ref[head, HEAD_SIZE:], t)
     m = m * LOG2_SCALE
     tops, sums = [], []
-    for p in packed:
-        x = p[...].astype(F32)
+    for c in codes:
+        x = c[GROUP * rows :, :].astype(F32)
         x = jnp.concatenate([x] + [pltpu.roll(x, 4 * STATS - k * STATS, 1) for k in range(1, 4)], axis=0)
         x = x * (1 / 16.0) + pltpu.roll(x, HEAD_SIZE - GROUP, 1) * (1 / 524288.0)
         tops.append(x)
@@ -250,7 +249,7 @@
         cols = slice(g * HEAD_SIZE, (g + 1) * HEAD_SIZE)
         n = n_ref[:, cols] * factors[0][:, g : g + 1]
         for c, f in zip(codes, factors[1:]):
-            n = n + c[:, cols].astype(F32) * f[:, g : g + 1]
+            n = n + c[g * rows : (g + 1) * rows, :].astype(F32) * f[:, g : g + 1]
         n = n.astype(BF16)
         for k in range(4):
             outs[k][:, cols] = n[k * part : (k + 1) * part]
@@ -306,11 +305,10 @@
     state |= attend({2: q[2], 3: q[3]}, near)
     kv[3], state = lax.optimization_barrier((kv[3], state))
     last = {3: kv[3]}
-    back = {}
-    for d in (2, 3, 1):
-        coded, stats = attend({d: q[d]}, last, prior=state, finish="encode")
-        back[d] = along(coded, d), along(stats, d)
-    back = [x for d in (2, 3, 1) for x in back[d]]
+    back = []
+    for d in (2, 1, 3):
+        (coded,) = attend({d: q[d]}, last, prior=state, finish="encode")
+        back.append(along(coded, d))
     mine = attend({0: q[0]}, last, prior=state, finish="span", before=q[1])[0]
     parts = local_call(functools.partial(final_kernel, q[0].shape[0]), [((part, WIDTH), BF16)] * 4, (*mine, *back))
     parts = [parts[0]] + [within(parts[j], j) for j in range(1, 4)]

time: 77.4 us -> 75 us (0.969)
  starting transfers between devices: 22.1 us -> 16 us
  waiting for transfers between devices: 32.9 us -> 36.6 us
    ppermute x9 -> x6, starting transfers between devices: 14 us -> 7.92 us  [along(): return lax.ppermute(x, 'kvp', [(i, i ^ 4 * d) for i in range(n)])]
    ppermute x9 -> x6, waiting for transfers between devices: 7.43 us -> 11.2 us  [along(): return lax.ppermute(x, 'kvp', [(i, i ^ 4 * d) for i in range(n)])]
  transfers between devices with their start and end apart: 18 -> 15, of which waited for: 8 -> 8; matrix products, arithmetic and copies ran while one was open for 0% -> 0% of each run, Pallas kernels for 23% -> 24%
where the time goes in v5:
time: 75 us; the launch traced here: 74.8 us
  waiting for transfers between devices  36.6 us (49%)
  Pallas kernels  22.1 us (29%)
  starting transfers between devices  16 us (21%)
    ppermute x9, waiting for transfers between devices, within(): return lax.ppermute(x, 'kvp', [(i, i ^ j) for i in range(n)])  25.5 us
    pallas_call x13, Pallas kernels, local_call(): pl.pallas_call(kernel, out_shape=[jax.ShapeDtypeStruct(s, t) for s, t in...  22.1 us
    ppermute x6, waiting for transfers between devices, along(): return lax.ppermute(x, 'kvp', [(i, i ^ 4 * d) for i in range(n)])  11.2 us
    ppermute x9, starting transfers between devices, within(): return lax.ppermute(x, 'kvp', [(i, i ^ j) for i in range(n)])  8.05 us
    ppermute x6, starting transfers between devices, along(): return lax.ppermute(x, 'kvp', [(i, i ^ 4 * d) for i in range(n)])  7.92 us
  transfers between devices with their start and end apart: 15, of which 8 were waited for; matrix products, arithmetic and copies ran while one was open for 0% of the time, Pallas kernels for 24%

profile of v5, /device:TPU:0, one launch (start us, length us, event | category | flops | bytes accessed | tf_op | source)
XLA Modules:
  0.0 74.8 jit_solution(13800409816966858808)
XLA Ops:
  0.0 1.3 %shard_map.73 = (bf16[1024,256]{1,0:T(8,128)(2,1)S(1)}, bf16[1024,256]{1,0:T(8,128)(2,1)S(1)}, f32[8,1024]{1,0:T(8,128)S(1)}) custom-call(s32[16]{0:T(128)} %lens_ref.1, s32[2]{0:T(128)} %starts_ref.1, bf16[1024,512]{1,0:T(8,128)(2,1)} %k_ref.3, bf16[1024,512]{1,0:T(8,128)(2,1)} %v_ref.3), custom_call_target="tpu_custom_call" | custom-call | bytes 2097224 | tf_op jit(solution)/shard_map/pallas_call | solution.py:88
  1.3 0.6 collective-permute-start.6
  1.8 1.5 %shard_map.74 = (bf16[16,1280]{1,0:T(8,128)(2,1)S(1)}, bf16[16,1280]{1,0:T(8,128)(2,1)S(1)}, bf16[16,1280]{1,0:T(8,128)(2,1)S(1)}, bf16[16,1280]{1,0:T(8,128)(2,...) custom-call(bf16[16,4096]{1,0:T(8,128)(2,1)} %q_ref.1, bf16[16,512]{1,0:T(8,128)(2,1)} %sk_ref.1, ...), custom_call_target="tpu_custom_call" | custom-call | bytes 2260992 | tf_op jit(solution)/shard_map/pallas_call | solution.py:88
  3.4 2.6 %collective-permute-start.5 = (bf16[1024,256]{1,0:T(8,128)(2,1)S(1)}, bf16[1024,256]{1,0:T(8,128)(2,1)S(1)}, u32[]{:S(2)}, u32[]{:S(2)}) collective-permute-start(bf16[1024,256]{1,0:T(8,128)(2,1)S(1)} %get-tuple-element.50), channel_id=1, source_target_pairs={{0,2},{1,3},{2,0},{3,1},{4,6},{5,7},{6,4},{7,5},{8,10},{9,11},{10,... | collective-permute-start | bytes 1572872 | tf_op jit(solution)/shard_map/ppermute | solution.py:269
  6.0 0.2 collective-permute-start.3
  6.1 0.0 collective-permute-start
  6.2 1.9 %collective-permute-start.1 = (bf16[16,1280]{1,0:T(8,128)(2,1)S(1)}, bf16[16,1280]{1,0:T(8,128)(2,1)S(1)}, u32[]{:S(2)}, u32[]{:S(2)}) collective-permute-start(bf16[16,1280]{1,0:T(8,128)(2,1)S(1)} %get-tuple-element.46), channel_id=1, source_target_pairs={{0,2},{1,3},{2,0},{3,1},{4,6},{5,7},{6,4},{7,5},{8,10},{9,11},{10,... | collective-permute-start | bytes 122888 | tf_op jit(solution)/shard_map/ppermute | solution.py:269
  8.1 0.0 collective-permute-done.refs_1_
  8.1 0.8 %collective-permute-start.2 = (bf16[16,1280]{1,0:T(8,128)(2,1)S(1)}, bf16[16,1280]{1,0:T(8,128)(2,1)S(1)}, u32[]{:S(2)}, u32[]{:S(2)}) collective-permute-start(bf16[16,1280]{1,0:T(8,128)(2,1)S(1)} %get-tuple-element.47), channel_id=1, source_target_pairs={{0,3},{1,2},{2,1},{3,0},{4,7},{5,6},{6,5},{7,4},{8,11},{9,10},{10,... | collective-permute-start | bytes 122888 | tf_op jit(solution)/shard_map/ppermute | solution.py:269
  8.9 21.9 %collective-permute-done.1.refs_2_ = bf16[16,1280]{1,0:T(8,128)(2,1)S(1)} collective-permute-done((bf16[16,1280]{1,0:T(8,128)(2,1)S(1)}, bf16[16,1280]{1,0:T(8,128)(2,1)S(1)}, u32[]{:S(2)}, u32[]{:S(2)}) %collective-permute-start.1) | collective-permute-done | bytes 40992 | tf_op jit(solution)/shard_map/ppermute | solution.py:269
  30.9 0.4 collective-permute-done.2.refs_3_
  31.3 1.6 %collective-permute-start.4 = (bf16[64,1280]{1,0:T(8,128)(2,1)S(1)}, bf16[64,1280]{1,0:T(8,128)(2,1)S(1)}, u32[]{:S(2)}, u32[]{:S(2)}) collective-permute-start(bf16[64,1280]{1,0:T(8,128)(2,1)S(1)} %get-tuple-element.48.refs_0_), channel_id=1, source_target_pairs={{0,4},{1,5},{2,6},{3,7},{4,0},{5,1},{6,2},{7,3},{8,12},{9,13},{10,... | collective-permute-start | bytes 491528 | tf_op jit(solution)/shard_map/ppermute | solution.py:272
  33.0 2.5 %collective-permute-start.8 = (bf16[64,1024]{1,0:T(8,128)(2,1)S(1)}, bf16[64,1024]{1,0:T(8,128)(2,1)S(1)}, u32[]{:S(2)}, u32[]{:S(2)}) collective-permute-start(bf16[64,1024]{1,0:T(8,128)(2,1)S(1)} %get-tuple-element.61), channel_id=1, source_target_pairs={{0,12},{1,13},{2,14},{3,15},{4,8},{5,9},{6,10},{7,11},{8,4},{9,5},... | collective-permute-start | bytes 393224 | tf_op jit(solution)/shard_map/ppermute | solution.py:272
  35.4 0.0 collective-permute-done.6.refs_2_.refs_3_
  35.4 0.1 collective-permute-start.7
  35.6 2.1 %shard_map.76 = (f32[64,1024]{1,0:T(8,128)S(1)}, f32[512,256]{1,0:T(8,128)S(1)}) custom-call(f32[8,1024]{1,0:T(8,128)S(1)} %get-tuple-element.43.bias_ref, bf16[64,1280]{1,0:T(8,128)(2,1)S(1)} %get-tuple-element.48.refs_0_, bf16[1024,256]{1,0:T(8,128)(2,1)S(1)} %get-tuple-element.51.refs_1_.refs_2_, bf16[1024,256]{1,0:T(8,128)(2,1)S(1)} %collective-permute-done.6.refs_2_.refs_3_), custom_call_target="tpu_custom_call" | custom-call | flops 536870912 | bytes 1245184 | tf_op jit(solution)/shard_map/pallas_call | solution.py:88
  37.7 0.0 collective-permute-done.4.refs_0_.refs_1_.refs_4_
  37.7 2.1 %shard_map.77 = (f32[64,1024]{1,0:T(8,128)S(1)}, f32[512,256]{1,0:T(8,128)S(1)}) custom-call(f32[8,1024]{1,0:T(8,128)S(1)} %get-tuple-element.43.bias_ref, bf16[64,1280]{1,0:T(8,128)(2,1)S(1)} %collective-permute-done.4.refs_0_.refs_1_.refs_4_, bf16[1024,256]{1,0:T(8,128)(2,1)S(1)} %get-tuple-element.51.refs_1_.refs_2_, ...), custom_call_target="tpu_custom_call" | custom-call | flops 536870912 | bytes 1245184 | tf_op jit(solution)/shard_map/pallas_call | solution.py:88
  39.9 0.0 collective-permute-done.5.refs_2_.refs_4_
  39.9 2.3 %shard_map.78 = (f32[64,1024]{1,0:T(8,128)S(1)}, f32[512,256]{1,0:T(8,128)S(1)}, f32[64,1024]{1,0:T(8,128)S(1)}, f32[512,256]{1,0:T(8,128)S(1)}) custom-call(f32[8,1024]{1,0:T(8,128)S(1)} %get-tuple-element.43.bias_ref, bf16[64,1280]{1,0:T(8,128)(2,1)S(1)} %get-tuple-element.48.refs_0_, bf16[64,1280]{1,0:T(8,128)(2,1)S(1)} %collective-permute-done.4.refs_0_.refs_1_.refs_4_, ...), custom_call_target="tpu_custom_call" | custom-call | flops 536870912 | bytes 2457600 | tf_op jit(solution)/shard_map/pallas_call | solution.py:88
  42.2 1.2 %collective-permute-done.8.refs_1_.refs_0_ = bf16[64,1024]{1,0:T(8,128)(2,1)S(1)} collective-permute-done((bf16[64,1024]{1,0:T(8,128)(2,1)S(1)}, bf16[64,1024]{1,0:T(8,128)(2,1)S(1)}, u32[]{:S(2)}, u32[]{:S(2)}) %collective-permute-start.8) | collective-permute-done | bytes 131104 | tf_op jit(solution)/shard_map/ppermute | solution.py:272
  43.4 4.2 %collective-permute-done.7.refs_0_ = bf16[64,1024]{1,0:T(8,128)(2,1)S(1)} collective-permute-done((bf16[64,1024]{1,0:T(8,128)(2,1)S(1)}, bf16[64,1024]{1,0:T(8,128)(2,1)S(1)}, u32[]{:S(2)}, u32[]{:S(2)}) %collective-permute-start.7) | collective-permute-done | bytes 131104 | tf_op jit(solution)/shard_map/ppermute | solution.py:272
  47.6 4.8 %shard_map.79 = (f32[64,1024]{1,0:T(8,128)S(1)}, f32[512,256]{1,0:T(8,128)S(1)}, f32[64,1024]{1,0:T(8,128)S(1)}, f32[512,256]{1,0:T(8,128)S(1)}) custom-call(f32[8,1024]{1,0:T(8,128)S(1)} %get-tuple-element.43.bias_ref, bf16[64,1024]{1,0:T(8,128)(2,1)S(1)} %collective-permute-done.7.refs_0_, bf16[64,1024]{1,0:T(8,128)(2,1)S(1)} %collective-permute-done.8.refs_1_.refs_0_, ...), custom_call_target="tpu_custom_call" | custom-call | flops 1610612736 | bytes 1867776 | tf_op jit(solution)/shard_map/pallas_call | solution.py:88
  52.5 0.0 collective-permute-done.3.refs_1_
  52.5 1.8 %shard_map.81 = s16[528,128]{1,0:T(8,128)(2,1)S(1)} custom-call(f32[8,1024]{1,0:T(8,128)S(1)} %get-tuple-element.43.bias_ref, bf16[64,1024]{1,0:T(8,128)(2,1)S(1)} %collective-permute-done.7.refs_0_, bf16[1024,256]{1,0:T(8,128)(2,1)S(1)} %collective-permute-done.3.refs_1_, f32[64,1024]{1,0:T(8,128)S(1)} %get-tuple-element.71.refs_2_, ...), custom_call_target="tpu_custom_call" | custom-call | flops 268435456 | bytes 1474560 | tf_op jit(solution)/shard_map/pallas_call | solution.py:88
  54.3 0.1 collective-permute-start.9
  54.3 1.6 %shard_map.83 = s16[528,128]{1,0:T(8,128)(2,1)S(1)} custom-call(f32[8,1024]{1,0:T(8,128)S(1)} %get-tuple-element.43.bias_ref, bf16[64,1024]{1,0:T(8,128)(2,1)S(1)} %collective-permute-done.8.refs_1_.refs_0_, bf16[1024,256]{1,0:T(8,128)(2,1)S(1)} %collective-permute-done.3.refs_1_, f32[64,1024]{1,0:T(8,128)S(1)} %get-tuple-element.75.refs_2_, ...), custom_call_target="tpu_custom_call" | custom-call | flops 268435456 | bytes 1474560 | tf_op jit(solution)/shard_map/pallas_call | solution.py:88
  56.0 2.7 %collective-permute-start.11 = (s16[528,128]{1,0:T(8,128)(2,1)S(1)}, s16[528,128]{1,0:T(8,128)(2,1)S(1)}, u32[]{:S(2)}, u32[]{:S(2)}) collective-permute-start(s16[528,128]{1,0:T(8,128)(2,1)S(1)} %shard_map.83), channel_id=1, source_target_pairs={{0,12},{1,13},{2,14},{3,15},{4,8},{5,9},{6,10},{7,11},{8,4},{9,5},... | collective-permute-start | bytes 405512 | tf_op jit(solution)/shard_map/ppermute | solution.py:272
  58.7 1.6 %shard_map.82 = s16[528,128]{1,0:T(8,128)(2,1)S(1)} custom-call(f32[8,1024]{1,0:T(8,128)S(1)} %get-tuple-element.43.bias_ref, bf16[64,1280]{1,0:T(8,128)(2,1)S(1)} %collective-permute-done.4.refs_0_.refs_1_.refs_4_, bf16[1024,256]{1,0:T(8,128)(2,1)S(1)} %collective-permute-done.3.refs_1_, f32[64,1024]{1,0:T(8,128)S(1)} %get-tuple-element.73.refs_2_, ...), custom_call_target="tpu_custom_call" | custom-call | flops 268435456 | bytes 1507328 | tf_op jit(solution)/shard_map/pallas_call | solution.py:88
  60.3 0.9 %collective-permute-start.10 = (s16[528,128]{1,0:T(8,128)(2,1)S(1)}, s16[528,128]{1,0:T(8,128)(2,1)S(1)}, u32[]{:S(2)}, u32[]{:S(2)}) collective-permute-start(s16[528,128]{1,0:T(8,128)(2,1)S(1)} %shard_map.82), channel_id=1, source_target_pairs={{0,4},{1,5},{2,6},{3,7},{4,0},{5,1},{6,2},{7,3},{8,12},{9,13},{10,... | collective-permute-start | bytes 405512 | tf_op jit(solution)/shard_map/ppermute | solution.py:272
  61.2 1.6 %shard_map.80 = (f32[64,1024]{1,0:T(8,128)S(1)}, f32[512,256]{1,0:T(8,128)S(1)}) custom-call(f32[8,1024]{1,0:T(8,128)S(1)} %get-tuple-element.43.bias_ref, bf16[64,1280]{1,0:T(8,128)(2,1)S(1)} %get-tuple-element.48.refs_0_, bf16[1024,256]{1,0:T(8,128)(2,1)S(1)} %collective-permute-done.3.refs_1_, f32[64,1024]{1,0:T(8,128)S(1)} %get-tuple-element.67.refs_2_, ...), custom_call_target="tpu_custom_call" | custom-call | flops 268435456 | bytes 1671168 | tf_op jit(solution)/shard_map/pallas_call | solution.py:88
  62.8 3.0 %collective-permute-done.9.refs_0_ = s16[528,128]{1,0:T(8,128)(2,1)S(1)} collective-permute-done((s16[528,128]{1,0:T(8,128)(2,1)S(1)}, s16[528,128]{1,0:T(8,128)(2,1)S(1)}, u32[]{:S(2)}, u32[]{:S(2)}) %collective-permute-start.9) | collective-permute-done | bytes 135200 | tf_op jit(solution)/shard_map/ppermute | solution.py:272
  65.8 0.0 collective-permute-done.11.refs_2_
  65.8 2.7 %collective-permute-done.10.refs_1_ = s16[528,128]{1,0:T(8,128)(2,1)S(1)} collective-permute-done((s16[528,128]{1,0:T(8,128)(2,1)S(1)}, s16[528,128]{1,0:T(8,128)(2,1)S(1)}, u32[]{:S(2)}, u32[]{:S(2)}) %collective-permute-start.10) | collective-permute-done | bytes 135200 | tf_op jit(solution)/shard_map/ppermute | solution.py:272
  68.5 0.6 shard_map.84
  69.1 0.1 collective-permute-start.12
  69.2 1.6 %collective-permute-start.13 = (bf16[16,1024]{1,0:T(8,128)(2,1)S(1)}, bf16[16,1024]{1,0:T(8,128)(2,1)S(1)}, u32[]{:S(2)}, u32[]{:S(2)}) collective-permute-start(bf16[16,1024]{1,0:T(8,128)(2,1)S(1)} %get-tuple-element.79), channel_id=1, source_target_pairs={{0,2},{1,3},{2,0},{3,1},{4,6},{5,7},{6,4},{7,5},{8,10},{9,11},{10,... | collective-permute-start | bytes 98312 | tf_op jit(solution)/shard_map/ppermute | solution.py:269
  70.8 0.3 collective-permute-start.14
  71.0 0.0 collective-permute-done.12.refs_1_
  71.0 2.1 %collective-permute-done.13.refs_2_ = bf16[16,1024]{1,0:T(8,128)(2,1)S(1)} collective-permute-done((bf16[16,1024]{1,0:T(8,128)(2,1)S(1)}, bf16[16,1024]{1,0:T(8,128)(2,1)S(1)}, u32[]{:S(2)}, u32[]{:S(2)}) %collective-permute-start.13) | collective-permute-done | bytes 32800 | tf_op jit(solution)/shard_map/ppermute | solution.py:269
  73.2 1.0 %collective-permute-done.14.refs_3_ = bf16[16,1024]{1,0:T(8,128)(2,1)S(1)} collective-permute-done((bf16[16,1024]{1,0:T(8,128)(2,1)S(1)}, bf16[16,1024]{1,0:T(8,128)(2,1)S(1)}, u32[]{:S(2)}, u32[]{:S(2)}) %collective-permute-start.14) | collective-permute-done | bytes 32800 | tf_op jit(solution)/shard_map/ppermute | solution.py:269
  74.1 0.7 shard_map.85
  (1 shorter events, 0.0 us)
Async XLA Ops:
  1.3 34.2 %collective-permute-start.6 = (bf16[1024,256]{1,0:T(8,128)(2,1)S(1)}, bf16[1024,256]{1,0:T(8,128)(2,1)S(1)}, u32[]{:S(2)}, u32[]{:S(2)}) collective-permute-start(bf16[1024,256]{1,0:T(8,128)(2,1)S(1)} %get-tuple-element.52), channel_id=1, source_target_pairs={{0,1},{1,0},{2,3},{3,2},{4,5},{5,4},{6,7},{7,6},{8,9},{9,8},{10,11... | collective-permute-start | bytes 1572872 | tf_op jit(solution)/shard_map/ppermute | solution.py:269
  3.4 36.5 %collective-permute-start.5 = (bf16[1024,256]{1,0:T(8,128)(2,1)S(1)}, bf16[1024,256]{1,0:T(8,128)(2,1)S(1)}, u32[]{:S(2)}, u32[]{:S(2)}) collective-permute-start(bf16[1024,256]{1,0:T(8,128)(2,1)S(1)} %get-tuple-element.50), channel_id=1, source_target_pairs={{0,2},{1,3},{2,0},{3,1},{4,6},{5,7},{6,4},{7,5},{8,10},{9,11},{10,... | collective-permute-start | bytes 1572872 | tf_op jit(solution)/shard_map/ppermute | solution.py:269
  6.0 46.5 %collective-permute-start.3 = (bf16[1024,256]{1,0:T(8,128)(2,1)S(1)}, bf16[1024,256]{1,0:T(8,128)(2,1)S(1)}, u32[]{:S(2)}, u32[]{:S(2)}) collective-permute-start(bf16[1024,256]{1,0:T(8,128)(2,1)S(1)} %get-tuple-element.49), channel_id=1, source_target_pairs={{0,3},{1,2},{2,1},{3,0},{4,7},{5,6},{6,5},{7,4},{8,11},{9,10},{10,... | collective-permute-start | bytes 1572872 | tf_op jit(solution)/shard_map/ppermute | solution.py:269
  6.1 2.0 %collective-permute-start = (bf16[16,1280]{1,0:T(8,128)(2,1)S(1)}, bf16[16,1280]{1,0:T(8,128)(2,1)S(1)}, u32[]{:S(2)}, u32[]{:S(2)}) collective-permute-start(bf16[16,1280]{1,0:T(8,128)(2,1)S(1)} %get-tuple-element.45), channel_id=1, source_target_pairs={{0,1},{1,0},{2,3},{3,2},{4,5},{5,4},{6,7},{7,6},{8,9},{9,8},{10,11... | collective-permute-start | bytes 122888 | tf_op jit(solution)/shard_map/ppermute | solution.py:269
  6.2 24.7 %collective-permute-start.1 = (bf16[16,1280]{1,0:T(8,128)(2,1)S(1)}, bf16[16,1280]{1,0:T(8,128)(2,1)S(1)}, u32[]{:S(2)}, u32[]{:S(2)}) collective-permute-start(bf16[16,1280]{1,0:T(8,128)(2,1)S(1)} %get-tuple-element.46), channel_id=1, source_target_pairs={{0,2},{1,3},{2,0},{3,1},{4,6},{5,7},{6,4},{7,5},{8,10},{9,11},{10,... | collective-permute-start | bytes 122888 | tf_op jit(solution)/shard_map/ppermute | solution.py:269
  8.1 23.2 %collective-permute-start.2 = (bf16[16,1280]{1,0:T(8,128)(2,1)S(1)}, bf16[16,1280]{1,0:T(8,128)(2,1)S(1)}, u32[]{:S(2)}, u32[]{:S(2)}) collective-permute-start(bf16[16,1280]{1,0:T(8,128)(2,1)S(1)} %get-tuple-element.47), channel_id=1, source_target_pairs={{0,3},{1,2},{2,1},{3,0},{4,7},{5,6},{6,5},{7,4},{8,11},{9,10},{10,... | collective-permute-start | bytes 122888 | tf_op jit(solution)/shard_map/ppermute | solution.py:269
  31.3 6.4 %collective-permute-start.4 = (bf16[64,1280]{1,0:T(8,128)(2,1)S(1)}, bf16[64,1280]{1,0:T(8,128)(2,1)S(1)}, u32[]{:S(2)}, u32[]{:S(2)}) collective-permute-start(bf16[64,1280]{1,0:T(8,128)(2,1)S(1)} %get-tuple-element.48.refs_0_), channel_id=1, source_target_pairs={{0,4},{1,5},{2,6},{3,7},{4,0},{5,1},{6,2},{7,3},{8,12},{9,13},{10,... | collective-permute-start | bytes 491528 | tf_op jit(solution)/shard_map/ppermute | solution.py:272
  33.0 10.4 %collective-permute-start.8 = (bf16[64,1024]{1,0:T(8,128)(2,1)S(1)}, bf16[64,1024]{1,0:T(8,128)(2,1)S(1)}, u32[]{:S(2)}, u32[]{:S(2)}) collective-permute-start(bf16[64,1024]{1,0:T(8,128)(2,1)S(1)} %get-tuple-element.61), channel_id=1, source_target_pairs={{0,12},{1,13},{2,14},{3,15},{4,8},{5,9},{6,10},{7,11},{8,4},{9,5},... | collective-permute-start | bytes 393224 | tf_op jit(solution)/shard_map/ppermute | solution.py:272
  35.4 12.2 %collective-permute-start.7 = (bf16[64,1024]{1,0:T(8,128)(2,1)S(1)}, bf16[64,1024]{1,0:T(8,128)(2,1)S(1)}, u32[]{:S(2)}, u32[]{:S(2)}) collective-permute-start(bf16[64,1024]{1,0:T(8,128)(2,1)S(1)} %get-tuple-element.61), channel_id=1, source_target_pairs={{0,8},{1,9},{2,10},{3,11},{4,12},{5,13},{6,14},{7,15},{8,0},{9,1},... | collective-permute-start | bytes 393224 | tf_op jit(solution)/shard_map/ppermute | solution.py:272
  54.3 11.5 %collective-permute-start.9 = (s16[528,128]{1,0:T(8,128)(2,1)S(1)}, s16[528,128]{1,0:T(8,128)(2,1)S(1)}, u32[]{:S(2)}, u32[]{:S(2)}) collective-permute-start(s16[528,128]{1,0:T(8,128)(2,1)S(1)} %shard_map.81), channel_id=1, source_target_pairs={{0,8},{1,9},{2,10},{3,11},{4,12},{5,13},{6,14},{7,15},{8,0},{9,1},... | collective-permute-start | bytes 405512 | tf_op jit(solution)/shard_map/ppermute | solution.py:272
  56.0 9.8 %collective-permute-start.11 = (s16[528,128]{1,0:T(8,128)(2,1)S(1)}, s16[528,128]{1,0:T(8,128)(2,1)S(1)}, u32[]{:S(2)}, u32[]{:S(2)}) collective-permute-start(s16[528,128]{1,0:T(8,128)(2,1)S(1)} %shard_map.83), channel_id=1, source_target_pairs={{0,12},{1,13},{2,14},{3,15},{4,8},{5,9},{6,10},{7,11},{8,4},{9,5},... | collective-permute-start | bytes 405512 | tf_op jit(solution)/shard_map/ppermute | solution.py:272
  60.3 8.2 %collective-permute-start.10 = (s16[528,128]{1,0:T(8,128)(2,1)S(1)}, s16[528,128]{1,0:T(8,128)(2,1)S(1)}, u32[]{:S(2)}, u32[]{:S(2)}) collective-permute-start(s16[528,128]{1,0:T(8,128)(2,1)S(1)} %shard_map.82), channel_id=1, source_target_pairs={{0,4},{1,5},{2,6},{3,7},{4,0},{5,1},{6,2},{7,3},{8,12},{9,13},{10,... | collective-permute-start | bytes 405512 | tf_op jit(solution)/shard_map/ppermute | solution.py:272
  69.1 1.9 %collective-permute-start.12 = (bf16[16,1024]{1,0:T(8,128)(2,1)S(1)}, bf16[16,1024]{1,0:T(8,128)(2,1)S(1)}, u32[]{:S(2)}, u32[]{:S(2)}) collective-permute-start(bf16[16,1024]{1,0:T(8,128)(2,1)S(1)} %get-tuple-element.78), channel_id=1, source_target_pairs={{0,1},{1,0},{2,3},{3,2},{4,5},{5,4},{6,7},{7,6},{8,9},{9,8},{10,11... | collective-permute-start | bytes 98312 | tf_op jit(solution)/shard_map/ppermute | solution.py:269
  69.2 4.0 %collective-permute-start.13 = (bf16[16,1024]{1,0:T(8,128)(2,1)S(1)}, bf16[16,1024]{1,0:T(8,128)(2,1)S(1)}, u32[]{:S(2)}, u32[]{:S(2)}) collective-permute-start(bf16[16,1024]{1,0:T(8,128)(2,1)S(1)} %get-tuple-element.79), channel_id=1, source_target_pairs={{0,2},{1,3},{2,0},{3,1},{4,6},{5,7},{6,4},{7,5},{8,10},{9,11},{10,... | collective-permute-start | bytes 98312 | tf_op jit(solution)/shard_map/ppermute | solution.py:269
  70.8 3.4 %collective-permute-start.14 = (bf16[16,1024]{1,0:T(8,128)(2,1)S(1)}, bf16[16,1024]{1,0:T(8,128)(2,1)S(1)}, u32[]{:S(2)}, u32[]{:S(2)}) collective-permute-start(bf16[16,1024]{1,0:T(8,128)(2,1)S(1)} %get-tuple-element.80), channel_id=1, source_target_pairs={{0,3},{1,2},{2,1},{3,0},{4,7},{5,6},{6,5},{7,4},{8,11},{9,10},{10,... | collective-permute-start | bytes 98312 | tf_op jit(solution)/shard_map/ppermute | solution.py:269

commit v6 on v5

--- a/solution.py
+++ b/solution.py
@@ -104,16 +104,17 @@
 
 
 def split_far_kernel(q_ref, sk_ref, sv_ref, k_ref, v_ref, *refs):
-    outs, sems = refs[:6], refs[6]
+    (here, core, far, *kv_outs), sems = refs[:5], refs[5]
+    rows = here.shape[0]
     pairs = []
-    for j in (2, 3, 1, 0):
-        at = columns(j, HEAD_SIZE)
-        pairs.append((q_ref.at[:, columns(j, WIDTH)], outs[j].at[:, pl.ds(0, WIDTH)]))
-        pairs.append((sk_ref.at[:, at], outs[j].at[:, pl.ds(WIDTH, HEAD_SIZE)]))
-        pairs.append((sv_ref.at[:, at], outs[j].at[:, pl.ds(WIDTH + HEAD_SIZE, HEAD_SIZE)]))
-    for out, j in zip(outs[4:], (2, 3)):
+    for out, j in zip(kv_outs, (2, 3)):
         pairs.append((k_ref.at[:, columns(j, HEAD_SIZE)], out.at[:, pl.ds(0, HEAD_SIZE)]))
         pairs.append((v_ref.at[:, columns(j, HEAD_SIZE)], out.at[:, pl.ds(HEAD_SIZE, HEAD_SIZE)]))
+    for j, out, first in ((2, far, 0), (3, far, rows), (1, core, 0), (0, here, 0)):
+        at, to = columns(j, HEAD_SIZE), pl.ds(first, rows)
+        pairs.append((q_ref.at[:, columns(j, WIDTH)], out.at[to, pl.ds(0, WIDTH)]))
+        pairs.append((sk_ref.at[:, at], out.at[to, pl.ds(WIDTH, HEAD_SIZE)]))
+        pairs.append((sv_ref.at[:, at], out.at[to, pl.ds(WIDTH + HEAD_SIZE, HEAD_SIZE)]))
     for c in start_all(pairs, sems):
         c.wait()
 
@@ -139,12 +140,12 @@
         c.wait()
 
 
-def stack_kernel(*refs):
-    rows = refs[0].shape[0]
-    both, only = refs[-2:]
-    for j, ref in enumerate(refs[:-2]):
-        both[j * rows : (j + 1) * rows, :] = ref[...]
-        only[j * rows : (j + 1) * rows, :] = ref[:, :WIDTH]
+def stack_kernel(here, core, far, passed, both, only):
+    rows = here.shape[0]
+    parts = (here[...], core[...], far[:rows, :], passed[rows:, :])
+    for j, part in enumerate(parts):
+        both[j * rows : (j + 1) * rows, :] = part
+        only[j * rows : (j + 1) * rows, :] = part[:, :WIDTH]
 
 
 def attend_kernel(cfg, bias_ref, *refs):
@@ -278,9 +279,9 @@
     wide = WIDTH + 2 * HEAD_SIZE
     ins = [queries, span_keys, span_values, keys, values]
     ins, tables = ([pltpu.with_memory_space_constraint(x, pltpu.HBM) for x in xs] for xs in (ins, tables))
-    *q_parts, kv2, kv3 = local_call(
+    here, core, far, kv2, kv3 = local_call(
         split_far_kernel,
-        [((part, wide), BF16)] * 4 + [((slots, 2 * HEAD_SIZE), BF16)] * 2,
+        [((part, wide), BF16)] * 2 + [((2 * part, wide), BF16)] + [((slots, 2 * HEAD_SIZE), BF16)] * 2,
         ins,
         scratch=[pltpu.SemaphoreType.DMA((16,))],
         space=pltpu.HBM,
@@ -292,24 +293,26 @@
         scratch=[pltpu.SMEM(x.shape, x.dtype) for x in tables] + [pltpu.SemaphoreType.DMA((6,))],
         space=pltpu.HBM,
     )
-    q_parts = [q_parts[0]] + [within(q_parts[j], j) for j in range(1, 4)]
+    core, far = within(core, 1), within(far, 2)
+    q_parts = (here, core, far, within(far, 1))
     kv = {0: kv0, 1: within(kv1, 1), 2: within(kv2, 2), 3: within(kv3, 3)}
-    both, only = local_call(stack_kernel, [((4 * part, wide), BF16), ((4 * part, WIDTH), BF16)], q_parts)
-    q = {0: both, 1: along(both, 1)} | {d: along(only, d) for d in range(2, zs)}
+    stacked, only = local_call(stack_kernel, [((4 * part, wide), BF16), ((4 * part, WIDTH), BF16)], q_parts)
+    q = {0: stacked, 1: along(stacked, 1)} | {d: along(only, d) for d in range(2, zs)}
 
     near = {j: kv[j] for j in (0, 1)}
     state = attend({0: q[0]}, near)
+    near[2] = kv[2]
     state |= attend({1: q[1]}, near)
-    state = attend({0: q[0], 1: q[1]}, {2: kv[2]}, prior=state)
-    near[2] = kv[2]
-    state |= attend({2: q[2], 3: q[3]}, near)
+    state |= attend({2: q[2]}, near)
+    state |= attend({3: q[3]}, near)
     kv[3], state = lax.optimization_barrier((kv[3], state))
     last = {3: kv[3]}
+    both = {2: kv[2], 3: kv[3]}
     back = []
     for d in (2, 1, 3):
         (coded,) = attend({d: q[d]}, last, prior=state, finish="encode")
         back.append(along(coded, d))
-    mine = attend({0: q[0]}, last, prior=state, finish="span", before=q[1])[0]
+    mine = attend({0: q[0]}, both, prior=state, finish="span", before=q[1])[0]
     parts = local_call(functools.partial(final_kernel, q[0].shape[0]), [((part, WIDTH), BF16)] * 4, (*mine, *back))
     parts = [parts[0]] + [within(parts[j], j) for j in range(1, 4)]
     return local_call(join_kernel, [((part, 4 * WIDTH), BF16)], parts)[0]

time: 75 us -> 64.2 us (0.86)
  waiting for transfers between devices: 36.6 us -> 22.3 us
  starting transfers between devices: 16 us -> 19.9 us
    ppermute x9, waiting for transfers between devices: 25.5 us -> 15.3 us  [within(): return lax.ppermute(x, 'kvp', [(i, i ^ j) for i in range(n)])]
    ppermute x6, starting transfers between devices: 7.92 us -> 12.5 us  [along(): return lax.ppermute(x, 'kvp', [(i, i ^ 4 * d) for i in range(n)])]
    ppermute x6, waiting for transfers between devices: 11.2 us -> 6.98 us  [along(): return lax.ppermute(x, 'kvp', [(i, i ^ 4 * d) for i in range(n)])]
  transfers between devices with their start and end apart: 15 -> 15, of which waited for: 8 -> 6; matrix products, arithmetic and copies ran while one was open for 0% -> 0% of each run, Pallas kernels for 24% -> 27%
where the time goes in v6:
time: 64.2 us; the launch traced here: 64 us
  waiting for transfers between devices  22.3 us (35%)
  Pallas kernels  21.7 us (34%)
  starting transfers between devices  19.9 us (31%)
    pallas_call x13, Pallas kernels, local_call(): pl.pallas_call(kernel, out_shape=[jax.ShapeDtypeStruct(s, t) for s, t in...  21.7 us
    ppermute x9, waiting for transfers between devices, within(): return lax.ppermute(x, 'kvp', [(i, i ^ j) for i in range(n)])  15.3 us
    ppermute x6, starting transfers between devices, along(): return lax.ppermute(x, 'kvp', [(i, i ^ 4 * d) for i in range(n)])  12.5 us
    ppermute x9, starting transfers between devices, within(): return lax.ppermute(x, 'kvp', [(i, i ^ j) for i in range(n)])  7.41 us
    ppermute x6, waiting for transfers between devices, along(): return lax.ppermute(x, 'kvp', [(i, i ^ 4 * d) for i in range(n)])  6.98 us
  transfers between devices with their start and end apart: 15, of which 6 were waited for; matrix products, arithmetic and copies ran while one was open for 0% of the time, Pallas kernels for 27%

profile of v6, /device:TPU:0, one launch (start us, length us, event | category | flops | bytes accessed | tf_op | source)
XLA Modules:
  0.0 64.0 jit_solution(7482399609339001377)
XLA Ops:
  0.0 1.4 %shard_map.74 = (bf16[16,1280]{1,0:T(8,128)(2,1)S(1)}, bf16[16,1280]{1,0:T(8,128)(2,1)S(1)}, bf16[32,1280]{1,0:T(8,128)(2,1)S(1)}, bf16[1024,256]{1,0:T(8,128)(2,1)S(1)}, bf16[1024,256]{1,0:T(8,128)(2,1)S(1)}) custom-call(bf16[16,4096]{1,0:T(8,128)(2,1)} %q_ref.1, bf16[16,512]{1,0:T(8,128)(2,1)} %sk_ref.1, bf16[16,512]{1,0:T(8,128)(2,1)} %sv_ref.1, ...), custom_call_target="tpu_custom_call" | custom-call | bytes 2260992 | tf_op jit(solution)/shard_map/pallas_call | solution.py:88
  1.4 3.1 %collective-permute-start.3 = (bf16[1024,256]{1,0:T(8,128)(2,1)S(1)}, bf16[1024,256]{1,0:T(8,128)(2,1)S(1)}, u32[]{:S(2)}, u32[]{:S(2)}) collective-permute-start(bf16[1024,256]{1,0:T(8,128)(2,1)S(1)} %get-tuple-element.43), channel_id=1, source_target_pairs={{0,2},{1,3},{2,0},{3,1},{4,6},{5,7},{6,4},{7,5},{8,10},{9,11},{10,... | collective-permute-start | bytes 1572872 | tf_op jit(solution)/shard_map/ppermute | solution.py:270
  4.4 1.3 %shard_map.73 = (bf16[1024,256]{1,0:T(8,128)(2,1)S(1)}, bf16[1024,256]{1,0:T(8,128)(2,1)S(1)}, f32[8,1024]{1,0:T(8,128)S(1)}) custom-call(s32[16]{0:T(128)} %lens_ref.1, s32[2]{0:T(128)} %starts_ref.1, bf16[1024,512]{1,0:T(8,128)(2,1)} %k_ref.3, bf16[1024,512]{1,0:T(8,128)(2,1)} %v_ref.3), custom_call_target="tpu_custom_call" | custom-call | bytes 2097224 | tf_op jit(solution)/shard_map/pallas_call | solution.py:88
  5.7 0.1 collective-permute-start.5
  5.8 0.1 collective-permute-start.1
  5.9 1.7 %collective-permute-start.4 = (bf16[1024,256]{1,0:T(8,128)(2,1)S(1)}, bf16[1024,256]{1,0:T(8,128)(2,1)S(1)}, u32[]{:S(2)}, u32[]{:S(2)}) collective-permute-start(bf16[1024,256]{1,0:T(8,128)(2,1)S(1)} %get-tuple-element.44), channel_id=1, source_target_pairs={{0,3},{1,2},{2,1},{3,0},{4,7},{5,6},{6,5},{7,4},{8,11},{9,10},{10,... | collective-permute-start | bytes 1572872 | tf_op jit(solution)/shard_map/ppermute | solution.py:270
  7.6 11.3 %collective-permute-done.1.far = bf16[32,1280]{1,0:T(8,128)(2,1)S(1)} collective-permute-done((bf16[32,1280]{1,0:T(8,128)(2,1)S(1)}, bf16[32,1280]{1,0:T(8,128)(2,1)S(1)}, u32[]{:S(2)}, u32[]{:S(2)}) %collective-permute-start.1) | collective-permute-done | bytes 81952 | tf_op jit(solution)/shard_map/ppermute | solution.py:270
  19.0 0.0 collective-permute-start.2
  19.0 0.5 collective-permute-start
  19.5 0.9 %collective-permute-done.core = bf16[16,1280]{1,0:T(8,128)(2,1)S(1)} collective-permute-done((bf16[16,1280]{1,0:T(8,128)(2,1)S(1)}, bf16[16,1280]{1,0:T(8,128)(2,1)S(1)}, u32[]{:S(2)}, u32[]{:S(2)}) %collective-permute-start) | collective-permute-done | bytes 40992 | tf_op jit(solution)/shard_map/ppermute | solution.py:270
  20.4 0.0 collective-permute-done.2.passed
  20.4 2.1 %collective-permute-start.6 = (bf16[64,1280]{1,0:T(8,128)(2,1)S(1)}, bf16[64,1280]{1,0:T(8,128)(2,1)S(1)}, u32[]{:S(2)}, u32[]{:S(2)}) collective-permute-start(bf16[64,1280]{1,0:T(8,128)(2,1)S(1)} %get-tuple-element.42.refs_0_), channel_id=1, source_target_pairs={{0,4},{1,5},{2,6},{3,7},{4,0},{5,1},{6,2},{7,3},{8,12},{9,13},{10,... | collective-permute-start | bytes 491528 | tf_op jit(solution)/shard_map/ppermute | solution.py:273
  22.5 2.6 %collective-permute-start.7 = (bf16[64,1024]{1,0:T(8,128)(2,1)S(1)}, bf16[64,1024]{1,0:T(8,128)(2,1)S(1)}, u32[]{:S(2)}, u32[]{:S(2)}) collective-permute-start(bf16[64,1024]{1,0:T(8,128)(2,1)S(1)} %get-tuple-element.51), channel_id=1, source_target_pairs={{0,8},{1,9},{2,10},{3,11},{4,12},{5,13},{6,14},{7,15},{8,0},{9,1},... | collective-permute-start | bytes 393224 | tf_op jit(solution)/shard_map/ppermute | solution.py:273
  25.1 4.9 %collective-permute-done.6.refs_0_.refs_5_ = bf16[64,1280]{1,0:T(8,128)(2,1)S(1)} collective-permute-done((bf16[64,1280]{1,0:T(8,128)(2,1)S(1)}, bf16[64,1280]{1,0:T(8,128)(2,1)S(1)}, u32[]{:S(2)}, u32[]{:S(2)}) %collective-permute-start.6) | collective-permute-done | bytes 163872 | tf_op jit(solution)/shard_map/ppermute | solution.py:273
  30.0 3.2 %collective-permute-start.8 = (bf16[64,1024]{1,0:T(8,128)(2,1)S(1)}, bf16[64,1024]{1,0:T(8,128)(2,1)S(1)}, u32[]{:S(2)}, u32[]{:S(2)}) collective-permute-start(bf16[64,1024]{1,0:T(8,128)(2,1)S(1)} %get-tuple-element.51), channel_id=1, source_target_pairs={{0,12},{1,13},{2,14},{3,15},{4,8},{5,9},{6,10},{7,11},{8,4},{9,5},... | collective-permute-start | bytes 393224 | tf_op jit(solution)/shard_map/ppermute | solution.py:273
  33.3 0.0 collective-permute-done.3.refs_3_.refs_1_
  33.3 0.0 collective-permute-done.5.refs_2_
  33.3 2.8 %shard_map.77 = (f32[64,1024]{1,0:T(8,128)S(1)}, f32[512,256]{1,0:T(8,128)S(1)}) custom-call(f32[8,1024]{1,0:T(8,128)S(1)} %get-tuple-element.38.bias_ref, bf16[64,1280]{1,0:T(8,128)(2,1)S(1)} %collective-permute-done.6.refs_0_.refs_5_, bf16[1024,256]{1,0:T(8,128)(2,1)S(1)} %get-tuple-element.45.refs_1_, ...), custom_call_target="tpu_custom_call" | custom-call | flops 805306368 | bytes 1769472 | tf_op jit(solution)/shard_map/pallas_call | solution.py:88
  36.1 2.1 %shard_map.76 = (f32[64,1024]{1,0:T(8,128)S(1)}, f32[512,256]{1,0:T(8,128)S(1)}) custom-call(f32[8,1024]{1,0:T(8,128)S(1)} %get-tuple-element.38.bias_ref, bf16[64,1280]{1,0:T(8,128)(2,1)S(1)} %get-tuple-element.42.refs_0_, bf16[1024,256]{1,0:T(8,128)(2,1)S(1)} %get-tuple-element.45.refs_1_, bf16[1024,256]{1,0:T(8,128)(2,1)S(1)} %collective-permute-done.5.refs_2_), custom_call_target="tpu_custom_call" | custom-call | flops 536870912 | bytes 1245184 | tf_op jit(solution)/shard_map/pallas_call | solution.py:88
  38.2 0.0 collective-permute-done.7.refs_0_
  38.2 2.8 %shard_map.78 = (f32[64,1024]{1,0:T(8,128)S(1)}, f32[512,256]{1,0:T(8,128)S(1)}) custom-call(f32[8,1024]{1,0:T(8,128)S(1)} %get-tuple-element.38.bias_ref, bf16[64,1024]{1,0:T(8,128)(2,1)S(1)} %collective-permute-done.7.refs_0_, bf16[1024,256]{1,0:T(8,128)(2,1)S(1)} %get-tuple-element.45.refs_1_, bf16[1024,256]{1,0:T(8,128)(2,1)S(1)} %collective-permute-done.5.refs_2_, ...), custom_call_target="tpu_custom_call" | custom-call | flops 805306368 | bytes 1736704 | tf_op jit(solution)/shard_map/pallas_call | solution.py:88
  41.0 0.0 collective-permute-done.8.refs_0_
  41.0 2.8 %shard_map.79 = (f32[64,1024]{1,0:T(8,128)S(1)}, f32[512,256]{1,0:T(8,128)S(1)}) custom-call(f32[8,1024]{1,0:T(8,128)S(1)} %get-tuple-element.38.bias_ref, bf16[64,1024]{1,0:T(8,128)(2,1)S(1)} %collective-permute-done.8.refs_0_, bf16[1024,256]{1,0:T(8,128)(2,1)S(1)} %get-tuple-element.45.refs_1_, bf16[1024,256]{1,0:T(8,128)(2,1)S(1)} %collective-permute-done.5.refs_2_, ...), custom_call_target="tpu_custom_call" | custom-call | flops 805306368 | bytes 1736704 | tf_op jit(solution)/shard_map/pallas_call | solution.py:88
  43.8 0.0 collective-permute-done.4.refs_2_.refs_1_
  43.8 1.8 %shard_map.81 = s16[528,128]{1,0:T(8,128)(2,1)S(1)} custom-call(f32[8,1024]{1,0:T(8,128)S(1)} %get-tuple-element.38.bias_ref, bf16[64,1024]{1,0:T(8,128)(2,1)S(1)} %collective-permute-done.7.refs_0_, bf16[1024,256]{1,0:T(8,128)(2,1)S(1)} %collective-permute-done.4.refs_2_.refs_1_, f32[64,1024]{1,0:T(8,128)S(1)} %get-tuple-element.61.refs_2_, ...), custom_call_target="tpu_custom_call" | custom-call | flops 268435456 | bytes 1474560 | tf_op jit(solution)/shard_map/pallas_call | solution.py:88
  45.6 0.1 collective-permute-start.9
  45.7 1.6 %shard_map.82 = s16[528,128]{1,0:T(8,128)(2,1)S(1)} custom-call(f32[8,1024]{1,0:T(8,128)S(1)} %get-tuple-element.38.bias_ref, bf16[64,1280]{1,0:T(8,128)(2,1)S(1)} %collective-permute-done.6.refs_0_.refs_5_, bf16[1024,256]{1,0:T(8,128)(2,1)S(1)} %collective-permute-done.4.refs_2_.refs_1_, f32[64,1024]{1,0:T(8,128)S(1)} %get-tuple-element.63.refs_2_, ...), custom_call_target="tpu_custom_call" | custom-call | flops 268435456 | bytes 1507328 | tf_op jit(solution)/shard_map/pallas_call | solution.py:88
  47.3 1.2 %collective-permute-start.10 = (s16[528,128]{1,0:T(8,128)(2,1)S(1)}, s16[528,128]{1,0:T(8,128)(2,1)S(1)}, u32[]{:S(2)}, u32[]{:S(2)}) collective-permute-start(s16[528,128]{1,0:T(8,128)(2,1)S(1)} %shard_map.82), channel_id=1, source_target_pairs={{0,4},{1,5},{2,6},{3,7},{4,0},{5,1},{6,2},{7,3},{8,12},{9,13},{10,... | collective-permute-start | bytes 405512 | tf_op jit(solution)/shard_map/ppermute | solution.py:273
  48.5 1.6 %shard_map.83 = s16[528,128]{1,0:T(8,128)(2,1)S(1)} custom-call(f32[8,1024]{1,0:T(8,128)S(1)} %get-tuple-element.38.bias_ref, bf16[64,1024]{1,0:T(8,128)(2,1)S(1)} %collective-permute-done.8.refs_0_, bf16[1024,256]{1,0:T(8,128)(2,1)S(1)} %collective-permute-done.4.refs_2_.refs_1_, f32[64,1024]{1,0:T(8,128)S(1)} %get-tuple-element.65.refs_2_, ...), custom_call_target="tpu_custom_call" | custom-call | flops 268435456 | bytes 1474560 | tf_op jit(solution)/shard_map/pallas_call | solution.py:88
  50.1 3.3 %collective-permute-start.11 = (s16[528,128]{1,0:T(8,128)(2,1)S(1)}, s16[528,128]{1,0:T(8,128)(2,1)S(1)}, u32[]{:S(2)}, u32[]{:S(2)}) collective-permute-start(s16[528,128]{1,0:T(8,128)(2,1)S(1)} %shard_map.83), channel_id=1, source_target_pairs={{0,12},{1,13},{2,14},{3,15},{4,8},{5,9},{6,10},{7,11},{8,4},{9,5},... | collective-permute-start | bytes 405512 | tf_op jit(solution)/shard_map/ppermute | solution.py:273
  53.4 2.3 %shard_map.80 = (f32[64,1024]{1,0:T(8,128)S(1)}, f32[512,256]{1,0:T(8,128)S(1)}) custom-call(f32[8,1024]{1,0:T(8,128)S(1)} %get-tuple-element.38.bias_ref, bf16[64,1280]{1,0:T(8,128)(2,1)S(1)} %get-tuple-element.42.refs_0_, bf16[1024,256]{1,0:T(8,128)(2,1)S(1)} %collective-permute-done.3.refs_3_.refs_1_, ...), custom_call_target="tpu_custom_call" | custom-call | flops 536870912 | bytes 2195456 | tf_op jit(solution)/shard_map/pallas_call | solution.py:88
  55.7 0.0 collective-permute-done.9.refs_0_
  55.7 2.0 %collective-permute-done.10.refs_1_ = s16[528,128]{1,0:T(8,128)(2,1)S(1)} collective-permute-done((s16[528,128]{1,0:T(8,128)(2,1)S(1)}, s16[528,128]{1,0:T(8,128)(2,1)S(1)}, u32[]{:S(2)}, u32[]{:S(2)}) %collective-permute-start.10) | collective-permute-done | bytes 135200 | tf_op jit(solution)/shard_map/ppermute | solution.py:273
  57.8 0.0 collective-permute-done.11.refs_2_
  57.8 0.6 shard_map.84
  58.4 0.1 collective-permute-start.12
  58.4 1.6 %collective-permute-start.13 = (bf16[16,1024]{1,0:T(8,128)(2,1)S(1)}, bf16[16,1024]{1,0:T(8,128)(2,1)S(1)}, u32[]{:S(2)}, u32[]{:S(2)}) collective-permute-start(bf16[16,1024]{1,0:T(8,128)(2,1)S(1)} %get-tuple-element.69), channel_id=1, source_target_pairs={{0,2},{1,3},{2,0},{3,1},{4,6},{5,7},{6,4},{7,5},{8,10},{9,11},{10,... | collective-permute-start | bytes 98312 | tf_op jit(solution)/shard_map/ppermute | solution.py:270
  60.0 0.3 collective-permute-start.14
  60.3 0.0 collective-permute-done.12.refs_1_
  60.3 2.1 %collective-permute-done.13.refs_2_ = bf16[16,1024]{1,0:T(8,128)(2,1)S(1)} collective-permute-done((bf16[16,1024]{1,0:T(8,128)(2,1)S(1)}, bf16[16,1024]{1,0:T(8,128)(2,1)S(1)}, u32[]{:S(2)}, u32[]{:S(2)}) %collective-permute-start.13) | collective-permute-done | bytes 32800 | tf_op jit(solution)/shard_map/ppermute | solution.py:270
  62.4 1.0 %collective-permute-done.14.refs_3_ = bf16[16,1024]{1,0:T(8,128)(2,1)S(1)} collective-permute-done((bf16[16,1024]{1,0:T(8,128)(2,1)S(1)}, bf16[16,1024]{1,0:T(8,128)(2,1)S(1)}, u32[]{:S(2)}, u32[]{:S(2)}) %collective-permute-start.14) | collective-permute-done | bytes 32800 | tf_op jit(solution)/shard_map/ppermute | solution.py:270
  63.4 0.7 %shard_map.85 = bf16[16,4096]{1,0:T(8,128)(2,1)} custom-call(bf16[16,1024]{1,0:T(8,128)(2,1)S(1)} %get-tuple-element.67.refs_0_, bf16[16,1024]{1,0:T(8,128)(2,1)S(1)} %collective-permute-done.12.refs_1_, bf16[16,1024]{1,0:T(8,128)(2,1)S(1)} %collective-permute-done.13.refs_2_, bf16[16,1024]{1,0:T(8,128)(2,1)S(1)} %collective-permute-done.14.refs_3_), custom_call_target="tpu_custom_call" | custom-call | bytes 131072 | tf_op jit(solution)/shard_map/pallas_call | solution.py:88
  (1 shorter events, 0.0 us)
Async XLA Ops:
  1.4 31.9 %collective-permute-start.3 = (bf16[1024,256]{1,0:T(8,128)(2,1)S(1)}, bf16[1024,256]{1,0:T(8,128)(2,1)S(1)}, u32[]{:S(2)}, u32[]{:S(2)}) collective-permute-start(bf16[1024,256]{1,0:T(8,128)(2,1)S(1)} %get-tuple-element.43), channel_id=1, source_target_pairs={{0,2},{1,3},{2,0},{3,1},{4,6},{5,7},{6,4},{7,5},{8,10},{9,11},{10,... | collective-permute-start | bytes 1572872 | tf_op jit(solution)/shard_map/ppermute | solution.py:270
  5.7 27.6 %collective-permute-start.5 = (bf16[1024,256]{1,0:T(8,128)(2,1)S(1)}, bf16[1024,256]{1,0:T(8,128)(2,1)S(1)}, u32[]{:S(2)}, u32[]{:S(2)}) collective-permute-start(bf16[1024,256]{1,0:T(8,128)(2,1)S(1)} %get-tuple-element.46), channel_id=1, source_target_pairs={{0,1},{1,0},{2,3},{3,2},{4,5},{5,4},{6,7},{7,6},{8,9},{9,8},{10,11... | collective-permute-start | bytes 1572872 | tf_op jit(solution)/shard_map/ppermute | solution.py:270
  5.8 13.2 %collective-permute-start.1 = (bf16[32,1280]{1,0:T(8,128)(2,1)S(1)}, bf16[32,1280]{1,0:T(8,128)(2,1)S(1)}, u32[]{:S(2)}, u32[]{:S(2)}) collective-permute-start(bf16[32,1280]{1,0:T(8,128)(2,1)S(1)} %get-tuple-element.41), channel_id=1, source_target_pairs={{0,2},{1,3},{2,0},{3,1},{4,6},{5,7},{6,4},{7,5},{8,10},{9,11},{10,... | collective-permute-start | bytes 245768 | tf_op jit(solution)/shard_map/ppermute | solution.py:270
  5.9 37.9 %collective-permute-start.4 = (bf16[1024,256]{1,0:T(8,128)(2,1)S(1)}, bf16[1024,256]{1,0:T(8,128)(2,1)S(1)}, u32[]{:S(2)}, u32[]{:S(2)}) collective-permute-start(bf16[1024,256]{1,0:T(8,128)(2,1)S(1)} %get-tuple-element.44), channel_id=1, source_target_pairs={{0,3},{1,2},{2,1},{3,0},{4,7},{5,6},{6,5},{7,4},{8,11},{9,10},{10,... | collective-permute-start | bytes 1572872 | tf_op jit(solution)/shard_map/ppermute | solution.py:270
  19.0 1.4 %collective-permute-start.2 = (bf16[32,1280]{1,0:T(8,128)(2,1)S(1)}, bf16[32,1280]{1,0:T(8,128)(2,1)S(1)}, u32[]{:S(2)}, u32[]{:S(2)}) collective-permute-start(bf16[32,1280]{1,0:T(8,128)(2,1)S(1)} %collective-permute-done.1.far), channel_id=1, source_target_pairs={{0,1},{1,0},{2,3},{3,2},{4,5},{5,4},{6,7},{7,6},{8,9},{9,8},{10,11... | collective-permute-start | bytes 245768 | tf_op jit(solution)/shard_map/ppermute | solution.py:270
  19.0 1.4 %collective-permute-start = (bf16[16,1280]{1,0:T(8,128)(2,1)S(1)}, bf16[16,1280]{1,0:T(8,128)(2,1)S(1)}, u32[]{:S(2)}, u32[]{:S(2)}) collective-permute-start(bf16[16,1280]{1,0:T(8,128)(2,1)S(1)} %get-tuple-element.40), channel_id=1, source_target_pairs={{0,1},{1,0},{2,3},{3,2},{4,5},{5,4},{6,7},{7,6},{8,9},{9,8},{10,11... | collective-permute-start | bytes 122888 | tf_op jit(solution)/shard_map/ppermute | solution.py:270
  20.4 9.7 %collective-permute-start.6 = (bf16[64,1280]{1,0:T(8,128)(2,1)S(1)}, bf16[64,1280]{1,0:T(8,128)(2,1)S(1)}, u32[]{:S(2)}, u32[]{:S(2)}) collective-permute-start(bf16[64,1280]{1,0:T(8,128)(2,1)S(1)} %get-tuple-element.42.refs_0_), channel_id=1, source_target_pairs={{0,4},{1,5},{2,6},{3,7},{4,0},{5,1},{6,2},{7,3},{8,12},{9,13},{10,... | collective-permute-start | bytes 491528 | tf_op jit(solution)/shard_map/ppermute | solution.py:273
  22.5 15.7 %collective-permute-start.7 = (bf16[64,1024]{1,0:T(8,128)(2,1)S(1)}, bf16[64,1024]{1,0:T(8,128)(2,1)S(1)}, u32[]{:S(2)}, u32[]{:S(2)}) collective-permute-start(bf16[64,1024]{1,0:T(8,128)(2,1)S(1)} %get-tuple-element.51), channel_id=1, source_target_pairs={{0,8},{1,9},{2,10},{3,11},{4,12},{5,13},{6,14},{7,15},{8,0},{9,1},... | collective-permute-start | bytes 393224 | tf_op jit(solution)/shard_map/ppermute | solution.py:273
  30.0 11.0 %collective-permute-start.8 = (bf16[64,1024]{1,0:T(8,128)(2,1)S(1)}, bf16[64,1024]{1,0:T(8,128)(2,1)S(1)}, u32[]{:S(2)}, u32[]{:S(2)}) collective-permute-start(bf16[64,1024]{1,0:T(8,128)(2,1)S(1)} %get-tuple-element.51), channel_id=1, source_target_pairs={{0,12},{1,13},{2,14},{3,15},{4,8},{5,9},{6,10},{7,11},{8,4},{9,5},... | collective-permute-start | bytes 393224 | tf_op jit(solution)/shard_map/ppermute | solution.py:273
  45.6 10.1 %collective-permute-start.9 = (s16[528,128]{1,0:T(8,128)(2,1)S(1)}, s16[528,128]{1,0:T(8,128)(2,1)S(1)}, u32[]{:S(2)}, u32[]{:S(2)}) collective-permute-start(s16[528,128]{1,0:T(8,128)(2,1)S(1)} %shard_map.81), channel_id=1, source_target_pairs={{0,8},{1,9},{2,10},{3,11},{4,12},{5,13},{6,14},{7,15},{8,0},{9,1},... | collective-permute-start | bytes 405512 | tf_op jit(solution)/shard_map/ppermute | solution.py:273
  47.3 10.5 %collective-permute-start.10 = (s16[528,128]{1,0:T(8,128)(2,1)S(1)}, s16[528,128]{1,0:T(8,128)(2,1)S(1)}, u32[]{:S(2)}, u32[]{:S(2)}) collective-permute-start(s16[528,128]{1,0:T(8,128)(2,1)S(1)} %shard_map.82), channel_id=1, source_target_pairs={{0,4},{1,5},{2,6},{3,7},{4,0},{5,1},{6,2},{7,3},{8,12},{9,13},{10,... | collective-permute-start | bytes 405512 | tf_op jit(solution)/shard_map/ppermute | solution.py:273
  50.1 7.7 %collective-permute-start.11 = (s16[528,128]{1,0:T(8,128)(2,1)S(1)}, s16[528,128]{1,0:T(8,128)(2,1)S(1)}, u32[]{:S(2)}, u32[]{:S(2)}) collective-permute-start(s16[528,128]{1,0:T(8,128)(2,1)S(1)} %shard_map.83), channel_id=1, source_target_pairs={{0,12},{1,13},{2,14},{3,15},{4,8},{5,9},{6,10},{7,11},{8,4},{9,5},... | collective-permute-start | bytes 405512 | tf_op jit(solution)/shard_map/ppermute | solution.py:273
  58.4 1.9 %collective-permute-start.12 = (bf16[16,1024]{1,0:T(8,128)(2,1)S(1)}, bf16[16,1024]{1,0:T(8,128)(2,1)S(1)}, u32[]{:S(2)}, u32[]{:S(2)}) collective-permute-start(bf16[16,1024]{1,0:T(8,128)(2,1)S(1)} %get-tuple-element.68), channel_id=1, source_target_pairs={{0,1},{1,0},{2,3},{3,2},{4,5},{5,4},{6,7},{7,6},{8,9},{9,8},{10,11... | collective-permute-start | bytes 98312 | tf_op jit(solution)/shard_map/ppermute | solution.py:270
  58.4 4.0 %collective-permute-start.13 = (bf16[16,1024]{1,0:T(8,128)(2,1)S(1)}, bf16[16,1024]{1,0:T(8,128)(2,1)S(1)}, u32[]{:S(2)}, u32[]{:S(2)}) collective-permute-start(bf16[16,1024]{1,0:T(8,128)(2,1)S(1)} %get-tuple-element.69), channel_id=1, source_target_pairs={{0,2},{1,3},{2,0},{3,1},{4,6},{5,7},{6,4},{7,5},{8,10},{9,11},{10,... | collective-permute-start | bytes 98312 | tf_op jit(solution)/shard_map/ppermute | solution.py:270
  60.0 3.4 %collective-permute-start.14 = (bf16[16,1024]{1,0:T(8,128)(2,1)S(1)}, bf16[16,1024]{1,0:T(8,128)(2,1)S(1)}, u32[]{:S(2)}, u32[]{:S(2)}) collective-permute-start(bf16[16,1024]{1,0:T(8,128)(2,1)S(1)} %get-tuple-element.70), channel_id=1, source_target_pairs={{0,3},{1,2},{2,1},{3,0},{4,7},{5,6},{6,5},{7,4},{8,11},{9,10},{10,... | collective-permute-start | bytes 98312 | tf_op jit(solution)/shard_map/ppermute | solution.py:270
